TPU v7x, 32 devices: a whole 2x2x4 slice. The times are simulated.
32 devices in a mesh: lat: 8 (over y, x, core), lon: 4 (over z).
Axes of the slice: x: 2, y: 2, z: 4, core: 2. Of those that a mesh axis runs over, the one named last changes fastest.
Arguments:
- ocean_state: bfloat16 [72, 1024, 128], P('lat', 'lon'), may hold values from -6 to 6
- cotangent: bfloat16 [72, 1024, 128], P('lat', 'lon'), may hold values from -6 to 6
- atm_embed: bfloat16 [16384, 256], P(('lat', 'lon')), may hold values from -6 to 6
- projection: bfloat16 [256, 128], replicated, may hold values from -0.375 to 0.375
- dw_kernel: float32 [7, 7, 128], replicated, may hold values from -0.875 to 0.875
- norm_gain: float32 [128], replicated, may hold values from 0.25 to 1.75
- w_in: bfloat16 [128, 512], replicated, may hold values from -0.5 to 0.5
- w_out: bfloat16 [512, 128], replicated, may hold values from -0.25 to 0.25
- margin_index: int32 [4, 72, 1024], P(None, 'lat', 'lon'), may hold values from 0 to 1023
- margin_weight: float32 [4, 72, 1024], P(None, 'lat', 'lon'), may hold values from 0.05 to 0.6
- sea_mask: int32 [72, 1024], P('lat', 'lon'), may hold values 0 or 1
Outputs:
- grad_state: float32 [72, 1024, 128], P('lat', 'lon')
- grad_embed: float32 [16384, 256], P(('lat', 'lon'))
- grad_projection: float32 [256, 128], replicated
- grad_kernel: float32 [7, 7, 128], replicated
- grad_gain: float32 [128], replicated
- grad_w_in: float32 [128, 512], replicated
- grad_w_out: float32 [512, 128], replicated
All inputs are finite; a program needn't handle non-finite values. No bound on the sum of `sea_mask` on one device may be relied on, other than what follows from the above.
Results may differ from a plain program's by a relative error of at most 0.0058.
Values may be sent and summed in bfloat16 or wider, within the bound.
No kernel may reach another device: no remote copies, remote signals or barrier semaphores. Data moves between devices by JAX's collectives and lax.ppermute only.
A program may use at most 64 MiB of HBM per device.

v0:
```python
import jax
import jax.numpy as jnp
from jax import lax
from jax.sharding import PartitionSpec as P

EPSILON = 1e-05


def shifted(x, axis, by):
    size = lax.axis_size(axis)
    pairs = [(i, i + by) for i in range(size) if 0 <= i + by < size]
    return lax.ppermute(x, axis, pairs)


def with_halo(block, sides, width):
    for axis, dim in sides:
        count = lax.axis_size(axis)
        forward = [(i, i + 1) for i in range(count - 1)]
        forward.append((count - 1, 0))
        backward = [(target, source) for source, target in forward]
        low = lax.ppermute(
            lax.slice_in_dim(block, block.shape[dim] - width, None, axis=dim), axis, forward
        )
        high = lax.ppermute(lax.slice_in_dim(block, 0, width, axis=dim), axis, backward)
        block = jnp.concatenate([low, block, high], axis=dim)
    return block


def depthwise(padded, kernel):
    height = padded.shape[0] - 6
    width = padded.shape[1] - 6
    total = jnp.zeros((height, width, padded.shape[2]), jnp.float32)
    for row_tap in range(7):
        for col_tap in range(7):
            total = (
                total
                + padded[row_tap : row_tap + height, col_tap : col_tap + width]
                * kernel[row_tap, col_tap]
            )
    return total


def depthwise_back(padded, kernel):
    height = padded.shape[0] - 6
    width = padded.shape[1] - 6
    total = jnp.zeros((height, width, padded.shape[2]), jnp.float32)
    for row_tap in range(7):
        for col_tap in range(7):
            total = (
                total
                + padded[6 - row_tap : 6 - row_tap + height, 6 - col_tap : 6 - col_tap + width]
                * kernel[row_tap, col_tap]
            )
    return total


def kernel_grad(grad, padded):
    height = grad.shape[0]
    width = grad.shape[1]
    pieces = []
    for row_tap in range(7):
        for col_tap in range(7):
            pieces.append(
                jnp.sum(
                    grad * padded[row_tap : row_tap + height, col_tap : col_tap + width],
                    axis=(0, 1),
                )
            )
    return jnp.stack(pieces).reshape(7, 7, grad.shape[2])


def norm_forward(field):
    center = field - jnp.mean(field, axis=-1, keepdims=True)
    sigma = jnp.sqrt(jnp.mean(center * center, axis=-1, keepdims=True) + EPSILON)
    return (center / sigma, sigma)


def norm_back(g_ln, normed, sigma, gain):
    gain_grad = jnp.sum(g_ln * normed, axis=(0, 1))
    g_norm = g_ln * gain
    g_field = (
        g_norm
        - jnp.mean(g_norm, axis=-1, keepdims=True)
        - normed * jnp.mean(g_norm * normed, axis=-1, keepdims=True)
    ) / sigma
    return (g_field, gain_grad)


def gelu_tanh(value):
    return jax.nn.gelu(value, approximate=True)


def mlp_back(ln_rows, gy_rows, w_in, w_out):
    pre_act = jnp.dot(ln_rows, w_in, preferred_element_type=jnp.float32)
    hidden, pullback = jax.vjp(gelu_tanh, pre_act)
    hidden = hidden.astype(jnp.bfloat16)
    grad_out = lax.dot_general(
        hidden, gy_rows, (((0,), (0,)), ((), ())), preferred_element_type=jnp.float32
    )
    g_hidden = lax.dot_general(
        gy_rows, w_out, (((1,), (1,)), ((), ())), preferred_element_type=jnp.float32
    )
    g_pre = pullback(g_hidden)[0].astype(jnp.bfloat16)
    grad_in = lax.dot_general(
        ln_rows, g_pre, (((0,), (0,)), ((), ())), preferred_element_type=jnp.float32
    )
    g_ln = lax.dot_general(
        g_pre, w_in, (((1,), (1,)), ((), ())), preferred_element_type=jnp.float32
    )
    return (g_ln, grad_in, grad_out)


def clear_ends(padded):
    band = lax.axis_index("lat")
    bands = lax.axis_size("lat")
    position = jnp.arange(padded.shape[0], dtype=jnp.int32)
    dropped = (band == 0) & (position < 3) | (band == bands - 1) & (position >= padded.shape[0] - 3)
    return padded * jnp.where(dropped, 0.0, 1.0).astype(jnp.float32)[:, None, None]


def margin_block(index_rows, weight_rows, slots):
    columns = jnp.arange(slots, dtype=jnp.int32)[None, :]
    dense = jnp.zeros((index_rows.shape[1], slots), jnp.float32)
    for slot in range(index_rows.shape[0]):
        dense = dense + jnp.where(
            index_rows[slot][:, None] == columns, weight_rows[slot][:, None], 0.0
        )
    return dense


def block_rows(height, width):
    limit = max(1, 2048 // width)
    best = 1
    for count in range(1, height + 1):
        if height % count == 0 and count <= limit:
            best = count
    return best


def shards(
    ocean_state,
    cotangent,
    atm_embed,
    projection,
    dw_kernel,
    norm_gain,
    w_in,
    w_out,
    margin_index,
    margin_weight,
    sea_mask,
):
    cells_atm = atm_embed.shape[0]
    channels = projection.shape[1]
    height = ocean_state.shape[0]
    width = ocean_state.shape[1]
    margins = margin_index.shape[0]
    slots = 2 * cells_atm
    group = block_rows(height, width) * width
    blocks = height * width // group
    index_blocks = jnp.transpose(margin_index.reshape(margins, blocks, group), (1, 0, 2))
    weight_blocks = jnp.transpose(margin_weight.reshape(margins, blocks, group), (1, 0, 2))
    next_embed = shifted(atm_embed, "lat", -1)
    window_embed = jnp.concatenate([atm_embed, next_embed], axis=0)
    window = jnp.dot(window_embed, projection, preferred_element_type=jnp.float32).astype(
        jnp.bfloat16
    )
    window = lax.optimization_barrier(window).astype(jnp.float32)

    def forward_block(pair):
        dense = margin_block(pair[0], pair[1], slots)
        return jnp.dot(dense, window, precision=lax.Precision.HIGHEST)

    forcing = lax.map(forward_block, (index_blocks, weight_blocks)).reshape(height, width, channels)
    field = ocean_state.astype(jnp.float32) + forcing
    padded = clear_ends(with_halo(field, (("lat", 0), ("lon", 1)), 3))
    conv_out = depthwise(padded, dw_kernel)
    normed, sigma = norm_forward(conv_out)
    ln_cells = (normed * norm_gain).astype(jnp.bfloat16)
    g_out = cotangent.astype(jnp.float32)
    gy_cells = (sea_mask.astype(jnp.float32)[..., None] * g_out).astype(jnp.bfloat16)
    g_ln, grad_in, grad_out = mlp_back(
        ln_cells.reshape(-1, channels), gy_cells.reshape(-1, channels), w_in, w_out
    )
    g_conv, grad_gain = norm_back(g_ln.reshape(height, width, channels), normed, sigma, norm_gain)
    grad_kernel = kernel_grad(g_conv, padded)
    g_padded = clear_ends(with_halo(g_conv, (("lat", 0), ("lon", 1)), 3))
    grad_state = g_out + depthwise_back(g_padded, dw_kernel)
    state_blocks = grad_state.reshape(blocks, group, channels)

    def backward_block(total, triple):
        dense = margin_block(triple[0], triple[1], slots)
        added = lax.dot_general(
            dense,
            triple[2],
            (((0,), (0,)), ((), ())),
            precision=lax.Precision.HIGHEST,
            preferred_element_type=jnp.float32,
        )
        return (total + added, None)

    g_window, unused = lax.scan(
        backward_block,
        jnp.zeros((slots, channels), jnp.float32),
        (index_blocks, weight_blocks, state_blocks),
    )
    g_window_embed = jnp.dot(
        g_window, projection.astype(jnp.float32).T, precision=lax.Precision.HIGHEST
    )
    returned = shifted(g_window_embed[cells_atm:], "lat", 1)
    grad_embed = g_window_embed[:cells_atm] + returned
    grad_projection = jnp.dot(
        window_embed.astype(jnp.float32).T, g_window, precision=lax.Precision.HIGHEST
    )
    partials = (grad_projection, grad_kernel, grad_gain, grad_in, grad_out)
    along = lax.psum((partials[0], partials[1], partials[2], partials[3], partials[4]), "lon")
    totals = lax.psum((along[0], along[1], along[2], along[3], along[4]), "lat")
    return (grad_state, grad_embed, totals[0], totals[1], totals[2], totals[3], totals[4])


def solution(mesh):
    return jax.shard_map(
        shards,
        mesh=mesh,
        in_specs=(
            P("lat", "lon", None),
            P("lat", "lon", None),
            P(("lat", "lon"), None),
            P(),
            P(),
            P(),
            P(),
            P(),
            P(None, "lat", "lon"),
            P(None, "lat", "lon"),
            P("lat", "lon"),
        ),
        out_specs=(P("lat", "lon", None), P(("lat", "lon"), None), P(), P(), P(), P(), P()),
        check_vma=False,
    )
```

profile of v0, /device:TPU:0, one launch (start us, length us, event | category | flops | bytes accessed | tf_op | source)
XLA Modules:
  0.0 251.0 jit_solution(17589620157451192160)
XLA Ops:
  14.5 17.9 %while.21 = (s32[]{:T(128)}, f32[3,768,128]{2,1,0:T(8,128)S(1)}, s32[3,4,768]{2,1,0:T(4,128)S(1)}, f32[3,4,768]{2,1,0:T(4,128)S(1)}, f32[1024,128]{1,0:T(8,128)S...) while((s32[]{:T(128)}, f32[3,768,128]{2,1,0:T(8,128)S(1)}, s32[3,4,768]{2,1,0:T(4,128)S(1)}, ...), condition=%wide.region_1.2_spmd, body=%wide.region_0.1_spmd.sunk | while | flops 1216610304 | bytes 999605 | solution.py:174
  14.6 5.8 %fusion.140 = f32[3,768,128]{2,1,0:T(8,128)S(1)} fusion(f32[3,768,128]{2,1,0:T(8,128)S(1)} %get-tuple-element.345, s32[]{:T(128)S(6)} %copy.22, f32[1024,128]{1,0:T(8,128)S(1)} %get-tuple-element.358, f32[768]{0:T(1024)S(1)} %get-tuple-element.313, s32[768]{0:T(1024)S(1)} %get-tuple-element.314, f32[768]{0:T(1024)S(1)} %get-tuple-element.315, ...), kind=kOutput, calls=%fused_computation.22.clone.1 | convolution fusion | flops 1216610304 | bytes 950276 | tf_op jit(solution)/shard_map/while/body/eval_jaxpr/dot_general | solution.py:172
  20.6 5.8 %fusion.140 = f32[3,768,128]{2,1,0:T(8,128)S(1)} fusion(f32[3,768,128]{2,1,0:T(8,128)S(1)} %get-tuple-element.345, s32[]{:T(128)S(6)} %copy.22, f32[1024,128]{1,0:T(8,128)S(1)} %get-tuple-element.358, f32[768]{0:T(1024)S(1)} %get-tuple-element.313, s32[768]{0:T(1024)S(1)} %get-tuple-element.314, f32[768]{0:T(1024)S(1)} %get-tuple-element.315, ...), kind=kOutput, calls=%fused_computation.22.clone.1 | convolution fusion | flops 1216610304 | bytes 950276 | tf_op jit(solution)/shard_map/while/body/eval_jaxpr/dot_general | solution.py:172
  26.5 5.8 %fusion.140 = f32[3,768,128]{2,1,0:T(8,128)S(1)} fusion(f32[3,768,128]{2,1,0:T(8,128)S(1)} %get-tuple-element.345, s32[]{:T(128)S(6)} %copy.22, f32[1024,128]{1,0:T(8,128)S(1)} %get-tuple-element.358, f32[768]{0:T(1024)S(1)} %get-tuple-element.313, s32[768]{0:T(1024)S(1)} %get-tuple-element.314, f32[768]{0:T(1024)S(1)} %get-tuple-element.315, ...), kind=kOutput, calls=%fused_computation.22.clone.1 | convolution fusion | flops 1216610304 | bytes 950276 | tf_op jit(solution)/shard_map/while/body/eval_jaxpr/dot_general | solution.py:172
  33.6 3.0 %collective-permute-start.1 = (f32[3,256,128]{2,1,0:T(8,128)S(1)}, f32[3,256,128]{2,1,0:T(8,128)S(1)}, u32[]{:S(2)}, u32[]{:S(2)}) collective-permute-start(f32[3,256,128]{2,1,0:T(8,128)S(1)} %get-tuple-element.187), channel_id=1, source_target_pairs={{0,4},{4,8},{8,12},{12,16},{16,20},{20,24},{24,28},{28,0},{1,5},{5... | collective-permute-start | bytes 1179656 | tf_op jit(solution)/shard_map/ppermute | solution.py:21
  36.6 1.8 collective-permute-start.2
  41.2 4.9 %collective-permute-done.1 = f32[3,256,128]{2,1,0:T(8,128)S(1)} collective-permute-done((f32[3,256,128]{2,1,0:T(8,128)S(1)}, f32[3,256,128]{2,1,0:T(8,128)S(1)}, u32[]{:S(2)}, u32[]{:S(2)}) %collective-permute-start.1) | collective-permute-done | bytes 393248 | tf_op jit(solution)/shard_map/ppermute | solution.py:21
  49.2 2.3 collective-permute-start.4
  55.2 8.8 %fusion.109 = (f32[9,256]{1,0:T(8,128)S(1)}, f32[9,256,128]{2,1,0:T(8,128)S(1)}) fusion(f32[128]{0:T(128)} %get-tuple-element.236, f32[15,262,128]{2,1,0:T(8,128)S(1)} %maximum_multiply_fusion, f32[128]{0:T(128)} %get-tuple-element.237, f32[128]{0:T(128)S(1)} %get-tuple-element.190, f32[128]{0:T(128)S(1)} %get-tuple-element.191, f32[128]{0:T(128)S(1)} %copy-done.21, ...), kind=kLoop, calls=%fused_computation.305 | loop fusion | flops 28899072 | bytes 59016704 | tf_op jit(solution)/shard_map/reduce_sum | solution.py:73
  66.9 3.5 %fusion.54 = bf16[2304,512]{1,0:T(8,128)(2,1)S(1)} fusion(f32[2304,512]{1,0:T(8,128)S(1)} %fusion.112, bf16[2304,128]{1,0:T(8,128)(2,1)S(1)} %bitcast.196, bf16[512,128]{1,0:T(8,128)(2,1)S(1)} %copy-done.119), kind=kOutput, calls=%fused_computation.74 | convolution fusion | flops 325582848 | bytes 7798784 | tf_op jit(solution)/shard_map/dot_general | solution.py:100
  70.4 1.8 multiply_reduce_fusion.51
  72.2 2.9 %multiply_reduce_fusion = (f32[128]{0:T(128)}, f32[9,256]{1,0:T(8,128)S(1)}) fusion(f32[9,256,128]{2,1,0:T(8,128)} %bitcast.187, f32[9,256]{1,0:T(8,128)S(1)} %add_sqrt_fusion, f32[9,256,128]{2,1,0:T(8,128)S(1)} %get-tuple-element.180, f32[9,256]{1,0:T(8,128)S(1)} %broadcast_multiply_fusion.1, f32[128]{0:T(128)S(1)} %copy-done.20), kind=kLoop, calls=%fused_computation.180 | loop fusion | flops 2061952 | bytes 2387968 | tf_op jit(solution)/shard_map/reduce_sum | solution.py:79
  75.1 5.9 %multiply_reduce_fusion.1 = (f32[128]{0:T(128)}, f32[128]{0:T(128)}, f32[128]{0:T(128)}, f32[128]{0:T(128)}, f32[128]{0:T(128)}, /*index=5*/f32[128]{0:T(128)}, ...) fusion(f32[15,262,128]{2,1,0:T(8,128)S(1)} %maximum_multiply_fu, ...), kind=kLoop, calls=%fused_computation.181 | loop fusion | flops 12678912 | bytes 24819200 | tf_op jit(solution)/shard_map/reduce_sum | solution.py:64
  82.1 1.8 collective-permute-start.6
  83.9 2.4 fusion.55
  86.3 6.8 %collective-permute-done.5 = f32[3,256,128]{2,1,0:T(8,128)S(1)} collective-permute-done((f32[3,256,128]{2,1,0:T(8,128)S(1)}, f32[3,256,128]{2,1,0:T(8,128)S(1)}, u32[]{:S(2)}, u32[]{:S(2)}) %collective-permute-start.5) | collective-permute-done | bytes 393248 | tf_op jit(solution)/shard_map/ppermute | solution.py:21
  93.1 1.9 collective-permute-start.7
  95.0 2.2 collective-permute-start.8
  100.5 9.5 %convert_add_fusion = f32[9,256,128]{2,1,0:T(8,128)} fusion(bf16[9,256,128]{2,1,0:T(8,128)(2,1)S(1)} %copy-done.11, f32[15,262,128]{2,1,0:T(8,128)S(1)} %maximum_multiply_fusion.1, f32[128]{0:T(128)} %get-tuple-element.236, f32[128]{0:T(128)} %get-tuple-element.237, f32[128]{0:T(128)S(1)} %get-tuple-element.190, f32[128]{0:T(128)S(1)} %get-tuple-element.191, ...), kind=kLoop, calls=%fused_computation.79 | loop fusion | flops 29196288 | bytes 59597312 | tf_op jit(solution)/shard_map/add | solution.py:188
  110.0 25.2 %while.22 = (s32[]{:T(128)}, f32[1024,128]{1,0:T(8,128)}, s32[3,4,768]{2,1,0:T(4,128)S(1)}, f32[3,4,768]{2,1,0:T(4,128)S(1)}, f32[3,768,128]{2,1,0:T(8,128)}, /*index=5*/s32[]{:T(128)}, s32[]{:T(128)}, s32[]{}, s32[]{}, s32[]{}) while((s32[]{:T(128)}, f32[1024,128]{1,0:T(8,128)}, s32[3,4,768]{2,1,0:T(4,128)S(1)}, ...), condition=%wide.region_7.8_spmd.clone, body=%wide.region_6.7_spmd.clone.sunk | while | flops 1216872448 | bytes 1515711 | solution.py:202
  110.1 8.2 %fusion.143 = f32[1024,128]{1,0:T(8,128)} fusion(f32[768]{0:T(1024)S(1)} %get-tuple-element.326, s32[768]{0:T(1024)S(1)} %get-tuple-element.327, f32[768]{0:T(1024)S(1)} %get-tuple-element.328, s32[768]{0:T(1024)S(1)} %get-tuple-element.329, f32[768]{0:T(1024)S(1)} %get-tuple-element.330, s32[768]{0:T(1024)S(1)} %get-tuple-element.331, ...), kind=kOutput, calls=%fused_computation.53.clone.1 | convolution fusion | flops 1216872448 | bytes 1466373 | tf_op jit(solution)/shard_map/while/body/eval_jaxpr/dot_general | solution.py:193
  118.4 8.4 %fusion.143 = f32[1024,128]{1,0:T(8,128)} fusion(f32[768]{0:T(1024)S(1)} %get-tuple-element.326, s32[768]{0:T(1024)S(1)} %get-tuple-element.327, f32[768]{0:T(1024)S(1)} %get-tuple-element.328, s32[768]{0:T(1024)S(1)} %get-tuple-element.329, f32[768]{0:T(1024)S(1)} %get-tuple-element.330, s32[768]{0:T(1024)S(1)} %get-tuple-element.331, ...), kind=kOutput, calls=%fused_computation.53.clone.1 | convolution fusion | flops 1216872448 | bytes 1466373 | tf_op jit(solution)/shard_map/while/body/eval_jaxpr/dot_general | solution.py:193
  126.9 8.4 %fusion.143 = f32[1024,128]{1,0:T(8,128)} fusion(f32[768]{0:T(1024)S(1)} %get-tuple-element.326, s32[768]{0:T(1024)S(1)} %get-tuple-element.327, f32[768]{0:T(1024)S(1)} %get-tuple-element.328, s32[768]{0:T(1024)S(1)} %get-tuple-element.329, f32[768]{0:T(1024)S(1)} %get-tuple-element.330, s32[768]{0:T(1024)S(1)} %get-tuple-element.331, ...), kind=kOutput, calls=%fused_computation.53.clone.1 | convolution fusion | flops 1216872448 | bytes 1466373 | tf_op jit(solution)/shard_map/while/body/eval_jaxpr/dot_general | solution.py:193
  135.2 2.5 %fusion.114 = f32[256,128]{1,0:T(8,128)} fusion(bf16[1024,256]{1,0:T(8,128)(2,1)} %copy-done.9, f32[1024,128]{1,0:T(8,128)} %get-tuple-element.62), kind=kOutput, calls=%fused_computation.310 | convolution fusion | flops 402653184 | bytes 1179648 | tf_op jit(solution)/shard_map/dot_general | solution.py:212
  138.1 2.7 %multiply_reduce_fusion.19 = (f32[128]{0:T(128)S(1)}, f32[128]{0:T(128)S(1)}, f32[128]{0:T(128)S(1)}, f32[128]{0:T(128)S(1)}, f32[128]{0:T(128)S(1)}, /*index=5*...) fusion(f32[9,256,128]{2,1,0:T(8,128)S(1)} %get-tuple-element.17, ...), kind=kLoop, calls=%fused_computation.199 | loop fusion | flops 10614528 | bytes 22422528 | tf_op jit(solution)/shard_map/reduce_sum | solution.py:64
  143.2 2.1 collective-permute-start.9
  145.3 35.3 %all-reduce.9.cloned.1.call-done = (f32[256,128]{1,0:T(8,128)}, f32[128,512]{1,0:T(8,128)}, f32[512,128]{1,0:T(8,128)}) async-done(((f32[256,128]{1,0:T(8,128)}, f32[128,512]{1,0:T(8,128)}, f32[512,128]{1,0:T(8,128)}), (f32[256,128]{1,0:T(8,128)}, f32[128,512]{1,0:T(8,128)}, f32[512,128]{1,0:T(8,128)})) %all-reduce.9.cloned.1.call-update) | async-done | bytes 655376 | tf_op jit(solution)/shard_map/psum | solution.py:216
  180.9 2.0 multiply_reduce_fusion.37
  183.2 17.6 %all-reduce.2 = (f32[7,7,128]{2,1,0:T(8,128)S(1)}, f32[128]{0:T(128)S(1)}) all-reduce(f32[7,7,128]{2,1,0:T(8,128)S(1)} %reshape.131, f32[128]{0:T(128)S(1)} %copy-done.117), channel_id=1, replica_groups=mesh['lat'=8,'lon'=4] {'lon'}, use_global_device_ids=true, to_apply=%region_59.60 | all-reduce | flops 6400 | bytes 51200 | tf_op jit(solution)/shard_map/psum | solution.py:216
  200.8 23.2 %all-reduce = (f32[7,7,128]{2,1,0:T(8,128)}, f32[128]{0:T(128)}) all-reduce(f32[7,7,128]{2,1,0:T(8,128)S(1)} %get-tuple-element.173, f32[128]{0:T(128)S(1)} %get-tuple-element.174), channel_id=1, replica_groups=mesh['lat'=8,'lon'=4] {'lat'}, use_global_device_ids=true, to_apply=%region_60.61 | all-reduce | flops 6400 | bytes 51200 | tf_op jit(solution)/shard_map/psum | solution.py:217
  224.0 2.1 slice_add_fusion
  226.1 13.2 %all-reduce.7.cloned.1.call-done = (f32[256,128]{1,0:T(8,128)}, f32[128,512]{1,0:T(8,128)}, f32[512,128]{1,0:T(8,128)}) async-done(((f32[256,128]{1,0:T(8,128)}, f32[128,512]{1,0:T(8,128)}, f32[512,128]{1,0:T(8,128)}), (f32[256,128]{1,0:T(8,128)}, f32[128,512]{1,0:T(8,128)}, f32[512,128]{1,0:T(8,128)})) %all-reduce.7.cloned.1.call-update) | async-done | bytes 655376 | tf_op jit(solution)/shard_map/psum | solution.py:217
  (307 shorter events, 32.4 us)
Async XLA Ops:
  7.2 58.4 %copy-start = (bf16[128,512]{1,0:T(8,128)(2,1)S(1)}, bf16[128,512]{1,0:T(8,128)(2,1)}, u32[]{:S(2)}) copy-start(bf16[128,512]{1,0:T(8,128)(2,1)} %param.21) | copy-start | bytes 393220
  7.2 6.5 %copy-start.19 = (bf16[256,128]{1,0:T(8,128)(2,1)S(1)}, bf16[256,128]{1,0:T(8,128)(2,1)}, u32[]{:S(2)}) copy-start(bf16[256,128]{1,0:T(8,128)(2,1)} %param.18) | copy-start | bytes 196612
  7.2 173.5 %all-reduce.9.cloned.1.call-start = ((), (), s32[]{:S(2)}) async-start(), calls=%async_computation.1 | async-start | bytes 1310720 | tf_op jit(solution)/shard_map/psum | solution.py:216
  7.2 6.4 %collective-permute-start = (bf16[512,256]{1,0:T(8,128)(2,1)}, bf16[512,256]{1,0:T(8,128)(2,1)S(1)}, u32[]{:S(2)}, u32[]{:S(2)}) collective-permute-start(bf16[512,256]{1,0:T(8,128)(2,1)} %param.17), channel_id=1, source_target_pairs={{4,0},{8,4},{12,8},{16,12},{20,16},{24,20},{28,24},{5,1},{9,5},{13... | collective-permute-start | bytes 786440 | tf_op jit(solution)/shard_map/ppermute | solution.py:12
  33.6 6.4 %copy-start.10 = (bf16[9,256,128]{2,1,0:T(8,128)(2,1)S(1)}, bf16[9,256,128]{2,1,0:T(8,128)(2,1)}, u32[]{:S(2)}) copy-start(bf16[9,256,128]{2,1,0:T(8,128)(2,1)} %param.16) | copy-start | bytes 1769476
  33.6 12.5 %collective-permute-start.1 = (f32[3,256,128]{2,1,0:T(8,128)S(1)}, f32[3,256,128]{2,1,0:T(8,128)S(1)}, u32[]{:S(2)}, u32[]{:S(2)}) collective-permute-start(f32[3,256,128]{2,1,0:T(8,128)S(1)} %get-tuple-element.187), channel_id=1, source_target_pairs={{0,4},{4,8},{8,12},{12,16},{16,20},{20,24},{24,28},{28,0},{1,5},{5... | collective-permute-start | bytes 1179656 | tf_op jit(solution)/shard_map/ppermute | solution.py:21
  36.6 9.6 %collective-permute-start.2 = (f32[3,256,128]{2,1,0:T(8,128)S(1)}, f32[3,256,128]{2,1,0:T(8,128)S(1)}, u32[]{:S(2)}, u32[]{:S(2)}) collective-permute-start(f32[3,256,128]{2,1,0:T(8,128)S(1)} %get-tuple-element.188), channel_id=1, source_target_pairs={{4,0},{8,4},{12,8},{16,12},{20,16},{24,20},{28,24},{0,28},{5,1},{9... | collective-permute-start | bytes 1179656 | tf_op jit(solution)/shard_map/ppermute | solution.py:24
  47.7 5.8 %collective-permute-start.3 = (f32[15,3,128]{2,1,0:T(4,128)S(1)}, f32[15,3,128]{2,1,0:T(4,128)S(1)}, u32[]{:S(2)}, u32[]{:S(2)}) collective-permute-start(f32[15,3,128]{2,1,0:T(4,128)S(1)} %get-tuple-element.183), channel_id=1, source_target_pairs={{0,1},{1,2},{2,3},{3,0},{4,5},{5,6},{6,7},{7,4},{8,9},{9,10},{10,1... | collective-permute-start | bytes 69128 | tf_op jit(solution)/shard_map/ppermute | solution.py:21
  49.2 4.2 %collective-permute-start.4 = (f32[15,3,128]{2,1,0:T(4,128)S(1)}, f32[15,3,128]{2,1,0:T(4,128)}, u32[]{:S(2)}, u32[]{:S(2)}) collective-permute-start(f32[15,3,128]{2,1,0:T(4,128)S(1)} %get-tuple-element.184), channel_id=1, source_target_pairs={{1,0},{2,1},{3,2},{0,3},{5,4},{6,5},{7,6},{4,7},{9,8},{10,9},{11,1... | collective-permute-start | bytes 69128 | tf_op jit(solution)/shard_map/ppermute | solution.py:24
  51.5 3.4 %copy-start.21 = (f32[128]{0:T(128)S(1)}, f32[128]{0:T(128)}, u32[]{:S(2)}) copy-start(f32[128]{0:T(128)} %get-tuple-element.192) | copy-start | bytes 1540
  51.5 3.4 %copy-start.23 = (f32[128]{0:T(128)S(1)}, f32[128]{0:T(128)}, u32[]{:S(2)}) copy-start(f32[128]{0:T(128)} %get-tuple-element.193) | copy-start | bytes 1540
  51.5 3.4 %copy-start.25 = (f32[128]{0:T(128)S(1)}, f32[128]{0:T(128)}, u32[]{:S(2)}) copy-start(f32[128]{0:T(128)} %get-tuple-element.194) | copy-start | bytes 1540
  51.5 3.4 %copy-start.27 = (f32[128]{0:T(128)S(1)}, f32[128]{0:T(128)}, u32[]{:S(2)}) copy-start(f32[128]{0:T(128)} %get-tuple-element.195) | copy-start | bytes 1540
  51.5 3.4 %copy-start.29 = (f32[128]{0:T(128)S(1)}, f32[128]{0:T(128)}, u32[]{:S(2)}) copy-start(f32[128]{0:T(128)} %get-tuple-element.196) | copy-start | bytes 1540
  51.5 3.4 %copy-start.31 = (f32[128]{0:T(128)S(1)}, f32[128]{0:T(128)}, u32[]{:S(2)}) copy-start(f32[128]{0:T(128)} %get-tuple-element.197) | copy-start | bytes 1540
  51.6 3.4 %copy-start.33 = (f32[128]{0:T(128)S(1)}, f32[128]{0:T(128)}, u32[]{:S(2)}) copy-start(f32[128]{0:T(128)} %get-tuple-element.198) | copy-start | bytes 1540
  51.6 3.4 %copy-start.35 = (f32[128]{0:T(128)S(1)}, f32[128]{0:T(128)}, u32[]{:S(2)}) copy-start(f32[128]{0:T(128)} %get-tuple-element.199) | copy-start | bytes 1540
  51.6 3.4 %copy-start.37 = (f32[128]{0:T(128)S(1)}, f32[128]{0:T(128)}, u32[]{:S(2)}) copy-start(f32[128]{0:T(128)} %get-tuple-element.200) | copy-start | bytes 1540
  51.6 3.4 %copy-start.39 = (f32[128]{0:T(128)S(1)}, f32[128]{0:T(128)}, u32[]{:S(2)}) copy-start(f32[128]{0:T(128)} %get-tuple-element.201) | copy-start | bytes 1540
  51.6 3.4 %copy-start.41 = (f32[128]{0:T(128)S(1)}, f32[128]{0:T(128)}, u32[]{:S(2)}) copy-start(f32[128]{0:T(128)} %get-tuple-element.202) | copy-start | bytes 1540
  64.0 8.2 %copy-start.1 = (f32[9,256,128]{2,1,0:T(8,128)}, f32[9,256,128]{2,1,0:T(8,128)S(1)}, u32[]{:S(2)}) copy-start(f32[9,256,128]{2,1,0:T(8,128)S(1)} %get-tuple-element.180) | copy-start | bytes 3538948
  66.5 3.9 %copy-start.7 = (f32[2304,512]{1,0:T(8,128)}, f32[2304,512]{1,0:T(8,128)S(1)}, u32[]{:S(2)}) copy-start(f32[2304,512]{1,0:T(8,128)S(1)} %fusion.112) | copy-start | bytes 14155780
  72.2 11.7 %slice-start = ((s8[4718592]{0:T(1024)(128)(4,1)}), s8[4194304]{0:T(1024)(128)(4,1)S(1)}, s32[]{:S(2)}) async-start(s8[4718592]{0:T(1024)(128)(4,1)} %bitcast.191), calls=%async_computation.2 | async-start | bytes 8388608
  75.1 8.8 %slice-start.1 = ((s8[4718592]{0:T(1024)(128)(4,1)}), s8[524288]{0:T(1024)(128)(4,1)S(1)}, s32[]{:S(2)}) async-start(s8[4718592]{0:T(1024)(128)(4,1)} %bitcast.191), calls=%async_computation.3 | async-start | bytes 1048576
  81.0 12.1 %collective-permute-start.5 = (f32[3,256,128]{2,1,0:T(8,128)S(1)}, f32[3,256,128]{2,1,0:T(8,128)S(1)}, u32[]{:S(2)}, u32[]{:S(2)}) collective-permute-start(f32[3,256,128]{2,1,0:T(8,128)S(1)} %get-tuple-element.185), channel_id=1, source_target_pairs={{0,4},{4,8},{8,12},{12,16},{16,20},{20,24},{24,28},{28,0},{1,5},{5... | collective-permute-start | bytes 1179656 | tf_op jit(solution)/shard_map/ppermute | solution.py:21
  82.1 11.0 %collective-permute-start.6 = (f32[3,256,128]{2,1,0:T(8,128)S(1)}, f32[3,256,128]{2,1,0:T(8,128)S(1)}, u32[]{:S(2)}, u32[]{:S(2)}) collective-permute-start(f32[3,256,128]{2,1,0:T(8,128)S(1)} %get-tuple-element.186), channel_id=1, source_target_pairs={{4,0},{8,4},{12,8},{16,12},{20,16},{24,20},{28,24},{0,28},{5,1},{9... | collective-permute-start | bytes 1179656 | tf_op jit(solution)/shard_map/ppermute | solution.py:24
  83.9 13.3 %copy-start.4 = (bf16[2304,512]{1,0:T(8,128)(2,1)S(1)}, bf16[2304,512]{1,0:T(8,128)(2,1)}, u32[]{:S(2)}) copy-start(bf16[2304,512]{1,0:T(8,128)(2,1)} %copy-done.3) | copy-start | bytes 7077892
  86.3 10.9 %copy-start.6 = (bf16[9,256,128]{2,1,0:T(8,128)(2,1)S(1)}, bf16[9,256,128]{2,1,0:T(8,128)(2,1)}, u32[]{:S(2)}) copy-start(bf16[9,256,128]{2,1,0:T(8,128)(2,1)} %copy-done.5) | copy-start | bytes 1769476
  93.1 6.0 %collective-permute-start.7 = (f32[15,3,128]{2,1,0:T(4,128)S(1)}, f32[15,3,128]{2,1,0:T(4,128)S(1)}, u32[]{:S(2)}, u32[]{:S(2)}) collective-permute-start(f32[15,3,128]{2,1,0:T(4,128)S(1)} %get-tuple-element.181), channel_id=1, source_target_pairs={{0,1},{1,2},{2,3},{3,0},{4,5},{5,6},{6,7},{7,4},{8,9},{9,10},{10,1... | collective-permute-start | bytes 69128 | tf_op jit(solution)/shard_map/ppermute | solution.py:21
  95.0 4.2 %collective-permute-start.8 = (f32[15,3,128]{2,1,0:T(4,128)S(1)}, f32[15,3,128]{2,1,0:T(4,128)S(1)}, u32[]{:S(2)}, u32[]{:S(2)}) collective-permute-start(f32[15,3,128]{2,1,0:T(4,128)S(1)} %get-tuple-element.182), channel_id=1, source_target_pairs={{1,0},{2,1},{3,2},{0,3},{5,4},{6,5},{7,6},{4,7},{9,8},{10,9},{11,1... | collective-permute-start | bytes 69128 | tf_op jit(solution)/shard_map/ppermute | solution.py:24
  137.8 101.5 %all-reduce.7.cloned.1.call-start = ((), (), s32[]{:S(2)}) async-start(), calls=%async_computation | async-start | bytes 1310720 | tf_op jit(solution)/shard_map/psum | solution.py:217
  143.2 80.8 %collective-permute-start.9 = (f32[512,256]{1,0:T(8,128)}, f32[512,256]{1,0:T(8,128)}, u32[]{:S(2)}, u32[]{:S(2)}) collective-permute-start(f32[512,256]{1,0:T(8,128)} %slice.901), channel_id=1, source_target_pairs={{0,4},{4,8},{8,12},{12,16},{16,20},{20,24},{24,28},{1,5},{5,9},{9,... | collective-permute-start | bytes 1572872 | tf_op jit(solution)/shard_map/ppermute | solution.py:12
  (102 other events, 228.1 us)
Sparse Core Ops, SparseCore 0:
  137.9 42.7 all-reduce.8
  184.1 55.1 all-reduce.6
where the time goes:
time: 252 us; the launch traced here: 251 us
  waiting for transfers between devices  62.3 us (25%)
  matrix products  55.4 us (22%)
  other arithmetic  40.9 us (16%)
  blocking collectives  40.8 us (16%)
  starting transfers between devices  19.4 us (8%)
  local copies, waits for them, and re-layouts  16.2 us (6%)
  between operations  16 us (6%)
    psum x1, waiting for transfers between devices, shards(): lax.psum((partials[0], partials[1], partials[2], partials[3], partials[4]...  35.3 us
    dot_general x3, matrix products, backward_block(): lax.dot_general(dense, triple[2], (((0,), (0,)), ((), ())), precision=lax...  24.9 us
    psum x1, blocking collectives, shards(): totals = lax.psum((along[0], along[1], along[2], along[3], along[4]), 'lat')  23.2 us
    psum x1, blocking collectives, shards(): lax.psum((partials[0], partials[1], partials[2], partials[3], partials[4]...  17.6 us
    dot_general x3, matrix products, forward_block(): return jnp.dot(dense, window, precision=lax.Precision.HIGHEST)  17.5 us
    ppermute x4, waiting for transfers between devices, with_halo(): lax.ppermute(lax.slice_in_dim(block, block.shape[dim] - width, None, axis...  13.6 us
    psum x1, waiting for transfers between devices, shards(): totals = lax.psum((along[0], along[1], along[2], along[3], along[4]), 'lat')  13.2 us
    reduce_sum x3, other arithmetic, kernel_grad(): jnp.sum(grad * padded[row_tap:row_tap + height, col_tap:col_tap + width],...  10.6 us
  transfers between devices with their start and end apart: 12, of which 8 were waited for; matrix products, arithmetic and copies ran while one was open for 8% of the time, Pallas kernels for 0%

commit v1 on v0

--- a/solution.py
+++ b/solution.py
@@ -10,6 +10,51 @@
     size = lax.axis_size(axis)
     pairs = [(i, i + by) for i in range(size) if 0 <= i + by < size]
     return lax.ppermute(x, axis, pairs)
+
+
+def xor_swap(x, axis, mask):
+    size = lax.axis_size(axis)
+    return lax.ppermute(x, axis, [(i, i ^ mask) for i in range(size)])
+
+
+def masks(axis):
+    size = lax.axis_size(axis)
+    if size & (size - 1):
+        return None
+    return [1 << k for k in range(size.bit_length() - 1)]
+
+
+def fold(value, axis, chosen):
+    for mask in chosen:
+        mine = value.astype(jnp.bfloat16)
+        other = xor_swap(mine, axis, mask)
+        value = mine.astype(jnp.float32) + other.astype(jnp.float32)
+    return value
+
+
+def sum_over_mesh(value):
+    for axis in ("lat", "lon"):
+        steps = masks(axis)
+        value = lax.psum(value, axis) if steps is None else fold(value, axis, steps)
+    return value
+
+
+def sum_pair_over_mesh(first, second):
+    steps = masks("lat")
+    if not steps or masks("lon") is None:
+        return lax.psum((first, second), ("lat", "lon"))
+    odd = lax.rem(lax.axis_index("lat"), 2) == 1
+    first, second = first.astype(jnp.bfloat16), second.astype(jnp.bfloat16)
+    kept = jnp.where(odd, second, first)
+    given = xor_swap(jnp.where(odd, first, second), "lat", 1)
+    value = kept.astype(jnp.float32) + given.astype(jnp.float32)
+    value = fold(value, "lat", steps[1:])
+    value = fold(value, "lon", masks("lon"))
+    mine = value.astype(jnp.bfloat16)
+    other = xor_swap(mine, "lat", 1)
+    low = jnp.where(odd, other, mine).astype(jnp.float32)
+    high = jnp.where(odd, mine, other).astype(jnp.float32)
+    return low, high
 
 
 def with_halo(block, sides, width):
@@ -18,10 +63,12 @@
         forward = [(i, i + 1) for i in range(count - 1)]
         forward.append((count - 1, 0))
         backward = [(target, source) for source, target in forward]
-        low = lax.ppermute(
-            lax.slice_in_dim(block, block.shape[dim] - width, None, axis=dim), axis, forward
+        rims = (
+            lax.slice_in_dim(block, block.shape[dim] - width, None, axis=dim).astype(jnp.bfloat16),
+            lax.slice_in_dim(block, 0, width, axis=dim).astype(jnp.bfloat16),
         )
-        high = lax.ppermute(lax.slice_in_dim(block, 0, width, axis=dim), axis, backward)
+        low = lax.ppermute(rims[0], axis, forward).astype(jnp.float32)
+        high = lax.ppermute(rims[1], axis, backward).astype(jnp.float32)
         block = jnp.concatenate([low, block, high], axis=dim)
     return block
 
@@ -95,7 +142,7 @@
     hidden, pullback = jax.vjp(gelu_tanh, pre_act)
     hidden = hidden.astype(jnp.bfloat16)
     grad_out = lax.dot_general(
-        hidden, gy_rows, (((0,), (0,)), ((), ())), preferred_element_type=jnp.float32
+        gy_rows, hidden, (((0,), (0,)), ((), ())), preferred_element_type=jnp.float32
     )
     g_hidden = lax.dot_general(
         gy_rows, w_out, (((1,), (1,)), ((), ())), preferred_element_type=jnp.float32
@@ -173,7 +220,7 @@
 
     forcing = lax.map(forward_block, (index_blocks, weight_blocks)).reshape(height, width, channels)
     field = ocean_state.astype(jnp.float32) + forcing
-    padded = clear_ends(with_halo(field, (("lat", 0), ("lon", 1)), 3))
+    padded = clear_ends(with_halo(field, (("lon", 1), ("lat", 0)), 3))
     conv_out = depthwise(padded, dw_kernel)
     normed, sigma = norm_forward(conv_out)
     ln_cells = (normed * norm_gain).astype(jnp.bfloat16)
@@ -182,9 +229,10 @@
     g_ln, grad_in, grad_out = mlp_back(
         ln_cells.reshape(-1, channels), gy_cells.reshape(-1, channels), w_in, w_out
     )
+    grad_in, grad_out = sum_pair_over_mesh(grad_in, grad_out)
     g_conv, grad_gain = norm_back(g_ln.reshape(height, width, channels), normed, sigma, norm_gain)
     grad_kernel = kernel_grad(g_conv, padded)
-    g_padded = clear_ends(with_halo(g_conv, (("lat", 0), ("lon", 1)), 3))
+    g_padded = clear_ends(with_halo(g_conv, (("lon", 1), ("lat", 0)), 3))
     grad_state = g_out + depthwise_back(g_padded, dw_kernel)
     state_blocks = grad_state.reshape(blocks, group, channels)
 
@@ -212,10 +260,21 @@
     grad_projection = jnp.dot(
         window_embed.astype(jnp.float32).T, g_window, precision=lax.Precision.HIGHEST
     )
-    partials = (grad_projection, grad_kernel, grad_gain, grad_in, grad_out)
-    along = lax.psum((partials[0], partials[1], partials[2], partials[3], partials[4]), "lon")
-    totals = lax.psum((along[0], along[1], along[2], along[3], along[4]), "lat")
-    return (grad_state, grad_embed, totals[0], totals[1], totals[2], totals[3], totals[4])
+    taps = grad_kernel.shape[0] * grad_kernel.shape[1]
+    late = jnp.concatenate(
+        [grad_projection, grad_kernel.reshape(taps, channels), grad_gain[None]], axis=0
+    )
+    late = sum_over_mesh(late)
+    rows = projection.shape[0]
+    return (
+        grad_state,
+        grad_embed,
+        late[:rows],
+        late[rows : rows + taps].reshape(grad_kernel.shape),
+        late[rows + taps],
+        grad_in,
+        grad_out.T,
+    )
 
 
 def solution(mesh):

time: 252 us -> 157 us (0.62)
  blocking collectives: 40.8 us -> 0 us
  waiting for transfers between devices: 62.3 us -> 25.3 us
  between operations: 16 us -> 2.89 us
  starting transfers between devices: 19.4 us -> 31.7 us
  matrix products: 55.4 us -> 46.7 us
  local copies, waits for them, and re-layouts: 16.2 us -> 10.6 us
    psum x2 -> x0, waiting for transfers between devices: 48.5 us -> none  [the longest x1 35.3 us: shards(): lax.psum((partials[0], partials[1], partials[2], partials[3], partials[4]...]
    psum x2 -> x0, blocking collectives: 40.8 us -> none  [the longest x1 23.2 us: shards(): totals = lax.psum((along[0], along[1], along[2], along[3], along[4]), 'lat')]
    ppermute x8 -> x19, starting transfers between devices: 15.6 us -> 28.4 us  [the longest x11 13.8 us: xor_swap(): return lax.ppermute(x, axis, [(i, i ^ mask) for i in range(size)])]
    ppermute x8 -> x19, waiting for transfers between devices: 13.7 us -> 25.2 us  [the longest x11 17.7 us: xor_swap(): return lax.ppermute(x, axis, [(i, i ^ mask) for i in range(size)])]
    unnamed x248 -> x260, local copies, waits for them, and re-layouts: 9.74 us -> 4.37 us
    dot_general x3, matrix products: 24.9 us -> 19.6 us  [backward_block(): lax.dot_general(dense, triple[2], (((0,), (0,)), ((), ())), precision=lax...]
  transfers between devices with their start and end apart: 12 -> 21, of which waited for: 8 -> 11; matrix products, arithmetic and copies ran while one was open for 8% -> 29% of each run, Pallas kernels for 0% -> 0%
where the time goes in v1:
time: 157 us; the launch traced here: 156 us
  matrix products  46.7 us (30%)
  other arithmetic  39.1 us (25%)
  starting transfers between devices  31.7 us (20%)
  waiting for transfers between devices  25.3 us (16%)
  local copies, waits for them, and re-layouts  10.6 us (7%)
  between operations  2.89 us (2%)
    dot_general x3, matrix products, backward_block(): lax.dot_general(dense, triple[2], (((0,), (0,)), ((), ())), precision=lax...  19.6 us
    ppermute x11, waiting for transfers between devices, xor_swap(): return lax.ppermute(x, axis, [(i, i ^ mask) for i in range(size)])  17.7 us
    dot_general x3, matrix products, forward_block(): return jnp.dot(dense, window, precision=lax.Precision.HIGHEST)  17.5 us
    ppermute x11, starting transfers between devices, xor_swap(): return lax.ppermute(x, axis, [(i, i ^ mask) for i in range(size)])  13.8 us
    reduce_sum x3, other arithmetic, kernel_grad(): jnp.sum(grad * padded[row_tap:row_tap + height, col_tap:col_tap + width],...  10.4 us
    add x1, other arithmetic, shards(): grad_state = g_out + depthwise_back(g_padded, dw_kernel)  8.75 us
    reduce_sum x1, other arithmetic, norm_forward(): center = field - jnp.mean(field, axis=-1, keepdims=True)  8.38 us
    ppermute x4, starting transfers between devices, with_halo(): high = lax.ppermute(rims[1], axis, backward).astype(jnp.float32)  7.65 us
  transfers between devices with their start and end apart: 21, of which 11 were waited for; matrix products, arithmetic and copies ran while one was open for 29% of the time, Pallas kernels for 0%

profile of v1, /device:TPU:0, one launch (start us, length us, event | category | flops | bytes accessed | tf_op | source)
XLA Modules:
  0.0 156.5 jit_solution(17463216911896509877)
XLA Ops:
  6.6 2.2 %fusion.56 = bf16[9,256,128]{2,1,0:T(8,128)(2,1)} fusion(bf16[9,256,128]{2,1,0:T(8,128)(2,1)} %param.16, f32[9,256]{1,0:T(8,128)S(1)} %convert_element_type.160), kind=kLoop, calls=%fused_computation.82 | loop fusion | flops 884736 | bytes 1188864 | tf_op jit(solution)/shard_map/convert_element_type | solution.py:228
  9.8 17.9 %while.21 = (s32[]{:T(128)}, f32[3,768,128]{2,1,0:T(8,128)S(1)}, s32[3,4,768]{2,1,0:T(4,128)S(1)}, f32[3,4,768]{2,1,0:T(4,128)S(1)}, f32[1024,128]{1,0:T(8,128)S...) while((s32[]{:T(128)}, f32[3,768,128]{2,1,0:T(8,128)S(1)}, s32[3,4,768]{2,1,0:T(4,128)S(1)}, ...), condition=%wide.region_1.2_spmd, body=%wide.region_0.1_spmd.sunk | while | flops 1216610304 | bytes 999597 | solution.py:221
  9.9 5.8 %fusion.142 = f32[3,768,128]{2,1,0:T(8,128)S(1)} fusion(f32[3,768,128]{2,1,0:T(8,128)S(1)} %get-tuple-element.349, s32[]{:T(128)} %get-tuple-element.348, f32[1024,128]{1,0:T(8,128)S(1)} %get-tuple-element.362, f32[768]{0:T(1024)S(1)} %get-tuple-element.317, s32[768]{0:T(1024)S(1)} %get-tuple-element.318, f32[768]{0:T(1024)S(1)} %get-tuple-element.319, ...), kind=kOutput, calls=%fused_computation.22.clone.1 | convolution fusion | flops 1216610304 | bytes 950276 | tf_op jit(solution)/shard_map/while/body/eval_jaxpr/dot_general | solution.py:219
  15.8 5.9 %fusion.142 = f32[3,768,128]{2,1,0:T(8,128)S(1)} fusion(f32[3,768,128]{2,1,0:T(8,128)S(1)} %get-tuple-element.349, s32[]{:T(128)} %get-tuple-element.348, f32[1024,128]{1,0:T(8,128)S(1)} %get-tuple-element.362, f32[768]{0:T(1024)S(1)} %get-tuple-element.317, s32[768]{0:T(1024)S(1)} %get-tuple-element.318, f32[768]{0:T(1024)S(1)} %get-tuple-element.319, ...), kind=kOutput, calls=%fused_computation.22.clone.1 | convolution fusion | flops 1216610304 | bytes 950276 | tf_op jit(solution)/shard_map/while/body/eval_jaxpr/dot_general | solution.py:219
  21.8 5.8 %fusion.142 = f32[3,768,128]{2,1,0:T(8,128)S(1)} fusion(f32[3,768,128]{2,1,0:T(8,128)S(1)} %get-tuple-element.349, s32[]{:T(128)} %get-tuple-element.348, f32[1024,128]{1,0:T(8,128)S(1)} %get-tuple-element.362, f32[768]{0:T(1024)S(1)} %get-tuple-element.317, s32[768]{0:T(1024)S(1)} %get-tuple-element.318, f32[768]{0:T(1024)S(1)} %get-tuple-element.319, ...), kind=kOutput, calls=%fused_computation.22.clone.1 | convolution fusion | flops 1216610304 | bytes 950276 | tf_op jit(solution)/shard_map/while/body/eval_jaxpr/dot_general | solution.py:219
  29.0 3.1 %collective-permute-start.1 = (bf16[9,3,128]{2,1,0:T(4,128)(2,1)S(1)}, bf16[9,3,128]{2,1,0:T(4,128)(2,1)S(1)}, u32[]{:S(2)}, u32[]{:S(2)}) collective-permute-start(bf16[9,3,128]{2,1,0:T(4,128)(2,1)S(1)} %get-tuple-element.187), channel_id=1, source_target_pairs={{0,1},{1,2},{2,3},{3,0},{4,5},{5,6},{6,7},{7,4},{8,9},{9,10},{10,1... | collective-permute-start | bytes 20744 | tf_op jit(solution)/shard_map/ppermute | solution.py:70
  32.1 2.1 %collective-permute-start.2 = (bf16[9,3,128]{2,1,0:T(4,128)(2,1)S(1)}, bf16[9,3,128]{2,1,0:T(4,128)(2,1)S(1)}, u32[]{:S(2)}, u32[]{:S(2)}) collective-permute-start(bf16[9,3,128]{2,1,0:T(4,128)(2,1)S(1)} %get-tuple-element.188), channel_id=1, source_target_pairs={{1,0},{2,1},{3,2},{0,3},{5,4},{6,5},{7,6},{4,7},{9,8},{10,9},{11,1... | collective-permute-start | bytes 20744 | tf_op jit(solution)/shard_map/ppermute | solution.py:71
  36.2 2.5 %collective-permute-start.4 = (bf16[3,262,128]{2,1,0:T(8,128)(2,1)S(1)}, bf16[3,262,128]{2,1,0:T(8,128)(2,1)S(1)}, u32[]{:S(2)}, u32[]{:S(2)}) collective-permute-start(bf16[3,262,128]{2,1,0:T(8,128)(2,1)S(1)} %get-tuple-element.183), channel_id=1, source_target_pairs={{4,0},{8,4},{12,8},{16,12},{20,16},{24,20},{28,24},{0,28},{5,1},{9... | collective-permute-start | bytes 603656 | tf_op jit(solution)/shard_map/ppermute | solution.py:71
  39.7 2.4 %collective-permute-done.3 = bf16[3,262,128]{2,1,0:T(8,128)(2,1)S(1)} collective-permute-done((bf16[3,262,128]{2,1,0:T(8,128)(2,1)S(1)}, bf16[3,262,128]{2,1,0:T(8,128)(2,1)S(1)}, u32[]{:S(2)}, u32[]{:S(2)}) %collective-permute-start.3) | collective-permute-done | bytes 201248 | tf_op jit(solution)/shard_map/ppermute | solution.py:70
  44.1 8.4 %fusion.112 = (f32[9,256]{1,0:T(8,128)S(1)}, f32[9,256,128]{2,1,0:T(8,128)S(1)}) fusion(f32[128]{0:T(128)S(1)} %get-tuple-element.238, f32[15,262,128]{2,1,0:T(8,128)S(1)} %maximum_multiply_fusion, f32[128]{0:T(128)S(1)} %get-tuple-element.239, f32[128]{0:T(128)S(1)} %get-tuple-element.192, f32[128]{0:T(128)S(1)} %get-tuple-element.193, ...), kind=kLoop, calls=%fused_computation.374 | loop fusion | flops 28899072 | bytes 59016704 | tf_op jit(solution)/shard_map/reduce_sum | solution.py:120
  55.3 3.5 %fusion.54 = bf16[2304,512]{1,0:T(8,128)(2,1)S(1)} fusion(f32[2304,512]{1,0:T(8,128)S(1)} %fusion.116, bf16[2304,128]{1,0:T(8,128)(2,1)S(1)} %bitcast.301, bf16[512,128]{1,0:T(8,128)(2,1)S(1)} %copy-done.126), kind=kOutput, calls=%fused_computation.74 | convolution fusion | flops 325582848 | bytes 7798784 | tf_op jit(solution)/shard_map/dot_general | solution.py:147
  62.0 5.8 %multiply_reduce_fusion.1 = (bf16[128]{0:T(256)(128)(2,1)}, bf16[128]{0:T(256)(128)(2,1)}, bf16[128]{0:T(256)(128)(2,1)}, bf16[128]{0:T(256)(128)(2,1)}, bf16[12...) fusion(f32[15,262,128]{2,1,0:T(8,128)S(1)} %maximum_multiply_fu, ...), kind=kLoop, calls=%fused_computation.181 | loop fusion | flops 12678912 | bytes 24814592 | tf_op jit(solution)/shard_map/reduce_sum | solution.py:111
  67.8 1.9 %multiply_reduce_fusion.37 = (bf16[128]{0:T(256)(128)(2,1)S(1)}, bf16[128]{0:T(256)(128)(2,1)S(1)}, bf16[128]{0:T(256)(128)(2,1)S(1)}, bf16[128]{0:T(256)(128)(2...) fusion(f32[9,256,128]{2,1,0:T(8,128)S(1)} %get-tuple-element.17, ...), kind=kLoop, calls=%fused_computation.217 | loop fusion | flops 7666048 | bytes 16518400 | tf_op jit(solution)/shard_map/reduce_sum | solution.py:111
  69.7 2.7 %multiply_reduce_fusion.19 = (bf16[128]{0:T(256)(128)(2,1)S(1)}, bf16[128]{0:T(256)(128)(2,1)S(1)}, bf16[128]{0:T(256)(128)(2,1)S(1)}, bf16[128]{0:T(256)(128)(2...) fusion(f32[9,256,128]{2,1,0:T(8,128)S(1)} %get-tuple-element.17, ...), kind=kLoop, calls=%fused_computation.199 | loop fusion | flops 10909440 | bytes 23007744 | tf_op jit(solution)/shard_map/reduce_sum | solution.py:111
  73.8 2.5 %collective-permute-start.6 = (bf16[9,3,128]{2,1,0:T(4,128)(2,1)S(1)}, bf16[9,3,128]{2,1,0:T(4,128)(2,1)S(1)}, u32[]{:S(2)}, u32[]{:S(2)}) collective-permute-start(bf16[9,3,128]{2,1,0:T(4,128)(2,1)S(1)} %get-tuple-element.186), channel_id=1, source_target_pairs={{1,0},{2,1},{3,2},{0,3},{5,4},{6,5},{7,6},{4,7},{9,8},{10,9},{11,1... | collective-permute-start | bytes 20744 | tf_op jit(solution)/shard_map/ppermute | solution.py:71
  78.2 2.3 %collective-permute-start.7 = (bf16[3,262,128]{2,1,0:T(8,128)(2,1)S(1)}, bf16[3,262,128]{2,1,0:T(8,128)(2,1)S(1)}, u32[]{:S(2)}, u32[]{:S(2)}) collective-permute-start(bf16[3,262,128]{2,1,0:T(8,128)(2,1)S(1)} %get-tuple-element.180), channel_id=1, source_target_pairs={{0,4},{4,8},{8,12},{12,16},{16,20},{20,24},{24,28},{28,0},{1,5},{5... | collective-permute-start | bytes 603656 | tf_op jit(solution)/shard_map/ppermute | solution.py:70
  82.6 3.0 %collective-permute-done.7 = bf16[3,262,128]{2,1,0:T(8,128)(2,1)S(1)} collective-permute-done((bf16[3,262,128]{2,1,0:T(8,128)(2,1)S(1)}, bf16[3,262,128]{2,1,0:T(8,128)(2,1)S(1)}, u32[]{:S(2)}, u32[]{:S(2)}) %collective-permute-start.7) | collective-permute-done | bytes 201248 | tf_op jit(solution)/shard_map/ppermute | solution.py:70
  87.0 8.8 %convert_add_fusion = f32[9,256,128]{2,1,0:T(8,128)S(1)} fusion(bf16[9,256,128]{2,1,0:T(8,128)(2,1)S(1)} %copy-done.9, f32[15,262,128]{2,1,0:T(8,128)S(1)} %maximum_multiply_fusion.1, f32[128]{0:T(128)} %copy-done.103, f32[128]{0:T(128)} %copy-done.104, f32[128]{0:T(128)S(1)} %copy-done.21, f32[128]{0:T(128)S(1)} %copy-done.23, f32[128]{0:T(128)S(1)} %copy-done.25, ...), kind=kLoop, calls=%fused_computation.79 | loop fusion | flops 29196288 | bytes 59597312 | tf_op jit(solution)/shard_map/add | solution.py:236
  95.8 20.0 %while.22 = (s32[]{:T(128)}, f32[1024,128]{1,0:T(8,128)S(1)}, s32[3,4,768]{2,1,0:T(4,128)S(1)}, f32[3,4,768]{2,1,0:T(4,128)S(1)}, f32[3,768,128]{2,1,0:T(8,128)S...) while((s32[]{:T(128)}, f32[1024,128]{1,0:T(8,128)S(1)}, s32[3,4,768]{2,1,0:T(4,128)S(1)}, ...), condition=%wide.region_7.8_spmd.clone, body=%wide.region_6.7_spmd.clone.sunk | while | flops 1216872448 | bytes 1523895 | solution.py:250
  96.0 6.5 %fusion.145 = f32[1024,128]{1,0:T(8,128)S(1)} fusion(f32[768]{0:T(1024)S(1)} %get-tuple-element.330, s32[768]{0:T(1024)S(1)} %get-tuple-element.331, f32[768]{0:T(1024)S(1)} %get-tuple-element.332, s32[768]{0:T(1024)S(1)} %get-tuple-element.333, f32[768]{0:T(1024)S(1)} %get-tuple-element.334, s32[768]{0:T(1024)S(1)} %get-tuple-element.335, ...), kind=kOutput, calls=%fused_computation.53.clone.1 | convolution fusion | flops 1216872448 | bytes 1474565 | tf_op jit(solution)/shard_map/while/body/eval_jaxpr/dot_general | solution.py:241
  102.6 6.5 %fusion.145 = f32[1024,128]{1,0:T(8,128)S(1)} fusion(f32[768]{0:T(1024)S(1)} %get-tuple-element.330, s32[768]{0:T(1024)S(1)} %get-tuple-element.331, f32[768]{0:T(1024)S(1)} %get-tuple-element.332, s32[768]{0:T(1024)S(1)} %get-tuple-element.333, f32[768]{0:T(1024)S(1)} %get-tuple-element.334, s32[768]{0:T(1024)S(1)} %get-tuple-element.335, ...), kind=kOutput, calls=%fused_computation.53.clone.1 | convolution fusion | flops 1216872448 | bytes 1474565 | tf_op jit(solution)/shard_map/while/body/eval_jaxpr/dot_general | solution.py:241
  109.3 6.5 %fusion.145 = f32[1024,128]{1,0:T(8,128)S(1)} fusion(f32[768]{0:T(1024)S(1)} %get-tuple-element.330, s32[768]{0:T(1024)S(1)} %get-tuple-element.331, f32[768]{0:T(1024)S(1)} %get-tuple-element.332, s32[768]{0:T(1024)S(1)} %get-tuple-element.333, f32[768]{0:T(1024)S(1)} %get-tuple-element.334, s32[768]{0:T(1024)S(1)} %get-tuple-element.335, ...), kind=kOutput, calls=%fused_computation.53.clone.1 | convolution fusion | flops 1216872448 | bytes 1474565 | tf_op jit(solution)/shard_map/while/body/eval_jaxpr/dot_general | solution.py:241
  119.8 3.1 %collective-permute-start.16 = (bf16[128,512]{1,0:T(8,128)(2,1)S(1)}, bf16[128,512]{1,0:T(8,128)(2,1)S(1)}, u32[]{:S(2)}, u32[]{:S(2)}) collective-permute-start(bf16[128,512]{1,0:T(8,128)(2,1)S(1)} %add_convert_fusion.4), channel_id=1, source_target_pairs={{0,8},{4,12},{8,0},{12,4},{16,24},{20,28},{24,16},{28,20},{1,9},{5... | collective-permute-start | bytes 393224 | tf_op jit(solution)/shard_map/ppermute | solution.py:17
  123.7 1.9 %collective-permute-start.9 = (f32[512,256]{1,0:T(8,128)S(1)}, f32[512,256]{1,0:T(8,128)S(1)}, u32[]{:S(2)}, u32[]{:S(2)}) collective-permute-start(f32[512,256]{1,0:T(8,128)S(1)} %slice.921), channel_id=1, source_target_pairs={{0,4},{4,8},{8,12},{12,16},{16,20},{20,24},{24,28},{1,5},{5,9},{9,... | collective-permute-start | bytes 1572872 | tf_op jit(solution)/shard_map/ppermute | solution.py:12
  125.6 2.8 %collective-permute-done.11 = bf16[306,128]{1,0:T(8,128)(2,1)S(1)} collective-permute-done((bf16[306,128]{1,0:T(8,128)(2,1)S(1)}, bf16[306,128]{1,0:T(8,128)(2,1)S(1)}, u32[]{:S(2)}, u32[]{:S(2)}) %collective-permute-start.11) | collective-permute-done | bytes 78368 | tf_op jit(solution)/shard_map/ppermute | solution.py:17
  128.4 1.9 %collective-permute-start.12 = (bf16[306,128]{1,0:T(8,128)(2,1)S(1)}, bf16[306,128]{1,0:T(8,128)(2,1)S(1)}, u32[]{:S(2)}, u32[]{:S(2)}) collective-permute-start(bf16[306,128]{1,0:T(8,128)(2,1)S(1)} %add_convert_fusion.7), channel_id=1, source_target_pairs={{0,16},{4,20},{8,24},{12,28},{16,0},{20,4},{24,8},{28,12},{1,17},{... | collective-permute-start | bytes 235016 | tf_op jit(solution)/shard_map/ppermute | solution.py:17
  130.6 5.5 %collective-permute-done.12 = bf16[306,128]{1,0:T(8,128)(2,1)S(1)} collective-permute-done((bf16[306,128]{1,0:T(8,128)(2,1)S(1)}, bf16[306,128]{1,0:T(8,128)(2,1)S(1)}, u32[]{:S(2)}, u32[]{:S(2)}) %collective-permute-start.12) | collective-permute-done | bytes 78368 | tf_op jit(solution)/shard_map/ppermute | solution.py:17
  136.9 1.9 %collective-permute-done.17 = bf16[128,512]{1,0:T(8,128)(2,1)S(1)} collective-permute-done((bf16[128,512]{1,0:T(8,128)(2,1)S(1)}, bf16[128,512]{1,0:T(8,128)(2,1)S(1)}, u32[]{:S(2)}, u32[]{:S(2)}) %collective-permute-start.17) | collective-permute-done | bytes 131104 | tf_op jit(solution)/shard_map/ppermute | solution.py:17
  140.6 2.4 %collective-permute-start.14 = (bf16[306,128]{1,0:T(8,128)(2,1)S(1)}, bf16[306,128]{1,0:T(8,128)(2,1)S(1)}, u32[]{:S(2)}, u32[]{:S(2)}) collective-permute-start(bf16[306,128]{1,0:T(8,128)(2,1)S(1)} %add_convert_fusion.5), channel_id=1, source_target_pairs={{0,2},{1,3},{2,0},{3,1},{4,6},{5,7},{6,4},{7,5},{8,10},{9,11},{10,... | collective-permute-start | bytes 235016 | tf_op jit(solution)/shard_map/ppermute | solution.py:17
  143.1 2.1 %collective-permute-done.18 = bf16[128,512]{1,0:T(8,128)(2,1)S(1)} collective-permute-done((bf16[128,512]{1,0:T(8,128)(2,1)S(1)}, bf16[128,512]{1,0:T(8,128)(2,1)S(1)}, u32[]{:S(2)}, u32[]{:S(2)}) %collective-permute-start.18) | collective-permute-done | bytes 131104 | tf_op jit(solution)/shard_map/ppermute | solution.py:17
  145.2 2.4 %collective-permute-start.19 = (bf16[128,512]{1,0:T(8,128)(2,1)S(1)}, bf16[128,512]{1,0:T(8,128)(2,1)S(1)}, u32[]{:S(2)}, u32[]{:S(2)}) collective-permute-start(bf16[128,512]{1,0:T(8,128)(2,1)S(1)} %add_convert_fusion.1), channel_id=1, source_target_pairs={{0,2},{1,3},{2,0},{3,1},{4,6},{5,7},{6,4},{7,5},{8,10},{9,11},{10,... | collective-permute-start | bytes 393224 | tf_op jit(solution)/shard_map/ppermute | solution.py:17
  149.4 4.0 %collective-permute-done.19 = bf16[128,512]{1,0:T(8,128)(2,1)S(1)} collective-permute-done((bf16[128,512]{1,0:T(8,128)(2,1)S(1)}, bf16[128,512]{1,0:T(8,128)(2,1)S(1)}, u32[]{:S(2)}, u32[]{:S(2)}) %collective-permute-start.19) | collective-permute-done | bytes 131104 | tf_op jit(solution)/shard_map/ppermute | solution.py:17
  (355 shorter events, 37.1 us)
Async XLA Ops:
  0.6 53.4 %copy-start = (bf16[128,512]{1,0:T(8,128)(2,1)S(1)}, bf16[128,512]{1,0:T(8,128)(2,1)}, u32[]{:S(2)}) copy-start(bf16[128,512]{1,0:T(8,128)(2,1)} %param.21) | copy-start | bytes 393220
  0.7 8.2 %collective-permute-start = (bf16[512,256]{1,0:T(8,128)(2,1)}, bf16[512,256]{1,0:T(8,128)(2,1)S(1)}, u32[]{:S(2)}, u32[]{:S(2)}) collective-permute-start(bf16[512,256]{1,0:T(8,128)(2,1)} %param.17), channel_id=1, source_target_pairs={{4,0},{8,4},{12,8},{16,12},{20,16},{24,20},{28,24},{5,1},{9,5},{13... | collective-permute-start | bytes 786440 | tf_op jit(solution)/shard_map/ppermute | solution.py:12
  3.1 40.5 %copy-start.18 = (f32[128]{0:T(128)}, f32[128]{0:T(128)S(1)}, u32[]{:S(2)}) copy-start(f32[128]{0:T(128)S(1)} %get-tuple-element.191) | copy-start | bytes 1540
  3.1 40.5 %copy-start.20 = (f32[128]{0:T(128)}, f32[128]{0:T(128)S(1)}, u32[]{:S(2)}) copy-start(f32[128]{0:T(128)S(1)} %get-tuple-element.192) | copy-start | bytes 1540
  3.1 40.5 %copy-start.22 = (f32[128]{0:T(128)}, f32[128]{0:T(128)S(1)}, u32[]{:S(2)}) copy-start(f32[128]{0:T(128)S(1)} %get-tuple-element.193) | copy-start | bytes 1540
  3.1 40.5 %copy-start.24 = (f32[128]{0:T(128)}, f32[128]{0:T(128)S(1)}, u32[]{:S(2)}) copy-start(f32[128]{0:T(128)S(1)} %get-tuple-element.194) | copy-start | bytes 1540
  3.1 40.5 %copy-start.26 = (f32[128]{0:T(128)}, f32[128]{0:T(128)S(1)}, u32[]{:S(2)}) copy-start(f32[128]{0:T(128)S(1)} %get-tuple-element.195) | copy-start | bytes 1540
  3.1 40.5 %copy-start.28 = (f32[128]{0:T(128)}, f32[128]{0:T(128)S(1)}, u32[]{:S(2)}) copy-start(f32[128]{0:T(128)S(1)} %get-tuple-element.196) | copy-start | bytes 1540
  3.1 40.5 %copy-start.30 = (f32[128]{0:T(128)}, f32[128]{0:T(128)S(1)}, u32[]{:S(2)}) copy-start(f32[128]{0:T(128)S(1)} %get-tuple-element.197) | copy-start | bytes 1540
  3.1 40.5 %copy-start.32 = (f32[128]{0:T(128)}, f32[128]{0:T(128)S(1)}, u32[]{:S(2)}) copy-start(f32[128]{0:T(128)S(1)} %get-tuple-element.198) | copy-start | bytes 1540
  3.1 40.5 %copy-start.34 = (f32[128]{0:T(128)}, f32[128]{0:T(128)S(1)}, u32[]{:S(2)}) copy-start(f32[128]{0:T(128)S(1)} %get-tuple-element.199) | copy-start | bytes 1540
  3.2 40.5 %copy-start.36 = (f32[128]{0:T(128)}, f32[128]{0:T(128)S(1)}, u32[]{:S(2)}) copy-start(f32[128]{0:T(128)S(1)} %get-tuple-element.200) | copy-start | bytes 1540
  29.0 6.9 %collective-permute-start.1 = (bf16[9,3,128]{2,1,0:T(4,128)(2,1)S(1)}, bf16[9,3,128]{2,1,0:T(4,128)(2,1)S(1)}, u32[]{:S(2)}, u32[]{:S(2)}) collective-permute-start(bf16[9,3,128]{2,1,0:T(4,128)(2,1)S(1)} %get-tuple-element.187), channel_id=1, source_target_pairs={{0,1},{1,2},{2,3},{3,0},{4,5},{5,6},{6,7},{7,4},{8,9},{9,10},{10,1... | collective-permute-start | bytes 20744 | tf_op jit(solution)/shard_map/ppermute | solution.py:70
  32.1 3.8 %collective-permute-start.2 = (bf16[9,3,128]{2,1,0:T(4,128)(2,1)S(1)}, bf16[9,3,128]{2,1,0:T(4,128)(2,1)S(1)}, u32[]{:S(2)}, u32[]{:S(2)}) collective-permute-start(bf16[9,3,128]{2,1,0:T(4,128)(2,1)S(1)} %get-tuple-element.188), channel_id=1, source_target_pairs={{1,0},{2,1},{3,2},{0,3},{5,4},{6,5},{7,6},{4,7},{9,8},{10,9},{11,1... | collective-permute-start | bytes 20744 | tf_op jit(solution)/shard_map/ppermute | solution.py:71
  36.0 6.1 %collective-permute-start.3 = (bf16[3,262,128]{2,1,0:T(8,128)(2,1)S(1)}, bf16[3,262,128]{2,1,0:T(8,128)(2,1)S(1)}, u32[]{:S(2)}, u32[]{:S(2)}) collective-permute-start(bf16[3,262,128]{2,1,0:T(8,128)(2,1)S(1)} %get-tuple-element.182), channel_id=1, source_target_pairs={{0,4},{4,8},{8,12},{12,16},{16,20},{20,24},{24,28},{28,0},{1,5},{5... | collective-permute-start | bytes 603656 | tf_op jit(solution)/shard_map/ppermute | solution.py:70
  36.2 6.9 %collective-permute-start.4 = (bf16[3,262,128]{2,1,0:T(8,128)(2,1)S(1)}, bf16[3,262,128]{2,1,0:T(8,128)(2,1)S(1)}, u32[]{:S(2)}, u32[]{:S(2)}) collective-permute-start(bf16[3,262,128]{2,1,0:T(8,128)(2,1)S(1)} %get-tuple-element.183), channel_id=1, source_target_pairs={{4,0},{8,4},{12,8},{16,12},{20,16},{24,20},{28,24},{0,28},{5,1},{9... | collective-permute-start | bytes 603656 | tf_op jit(solution)/shard_map/ppermute | solution.py:71
  72.4 5.7 %collective-permute-start.5 = (bf16[9,3,128]{2,1,0:T(4,128)(2,1)S(1)}, bf16[9,3,128]{2,1,0:T(4,128)(2,1)S(1)}, u32[]{:S(2)}, u32[]{:S(2)}) collective-permute-start(bf16[9,3,128]{2,1,0:T(4,128)(2,1)S(1)} %get-tuple-element.185), channel_id=1, source_target_pairs={{0,1},{1,2},{2,3},{3,0},{4,5},{5,6},{6,7},{7,4},{8,9},{9,10},{10,1... | collective-permute-start | bytes 20744 | tf_op jit(solution)/shard_map/ppermute | solution.py:70
  73.8 4.3 %collective-permute-start.6 = (bf16[9,3,128]{2,1,0:T(4,128)(2,1)S(1)}, bf16[9,3,128]{2,1,0:T(4,128)(2,1)S(1)}, u32[]{:S(2)}, u32[]{:S(2)}) collective-permute-start(bf16[9,3,128]{2,1,0:T(4,128)(2,1)S(1)} %get-tuple-element.186), channel_id=1, source_target_pairs={{1,0},{2,1},{3,2},{0,3},{5,4},{6,5},{7,6},{4,7},{9,8},{10,9},{11,1... | collective-permute-start | bytes 20744 | tf_op jit(solution)/shard_map/ppermute | solution.py:71
  78.2 7.3 %collective-permute-start.7 = (bf16[3,262,128]{2,1,0:T(8,128)(2,1)S(1)}, bf16[3,262,128]{2,1,0:T(8,128)(2,1)S(1)}, u32[]{:S(2)}, u32[]{:S(2)}) collective-permute-start(bf16[3,262,128]{2,1,0:T(8,128)(2,1)S(1)} %get-tuple-element.180), channel_id=1, source_target_pairs={{0,4},{4,8},{8,12},{12,16},{16,20},{20,24},{24,28},{28,0},{1,5},{5... | collective-permute-start | bytes 603656 | tf_op jit(solution)/shard_map/ppermute | solution.py:70
  80.5 5.0 %collective-permute-start.8 = (bf16[3,262,128]{2,1,0:T(8,128)(2,1)S(1)}, bf16[3,262,128]{2,1,0:T(8,128)(2,1)S(1)}, u32[]{:S(2)}, u32[]{:S(2)}) collective-permute-start(bf16[3,262,128]{2,1,0:T(8,128)(2,1)S(1)} %get-tuple-element.181), channel_id=1, source_target_pairs={{4,0},{8,4},{12,8},{16,12},{20,16},{24,20},{28,24},{0,28},{5,1},{9... | collective-permute-start | bytes 603656 | tf_op jit(solution)/shard_map/ppermute | solution.py:71
  82.3 36.6 %collective-permute-start.15 = (bf16[128,512]{1,0:T(8,128)(2,1)}, bf16[128,512]{1,0:T(8,128)(2,1)}, u32[]{:S(2)}, u32[]{:S(2)}) collective-permute-start(bf16[128,512]{1,0:T(8,128)(2,1)} %get-tuple-element.242), channel_id=1, source_target_pairs={{0,4},{4,0},{8,12},{12,8},{16,20},{20,16},{24,28},{28,24},{1,5},{5... | collective-permute-start | bytes 393224 | tf_op jit(solution)/shard_map/ppermute | solution.py:17
  117.2 5.7 %collective-permute-start.10 = (bf16[306,128]{1,0:T(8,128)(2,1)S(1)}, bf16[306,128]{1,0:T(8,128)(2,1)S(1)}, u32[]{:S(2)}, u32[]{:S(2)}) collective-permute-start(bf16[306,128]{1,0:T(8,128)(2,1)S(1)} %concatenate.24), channel_id=1, source_target_pairs={{0,4},{4,0},{8,12},{12,8},{16,20},{20,16},{24,28},{28,24},{1,5},{5... | collective-permute-start | bytes 235016 | tf_op jit(solution)/shard_map/ppermute | solution.py:17
  119.8 10.5 %collective-permute-start.16 = (bf16[128,512]{1,0:T(8,128)(2,1)S(1)}, bf16[128,512]{1,0:T(8,128)(2,1)S(1)}, u32[]{:S(2)}, u32[]{:S(2)}) collective-permute-start(bf16[128,512]{1,0:T(8,128)(2,1)S(1)} %add_convert_fusion.4), channel_id=1, source_target_pairs={{0,8},{4,12},{8,0},{12,4},{16,24},{20,28},{24,16},{28,20},{1,9},{5... | collective-permute-start | bytes 393224 | tf_op jit(solution)/shard_map/ppermute | solution.py:17
  123.0 5.4 %collective-permute-start.11 = (bf16[306,128]{1,0:T(8,128)(2,1)S(1)}, bf16[306,128]{1,0:T(8,128)(2,1)S(1)}, u32[]{:S(2)}, u32[]{:S(2)}) collective-permute-start(bf16[306,128]{1,0:T(8,128)(2,1)S(1)} %add_convert_fusion.8), channel_id=1, source_target_pairs={{0,8},{4,12},{8,0},{12,4},{16,24},{20,28},{24,16},{28,20},{1,9},{5... | collective-permute-start | bytes 235016 | tf_op jit(solution)/shard_map/ppermute | solution.py:17
  123.7 29.8 %collective-permute-start.9 = (f32[512,256]{1,0:T(8,128)S(1)}, f32[512,256]{1,0:T(8,128)S(1)}, u32[]{:S(2)}, u32[]{:S(2)}) collective-permute-start(f32[512,256]{1,0:T(8,128)S(1)} %slice.921), channel_id=1, source_target_pairs={{0,4},{4,8},{8,12},{12,16},{16,20},{20,24},{24,28},{1,5},{5,9},{9,... | collective-permute-start | bytes 1572872 | tf_op jit(solution)/shard_map/ppermute | solution.py:12
  128.4 7.7 %collective-permute-start.12 = (bf16[306,128]{1,0:T(8,128)(2,1)S(1)}, bf16[306,128]{1,0:T(8,128)(2,1)S(1)}, u32[]{:S(2)}, u32[]{:S(2)}) collective-permute-start(bf16[306,128]{1,0:T(8,128)(2,1)S(1)} %add_convert_fusion.7), channel_id=1, source_target_pairs={{0,16},{4,20},{8,24},{12,28},{16,0},{20,4},{24,8},{28,12},{1,17},{... | collective-permute-start | bytes 235016 | tf_op jit(solution)/shard_map/ppermute | solution.py:17
  130.3 8.5 %collective-permute-start.17 = (bf16[128,512]{1,0:T(8,128)(2,1)S(1)}, bf16[128,512]{1,0:T(8,128)(2,1)S(1)}, u32[]{:S(2)}, u32[]{:S(2)}) collective-permute-start(bf16[128,512]{1,0:T(8,128)(2,1)S(1)} %add_convert_fusion.3), channel_id=1, source_target_pairs={{0,16},{4,20},{8,24},{12,28},{16,0},{20,4},{24,8},{28,12},{1,17},{... | collective-permute-start | bytes 393224 | tf_op jit(solution)/shard_map/ppermute | solution.py:17
  136.1 4.5 %collective-permute-start.13 = (bf16[306,128]{1,0:T(8,128)(2,1)S(1)}, bf16[306,128]{1,0:T(8,128)(2,1)S(1)}, u32[]{:S(2)}, u32[]{:S(2)}) collective-permute-start(bf16[306,128]{1,0:T(8,128)(2,1)S(1)} %add_convert_fusion.6), channel_id=1, source_target_pairs={{0,1},{1,0},{2,3},{3,2},{4,5},{5,4},{6,7},{7,6},{8,9},{9,8},{10,11... | collective-permute-start | bytes 235016 | tf_op jit(solution)/shard_map/ppermute | solution.py:17
  138.9 6.4 %collective-permute-start.18 = (bf16[128,512]{1,0:T(8,128)(2,1)S(1)}, bf16[128,512]{1,0:T(8,128)(2,1)S(1)}, u32[]{:S(2)}, u32[]{:S(2)}) collective-permute-start(bf16[128,512]{1,0:T(8,128)(2,1)S(1)} %add_convert_fusion.2), channel_id=1, source_target_pairs={{0,1},{1,0},{2,3},{3,2},{4,5},{5,4},{6,7},{7,6},{8,9},{9,8},{10,11... | collective-permute-start | bytes 393224 | tf_op jit(solution)/shard_map/ppermute | solution.py:17
  140.6 7.0 %collective-permute-start.14 = (bf16[306,128]{1,0:T(8,128)(2,1)S(1)}, bf16[306,128]{1,0:T(8,128)(2,1)S(1)}, u32[]{:S(2)}, u32[]{:S(2)}) collective-permute-start(bf16[306,128]{1,0:T(8,128)(2,1)S(1)} %add_convert_fusion.5), channel_id=1, source_target_pairs={{0,2},{1,3},{2,0},{3,1},{4,6},{5,7},{6,4},{7,5},{8,10},{9,11},{10,... | collective-permute-start | bytes 235016 | tf_op jit(solution)/shard_map/ppermute | solution.py:17
  145.2 8.2 %collective-permute-start.19 = (bf16[128,512]{1,0:T(8,128)(2,1)S(1)}, bf16[128,512]{1,0:T(8,128)(2,1)S(1)}, u32[]{:S(2)}, u32[]{:S(2)}) collective-permute-start(bf16[128,512]{1,0:T(8,128)(2,1)S(1)} %add_convert_fusion.1), channel_id=1, source_target_pairs={{0,2},{1,3},{2,0},{3,1},{4,6},{5,7},{6,4},{7,5},{8,10},{9,11},{10,... | collective-permute-start | bytes 393224 | tf_op jit(solution)/shard_map/ppermute | solution.py:17
  153.5 1.4 collective-permute-start.20
  (118 other events, 581.1 us)

commit v2 on v1

v2 whole, which is shorter than its diff:
```python
import functools
import jax
import jax.numpy as jnp
from jax import lax
from jax.experimental import pallas as pl
from jax.experimental.pallas import tpu as pltpu
from jax.sharding import PartitionSpec as P

EPSILON = 1e-05
ROOT = 0.7978845608028654
CUBIC = 0.044715
ROWS = 128
EDGE = 8
LIMIT = 20 << 20
bf16 = jnp.bfloat16
f32 = jnp.float32


def kernel_call(body, outs, scratch, args, name, flops, nbytes):
    vmem = pl.BlockSpec(memory_space=pltpu.VMEM)
    return pl.pallas_call(
        body,
        in_specs=[vmem] * len(args),
        out_specs=[vmem] * len(outs),
        out_shape=[jax.ShapeDtypeStruct(shape, dtype) for shape, dtype in outs],
        scratch_shapes=[pltpu.VMEM(shape, dtype) for shape, dtype in scratch],
        compiler_params=pltpu.CompilerParams(vmem_limit_bytes=LIMIT),
        cost_estimate=pl.CostEstimate(flops=flops, bytes_accessed=nbytes, transcendentals=0),
        name=name,
    )(*args)


def merged_margins(index, weight):
    merged = []
    for slot in range(len(index)):
        total = weight[slot]
        for before in range(slot):
            total = total + jnp.where(index[before] == index[slot], weight[before], 0.0)
        merged.append(total.astype(bf16))
    return merged


def dense_block(index, weight, block, places):
    dense = jnp.zeros(places.shape, bf16)
    for slot in range(len(index)):
        place = jnp.where(index[slot] // ROWS == block, index[slot] % ROWS, -1)
        place = jnp.broadcast_to(place.astype(f32).astype(bf16), places.shape)
        dense = jnp.where(places == place, jnp.broadcast_to(weight[slot], places.shape), dense)
    return dense


def margins_kernel(index_ref, weight_ref, window_ref, dense_ref, part_ref):
    margins, height, width = index_ref.shape
    own = window_ref.shape[1]
    places = lax.broadcasted_iota(jnp.int32, (ROWS, width), 0).astype(f32).astype(bf16)

    @pl.loop(0, height)
    def _(row):
        index = [index_ref[slot, pl.ds(row, 1), :] for slot in range(margins)]
        weight = [weight_ref[slot, pl.ds(row, 1), :] for slot in range(margins)]
        weight = merged_margins(index, weight)
        cells = pl.ds(pl.multiple_of(row * width, width), width)
        for block in range(dense_ref.shape[0] // ROWS):
            dense_ref[block * ROWS : (block + 1) * ROWS, cells] = dense_block(
                index, weight, block, places
            )
        part = jnp.dot(window_ref[...], dense_ref[:own, cells], preferred_element_type=f32)
        part_ref[row] = part.T


def field_kernel(dense_ref, window_ref, part_ref, state_ref, field_ref, side_ref, end_ref):
    height, width, channels = field_ref.shape
    own = window_ref.shape[1]

    @pl.loop(0, height)
    def _(row):
        cells = pl.ds(pl.multiple_of(row * width, width), width)
        part = jnp.dot(window_ref[...], dense_ref[own:, cells], preferred_element_type=f32)
        field = state_ref[row].astype(f32) + (part_ref[row] + part.T)
        field_ref[row] = field
        side_ref[0, row] = field[width - EDGE :].astype(bf16)
        side_ref[1, row] = field[:EDGE].astype(bf16)

    end_ref[0] = field_ref[height - 3 :].astype(bf16)
    end_ref[1] = field_ref[:3].astype(bf16)


def spread(kernel_ref, spread_ref, flip):
    taps = kernel_ref.shape[0]
    for row in range(taps):
        for col in range(taps):
            source = kernel_ref[row, col : col + 1, :]
            place = (taps - 1 - row) * taps + taps - 1 - col if flip else row * taps + col
            spread_ref[place] = jnp.broadcast_to(source, (8, source.shape[1]))


def tap_sums(sums, rows, load, spread_ref):
    taps = 7
    for col_tap in range(taps):
        for row in rows:
            value = None
            for row_tap in range(taps):
                out = row - row_tap
                if 0 <= out < len(sums):
                    value = load(row, col_tap) if value is None else value
                    term = value * spread_ref[row_tap * taps + col_tap]
                    sums[out] = term if sums[out] is None else sums[out] + term


def local_taps(padded_ref, spread_ref, out_ref):
    height, width, channels = out_ref.shape

    @pl.loop(0, width // 8)
    def _(block):
        col = pl.multiple_of(block * 8, 8)
        sums = [None] * height

        def load(row, tap):
            return padded_ref[row - 3, pl.ds(col + (tap + EDGE - 3), 8), :]

        tap_sums(sums, range(3, height + 3), load, spread_ref)
        for row in range(height):
            out_ref[row, pl.ds(col, 8), :] = sums[row]


def pad_cols(source_ref, padded_ref):
    height, width, channels = source_ref.shape
    padded_ref[:, :EDGE, :] = jnp.zeros((height, EDGE, channels), f32)
    padded_ref[:, EDGE + width :, :] = jnp.zeros((height, EDGE, channels), f32)
    padded_ref[:, EDGE : EDGE + width, :] = source_ref[...]


def rest_taps(base_ref, left_ref, right_ref, low_ref, high_ref, spread_ref, out_ref, strip, ends):
    height, width, channels = base_ref.shape
    strip[...] = jnp.zeros(strip.shape, f32)
    strip[0, :, :EDGE, :] = left_ref[...].astype(f32)
    strip[1, :, 2 * EDGE :, :] = right_ref[...].astype(f32)
    ends[0:3] = low_ref[...].astype(f32)
    ends[3:6] = high_ref[...].astype(f32)

    @pl.loop(0, width // 8)
    def _(block):
        col = pl.multiple_of(block * 8, 8)
        sums = [base_ref[row, pl.ds(col, 8), :] for row in range(height)]

        def load(row, tap):
            place = row if row < 3 else row - height
            return ends[place, pl.ds(col + (tap + EDGE - 3), 8), :]

        tap_sums(sums, (0, 1, 2, height + 3, height + 4, height + 5), load, spread_ref)
        for row in range(height):
            out_ref[row, pl.ds(col, 8), :] = sums[row]

    @pl.loop(0, 2)
    def _(side):
        col = pl.multiple_of(side * (width - 8), 8)
        sums = [out_ref[row, pl.ds(col, 8), :] for row in range(height)]

        def load(row, tap):
            return strip[side, row - 3, pl.ds(tap + EDGE - 3, 8), :]

        tap_sums(sums, range(3, height + 3), load, spread_ref)
        for row in range(height):
            out_ref[row, pl.ds(col, 8), :] = sums[row]


def conv_kernel(field_ref, kernel_ref, out_ref, padded, weights):
    spread(kernel_ref, weights, False)
    pad_cols(field_ref, padded)
    local_taps(padded, weights, out_ref)


def mlp_kernel(
    base_ref,
    field_ref,
    left_ref,
    right_ref,
    low_ref,
    high_ref,
    kernel_ref,
    cotangent_ref,
    mask_ref,
    gain_ref,
    w_in_ref,
    w_out_ref,
    w_in_t_ref,
    w_out_t_ref,
    g_ref,
    padded_ref,
    pair_ref,
    gain_out_ref,
    side_ref,
    end_ref,
    conv,
    weights,
    strip,
    ends,
):
    height, width, channels = base_ref.shape
    spread(kernel_ref, weights, False)
    rest_taps(base_ref, left_ref, right_ref, low_ref, high_ref, weights, conv, strip, ends)
    padded_ref[3 : 3 + height, EDGE : EDGE + width, :] = field_ref[...]
    padded_ref[3 : 3 + height, :EDGE, :] = strip[0, :, :EDGE, :]
    padded_ref[3 : 3 + height, EDGE + width :, :] = strip[1, :, 2 * EDGE :, :]
    padded_ref[:3] = ends[0:3]
    padded_ref[3 + height :] = ends[3:6]
    pair_ref[...] = jnp.zeros(pair_ref.shape, f32)
    gain_out_ref[...] = jnp.zeros(gain_out_ref.shape, f32)
    gain = gain_ref[...]

    @pl.loop(0, height)
    def _(row):
        value = conv[row]
        center = value - jnp.mean(value, axis=-1, keepdims=True)
        scale = lax.rsqrt(jnp.mean(center * center, axis=-1, keepdims=True) + EPSILON)
        normed = center * scale
        ln_rows = (normed * gain).astype(bf16)
        mask = jnp.broadcast_to(mask_ref[pl.ds(row, 1), :].astype(f32), (channels, width)).T
        gy_rows = (mask * cotangent_ref[row].astype(f32)).astype(bf16)
        pre = jnp.dot(ln_rows, w_in_ref[...], preferred_element_type=f32)
        g_hidden = jnp.dot(gy_rows, w_out_t_ref[...], preferred_element_type=f32)
        square = pre * pre
        half = 0.5 + 0.5 * jnp.tanh(pre * (ROOT + (ROOT * CUBIC) * square))
        hidden = pre * half
        slope = half + hidden * (1.0 - half) * (2 * ROOT + (6 * ROOT * CUBIC) * square)
        g_pre = (g_hidden * slope).astype(bf16)
        hidden = hidden.astype(bf16)
        pair_ref[0] += lax.dot_general(
            ln_rows, g_pre, (((0,), (0,)), ((), ())), preferred_element_type=f32
        )
        pair_ref[1] += lax.dot_general(
            gy_rows, hidden, (((0,), (0,)), ((), ())), preferred_element_type=f32
        )
        g_ln = jnp.dot(g_pre, w_in_t_ref[...], preferred_element_type=f32)
        gain_out_ref[...] += jnp.sum((g_ln * normed).reshape(width // 8, 8, channels), axis=0)
        g_norm = g_ln * gain
        g_conv = (
            g_norm
            - jnp.mean(g_norm, axis=-1, keepdims=True)
            - normed * jnp.mean(g_norm * normed, axis=-1, keepdims=True)
        ) * scale
        g_ref[row] = g_conv
        side_ref[0, row] = g_conv[width - EDGE :].astype(bf16)
        side_ref[1, row] = g_conv[:EDGE].astype(bf16)

    end_ref[0] = g_ref[height - 3 :].astype(bf16)
    end_ref[1] = g_ref[:3].astype(bf16)


def grads_kernel(g_ref, field_ref, kernel_ref, grad_ref, out_ref, padded, weights):
    height, width, channels = g_ref.shape
    taps = kernel_ref.shape[0]
    for col_tap in range(taps):

        def body(block, sums):
            sums = list(sums)
            col = pl.multiple_of(block * 8, 8)
            g_rows = [g_ref[row, pl.ds(col, 8), :] for row in range(height)]
            for row in range(height + taps - 1):
                value = field_ref[row, pl.ds(col + (col_tap + EDGE - 3), 8), :]
                for row_tap in range(taps):
                    if 0 <= row - row_tap < height:
                        sums[row_tap] = sums[row_tap] + g_rows[row - row_tap] * value
            return tuple(sums)

        start = tuple(jnp.zeros((8, channels), f32) for _ in range(taps))
        sums = lax.fori_loop(0, width // 8, body, start)
        for row_tap in range(taps):
            place = row_tap * taps + col_tap
            grad_ref[place : place + 1, :] = jnp.sum(sums[row_tap], axis=0, keepdims=True)
    spread(kernel_ref, weights, True)
    pad_cols(g_ref, padded)
    local_taps(padded, weights, out_ref)


def state_kernel(
    base_ref,
    left_ref,
    right_ref,
    low_ref,
    high_ref,
    kernel_ref,
    cotangent_ref,
    dense_ref,
    state_ref,
    window_ref,
    weights,
    strip,
    ends,
    sums,
    halves,
):
    height, width, channels = base_ref.shape
    spread(kernel_ref, weights, True)
    rest_taps(base_ref, left_ref, right_ref, low_ref, high_ref, weights, sums, strip, ends)

    @pl.loop(0, height)
    def _(row):
        state = cotangent_ref[row].astype(f32) + sums[row]
        state_ref[row] = state
        high = state.astype(bf16)
        cells = pl.ds(pl.multiple_of(row * width, width), width)
        halves[cells, :channels] = high
        halves[cells, channels:] = (state - high.astype(f32)).astype(bf16)

    @pl.loop(0, window_ref.shape[0] // 256)
    def _(block):
        slots = pl.ds(pl.multiple_of(block * 256, 256), 256)
        both = jnp.dot(dense_ref[slots, :], halves[...], preferred_element_type=f32)
        window_ref[slots, :] = both[:, :channels] + both[:, channels:]


def shifted(x, axis, by, wrap=False):
    size = lax.axis_size(axis)
    pairs = [(i, (i + by) % size) for i in range(size) if wrap or 0 <= i + by < size]
    return lax.ppermute(x, axis, pairs)


def exchange(side, end):
    left = shifted(side[0], "lon", 1, True)
    right = shifted(side[1], "lon", -1, True)
    height = left.shape[0]
    to_high = jnp.concatenate([left[height - 3 :], end[0], right[height - 3 :]], axis=1)
    to_low = jnp.concatenate([left[:3], end[1], right[:3]], axis=1)
    low = shifted(to_high, "lat", 1)
    high = shifted(to_low, "lat", -1)
    return left, right, low, high


def xor_swap(x, axis, mask):
    size = lax.axis_size(axis)
    return lax.ppermute(x, axis, [(i, i ^ mask) for i in range(size)])


def masks(axis):
    size = lax.axis_size(axis)
    if size & (size - 1):
        return None
    return [1 << k for k in range(size.bit_length() - 1)]


def fold(value, axis, chosen, dtype=bf16):
    for mask in chosen:
        mine = value.astype(dtype)
        other = xor_swap(mine, axis, mask)
        value = mine.astype(f32) + other.astype(f32)
    return value


def sum_over_mesh(value):
    for axis in ("lat", "lon"):
        steps = masks(axis)
        value = lax.psum(value, axis) if steps is None else fold(value, axis, steps, f32)
    return value


def sum_pair_over_mesh(pair):
    steps = masks("lat")
    if not steps or masks("lon") is None:
        return lax.psum(pair, ("lat", "lon"))
    odd = lax.rem(lax.axis_index("lat"), 2) == 1
    kept = jnp.where(odd, pair[1], pair[0])
    given = xor_swap(jnp.where(odd, pair[0], pair[1]), "lat", 1)
    value = kept + given
    value = fold(value, "lat", steps[1:])
    value = fold(value, "lon", masks("lon"))
    other = xor_swap(value, "lat", 1)
    return jnp.where(odd, other, value), jnp.where(odd, value, other)


def shards(
    ocean_state,
    cotangent,
    atm_embed,
    projection,
    dw_kernel,
    norm_gain,
    w_in,
    w_out,
    margin_index,
    margin_weight,
    sea_mask,
):
    cells_atm = atm_embed.shape[0]
    channels = projection.shape[1]
    height, width = ocean_state.shape[:2]
    taps = dw_kernel.shape[0]
    hidden = w_in.shape[1]
    slots = 2 * cells_atm
    cells = height * width
    grid = (height, width, channels)
    wide = width + 2 * EDGE
    tap_scratch = ((taps * taps, 8, channels), f32)
    strip = ((2, height, 3 * EDGE, channels), f32)
    ends = ((6, wide, channels), f32)
    own = lax.dot_general(
        projection, atm_embed, (((0,), (1,)), ((), ())), preferred_element_type=f32
    ).astype(bf16)
    following = shifted(own, "lat", -1)
    next_embed = shifted(atm_embed, "lat", -1)
    dense, part = kernel_call(
        margins_kernel,
        [((slots, cells), bf16), (grid, f32)],
        [],
        (margin_index, margin_weight, own),
        "margins",
        2 * cells * cells_atm * channels,
        8 << 20,
    )
    field, side, end = kernel_call(
        field_kernel,
        [(grid, f32), ((2, height, EDGE, channels), bf16), ((2, 3, width, channels), bf16)],
        [],
        (dense, following, part, ocean_state),
        "field",
        2 * cells * cells_atm * channels,
        8 << 20,
    )
    left, right, low, high = exchange(side, end)
    (conv,) = kernel_call(
        conv_kernel,
        [(grid, f32)],
        [((height, wide, channels), f32), tap_scratch],
        (field, dw_kernel),
        "conv",
        cells * channels * 98,
        16 << 20,
    )
    g_conv, padded, pair, gain_rows, side, end = kernel_call(
        mlp_kernel,
        [
            (grid, f32),
            ((height + 6, wide, channels), f32),
            ((2, channels, hidden), f32),
            ((8, channels), f32),
            ((2, height, EDGE, channels), bf16),
            ((2, 3, width, channels), bf16),
        ],
        [(grid, f32), tap_scratch, strip, ends],
        (
            conv,
            field,
            left,
            right,
            low,
            high,
            dw_kernel,
            cotangent,
            sea_mask,
            norm_gain[None],
            w_in,
            w_out,
            w_in.T,
            w_out.T,
        ),
        "mlp",
        cells * channels * hidden * 10,
        32 << 20,
    )
    left, right, low, high = exchange(side, end)
    grad_in, grad_out = sum_pair_over_mesh(pair)
    grad_kernel, back = kernel_call(
        grads_kernel,
        [((taps * taps, channels), f32), (grid, f32)],
        [((height, wide, channels), f32), tap_scratch],
        (g_conv, padded, dw_kernel),
        "grads",
        cells * channels * 196,
        32 << 20,
    )
    grad_state, g_window = kernel_call(
        state_kernel,
        [(grid, f32), ((slots, channels), f32)],
        [tap_scratch, strip, ends, (grid, f32), ((cells, 2 * channels), bf16)],
        (back, left, right, low, high, dw_kernel, cotangent, dense),
        "state",
        cells * slots * channels * 4,
        16 << 20,
    )
    returned = shifted(g_window[cells_atm:].astype(bf16), "lat", 1)
    grad_projection = lax.dot_general(
        jnp.concatenate([atm_embed, next_embed], axis=0),
        g_window.astype(bf16),
        (((0,), (0,)), ((), ())),
        preferred_element_type=f32,
    )
    late = jnp.concatenate(
        [grad_projection, grad_kernel, jnp.sum(gain_rows, axis=0)[None]], axis=0
    )
    late = sum_over_mesh(late)
    g_projected = (g_window[:cells_atm] + returned.astype(f32)).astype(bf16)
    grad_embed = lax.dot_general(
        g_projected, projection, (((1,), (1,)), ((), ())), preferred_element_type=f32
    )
    rows = projection.shape[0]
    return (
        grad_state,
        grad_embed,
        late[:rows],
        late[rows : rows + taps * taps].reshape(dw_kernel.shape),
        late[rows + taps * taps],
        grad_in,
        grad_out.T,
    )


def solution(mesh):
    return jax.shard_map(
        shards,
        mesh=mesh,
        in_specs=(
            P("lat", "lon", None),
            P("lat", "lon", None),
            P(("lat", "lon"), None),
            P(),
            P(),
            P(),
            P(),
            P(),
            P(None, "lat", "lon"),
            P(None, "lat", "lon"),
            P("lat", "lon"),
        ),
        out_specs=(P("lat", "lon", None), P(("lat", "lon"), None), P(), P(), P(), P(), P()),
        check_vma=False,
    )
```

time: 157 us -> 122 us (0.78)
  matrix products: 46.7 us -> 3.56 us
  Pallas kernels: 0 us -> 35.4 us
  other arithmetic: 39.1 us -> 4.25 us
  starting transfers between devices: 31.7 us -> 38.3 us
  local copies, waits for them, and re-layouts: 10.6 us -> 14.8 us
  between operations: 2.89 us -> 1.09 us
    dot_general x14 -> x3, matrix products: 46.7 us -> 3.56 us  [the longest x1 1.37 us: shards(): lax.dot_general(jnp.concatenate([atm_embed, next_embed], axis=0), g_windo...]
    pallas_call x0 -> x6, Pallas kernels: none -> 35.4 us  [kernel_call(): pl.pallas_call(body, in_specs=[vmem] * len(args), out_specs=[vmem] * len(...]
    reduce_sum x6 -> x1, other arithmetic: 21.2 us -> 0.02 us  [shards(): jnp.sum(gain_rows, axis=0)[None]]
    ppermute x2 -> x11, starting transfers between devices: 3.29 us -> 22.4 us  [shifted(): return lax.ppermute(x, axis, pairs)]
    ppermute x8 -> x0, starting transfers between devices: 14.7 us -> none  [the longest x4 7.65 us: with_halo(): high = lax.ppermute(rims[1], axis, backward).astype(jnp.float32)]
    add x3 -> x6, other arithmetic: 9.63 us -> 0.13 us  [fold(): value = mine.astype(f32) + other.astype(f32)]
    unnamed x260 -> x47, local copies, waits for them, and re-layouts: 4.37 us -> 12.9 us
    ppermute x8 -> x0, waiting for transfers between devices: 7.52 us -> none  [the longest x4 6.52 us: with_halo(): low = lax.ppermute(rims[0], axis, forward).astype(jnp.float32)]
  transfers between devices with their start and end apart: 21 -> 22, of which waited for: 11 -> 10; matrix products, arithmetic and copies ran while one was open for 29% -> 8% of each run, Pallas kernels for 0% -> 18%
where the time goes in v2:
time: 122 us
  starting transfers between devices  38.3 us (31%)
  Pallas kernels  35.4 us (29%)
  waiting for transfers between devices  24.2 us (20%)
  local copies, waits for them, and re-layouts  14.8 us (12%)
  other arithmetic  4.25 us (3%)
  matrix products  3.56 us (3%)
    pallas_call x6, Pallas kernels, kernel_call(): pl.pallas_call(body, in_specs=[vmem] * len(args), out_specs=[vmem] * len(...  35.4 us
    ppermute x11, starting transfers between devices, shifted(): return lax.ppermute(x, axis, pairs)  22.4 us
    ppermute x11, waiting for transfers between devices, xor_swap(): return lax.ppermute(x, axis, [(i, i ^ mask) for i in range(size)])  20.4 us
    ppermute x11, starting transfers between devices, xor_swap(): return lax.ppermute(x, axis, [(i, i ^ mask) for i in range(size)])  15.9 us
    unnamed x47, local copies, waits for them, and re-layouts  12.9 us
    ppermute x11, waiting for transfers between devices, shifted(): return lax.ppermute(x, axis, pairs)  3.83 us
  transfers between devices with their start and end apart: 22, of which 10 were waited for; matrix products, arithmetic and copies ran while one was open for 8% of the time, Pallas kernels for 18%

profile of v2, /device:TPU:0, one launch (start us, length us, event | category | flops | bytes accessed | tf_op | source)
XLA Modules:
  0.0 121.6 jit_solution(16593186901176816107)
XLA Ops:
  2.7 1.3 %collective-permute-start = (bf16[128,512]{1,0:T(8,128)(2,1)S(1)}, bf16[128,512]{1,0:T(8,128)(2,1)S(1)}, u32[]{:S(2)}, u32[]{:S(2)}) collective-permute-start(bf16[128,512]{1,0:T(8,128)(2,1)S(1)} %convolution_convert_fusion.window_ref), channel_id=1, source_target_pairs={{4,0},{8,4},{12,8},{16,12},{20,16},{24,20},{28,24},{5,1},{9,5},{13... | collective-permute-start | bytes 393224 | tf_op jit(solution)/shard_map/ppermute | solution.py:316
  5.5 4.1 %margins.1 = (bf16[1024,2304]{1,0:T(8,128)(2,1)S(1)}, f32[9,256,128]{2,1,0:T(8,128)S(1)}) custom-call(s32[4,9,256]{2,1,0:T(8,128)S(1)} %copy.18.index_ref, f32[4,9,256]{2,1,0:T(8,128)S(1)} %copy.19.weight_ref, bf16[128,512]{1,0:T(8,128)(2,1)S(1)} %convolution_convert_fusion.window_ref), custom_call_target="tpu_custom_call" | custom-call | flops 301989888 | bytes 8388608 | tf_op jit(solution)/shard_map/margins/pallas_call | solution.py:21
  9.6 2.4 %field.1 = (f32[9,256,128]{2,1,0:T(8,128)S(1)}, bf16[2,9,8,128]{3,2,1,0:T(8,128)(2,1)S(1)}, bf16[2,3,256,128]{3,2,1,0:T(8,128)(2,1)S(1)}) custom-call(bf16[1024,2304]{1,0:T(8,128)(2,1)S(1)} %get-tuple-element.22.dense_ref, bf16[128,512]{1,0:T(8,128)(2,1)S(1)} %collective-permute-done.window_ref, f32[9,256,128]{2,1,0:T(8,128)S(1)} %get-tuple-element.23.part_ref, ...), custom_call_target="tpu_custom_call" | custom-call | flops 301989888 | bytes 8388608 | tf_op jit(solution)/shard_map/field/pallas_call | solution.py:21
  12.1 3.1 %collective-permute-start.1 = (bf16[9,8,128]{2,1,0:T(8,128)(2,1)S(1)}, bf16[9,8,128]{2,1,0:T(8,128)(2,1)S(1)}, u32[]{:S(2)}, u32[]{:S(2)}) collective-permute-start(bf16[9,8,128]{2,1,0:T(8,128)(2,1)S(1)} %get-tuple-element.53), channel_id=1, source_target_pairs={{0,1},{1,2},{2,3},{3,0},{4,5},{5,6},{6,7},{7,4},{8,9},{9,10},{10,1... | collective-permute-start | bytes 55304 | tf_op jit(solution)/shard_map/ppermute | solution.py:316
  15.2 2.1 %collective-permute-start.2 = (bf16[9,8,128]{2,1,0:T(8,128)(2,1)S(1)}, bf16[9,8,128]{2,1,0:T(8,128)(2,1)S(1)}, u32[]{:S(2)}, u32[]{:S(2)}) collective-permute-start(bf16[9,8,128]{2,1,0:T(8,128)(2,1)S(1)} %get-tuple-element.52), channel_id=1, source_target_pairs={{0,3},{1,0},{2,1},{3,2},{4,7},{5,4},{6,5},{7,6},{8,11},{9,8},{10,9... | collective-permute-start | bytes 55304 | tf_op jit(solution)/shard_map/ppermute | solution.py:316
  17.3 1.7 %collective-permute-done.1.left_ref = bf16[9,8,128]{2,1,0:T(8,128)(2,1)S(1)} collective-permute-done((bf16[9,8,128]{2,1,0:T(8,128)(2,1)S(1)}, bf16[9,8,128]{2,1,0:T(8,128)(2,1)S(1)}, u32[]{:S(2)}, u32[]{:S(2)}) %collective-permute-start.1) | collective-permute-done | bytes 18464 | tf_op jit(solution)/shard_map/ppermute | solution.py:316
  19.5 1.3 %collective-permute-start.4 = (bf16[3,272,128]{2,1,0:T(8,128)(2,1)S(1)}, bf16[3,272,128]{2,1,0:T(8,128)(2,1)S(1)}, u32[]{:S(2)}, u32[]{:S(2)}) collective-permute-start(bf16[3,272,128]{2,1,0:T(8,128)(2,1)S(1)} %pad_maximum_fusion.1), channel_id=1, source_target_pairs={{4,0},{8,4},{12,8},{16,12},{20,16},{24,20},{28,24},{5,1},{9,5},{13... | collective-permute-start | bytes 626696 | tf_op jit(solution)/shard_map/ppermute | solution.py:316
  20.8 3.0 %collective-permute-start.3 = (bf16[3,272,128]{2,1,0:T(8,128)(2,1)S(1)}, bf16[3,272,128]{2,1,0:T(8,128)(2,1)S(1)}, u32[]{:S(2)}, u32[]{:S(2)}) collective-permute-start(bf16[3,272,128]{2,1,0:T(8,128)(2,1)S(1)} %pad_maximum_fusion), channel_id=1, source_target_pairs={{0,4},{4,8},{8,12},{12,16},{16,20},{20,24},{24,28},{1,5},{5,9},{9,... | collective-permute-start | bytes 626696 | tf_op jit(solution)/shard_map/ppermute | solution.py:316
  25.4 3.9 %conv.1.base_ref = f32[9,256,128]{2,1,0:T(8,128)S(1)} custom-call(f32[9,256,128]{2,1,0:T(8,128)S(1)} %get-tuple-element.24.field_ref, f32[7,7,128]{2,1,0:T(8,128)S(1)} %copy-done.9), custom_call_target="tpu_custom_call" | custom-call | flops 28901376 | bytes 16777216 | tf_op jit(solution)/shard_map/conv/pallas_call | solution.py:21
  30.7 1.3 %copy-done.4 = f32[9,256,128]{2,1,0:T(8,128)S(1)} copy-done((f32[9,256,128]{2,1,0:T(8,128)S(1)}, f32[9,256,128]{2,1,0:T(8,128)}, u32[]{:S(2)}) %copy-start.4) | copy-done | bytes 1179672
  33.9 10.6 %mlp.1 = (f32[9,256,128]{2,1,0:T(8,128)S(1)}, f32[15,272,128]{2,1,0:T(8,128)S(1)}, f32[2,128,512]{2,1,0:T(8,128)S(1)}, f32[8,128]{1,0:T(8,128)S(1)}, bf16[2,9,8,...) custom-call(f32[9,256,128]{2,1,0:T(8,128)S(1)} %conv.1.base_ref, f32[9,256,128]{2,1,0:T(8,128)S(1)} %copy-done.4, ...), custom_call_target="tpu_custom_call" | custom-call | flops 1509949440 | bytes 33554432 | tf_op jit(solution)/shard_map/mlp/pallas_call | solution.py:21
  45.8 2.6 %collective-permute-start.6 = (bf16[9,8,128]{2,1,0:T(8,128)(2,1)S(1)}, bf16[9,8,128]{2,1,0:T(8,128)(2,1)S(1)}, u32[]{:S(2)}, u32[]{:S(2)}) collective-permute-start(bf16[9,8,128]{2,1,0:T(8,128)(2,1)S(1)} %get-tuple-element.50), channel_id=1, source_target_pairs={{0,3},{1,0},{2,1},{3,2},{4,7},{5,4},{6,5},{7,6},{8,11},{9,8},{10,9... | collective-permute-start | bytes 55304 | tf_op jit(solution)/shard_map/ppermute | solution.py:316
  48.4 1.7 %collective-permute-done.5.left_ref = bf16[9,8,128]{2,1,0:T(8,128)(2,1)S(1)} collective-permute-done((bf16[9,8,128]{2,1,0:T(8,128)(2,1)S(1)}, bf16[9,8,128]{2,1,0:T(8,128)(2,1)S(1)}, u32[]{:S(2)}, u32[]{:S(2)}) %collective-permute-start.5) | collective-permute-done | bytes 18464 | tf_op jit(solution)/shard_map/ppermute | solution.py:316
  50.9 1.3 %collective-permute-start.8 = (bf16[3,272,128]{2,1,0:T(8,128)(2,1)}, bf16[3,272,128]{2,1,0:T(8,128)(2,1)S(1)}, u32[]{:S(2)}, u32[]{:S(2)}) collective-permute-start(bf16[3,272,128]{2,1,0:T(8,128)(2,1)} %pad_maximum_fusion.3), channel_id=1, source_target_pairs={{4,0},{8,4},{12,8},{16,12},{20,16},{24,20},{28,24},{5,1},{9,5},{13... | collective-permute-start | bytes 626696 | tf_op jit(solution)/shard_map/ppermute | solution.py:316
  52.8 3.8 %collective-permute-start.7 = (bf16[3,272,128]{2,1,0:T(8,128)(2,1)}, bf16[3,272,128]{2,1,0:T(8,128)(2,1)}, u32[]{:S(2)}, u32[]{:S(2)}) collective-permute-start(bf16[3,272,128]{2,1,0:T(8,128)(2,1)} %pad_maximum_fusion.2), channel_id=1, source_target_pairs={{0,4},{4,8},{8,12},{12,16},{16,20},{20,24},{24,28},{1,5},{5,9},{9,... | collective-permute-start | bytes 626696 | tf_op jit(solution)/shard_map/ppermute | solution.py:316
  58.5 1.3 %collective-permute-start.10 = (bf16[512,256]{1,0:T(8,128)(2,1)}, bf16[512,256]{1,0:T(8,128)(2,1)}, u32[]{:S(2)}, u32[]{:S(2)}) collective-permute-start(bf16[512,256]{1,0:T(8,128)(2,1)} %param.13), channel_id=1, source_target_pairs={{4,0},{8,4},{12,8},{16,12},{20,16},{24,20},{28,24},{5,1},{9,5},{13... | collective-permute-start | bytes 786440 | tf_op jit(solution)/shard_map/ppermute | solution.py:316
  61.1 9.2 %grads.1 = (f32[49,128]{1,0:T(8,128)S(1)}, f32[9,256,128]{2,1,0:T(8,128)S(1)}) custom-call(f32[9,256,128]{2,1,0:T(8,128)S(1)} %copy-done.6, f32[15,272,128]{2,1,0:T(8,128)S(1)} %get-tuple-element.28.field_ref, f32[7,7,128]{2,1,0:T(8,128)S(1)} %copy-done.9), custom_call_target="tpu_custom_call" | custom-call | flops 57802752 | bytes 33554432 | tf_op jit(solution)/shard_map/grads/pallas_call | solution.py:21
  70.3 2.3 %copy-done.2 = bf16[1024,2304]{1,0:T(8,128)(2,1)S(1)} copy-done((bf16[1024,2304]{1,0:T(8,128)(2,1)S(1)}, bf16[1024,2304]{1,0:T(8,128)(2,1)}, u32[]{:S(2)}) %copy-start.2) | copy-done | bytes 4718616
  72.6 5.3 %state.1 = (f32[9,256,128]{2,1,0:T(8,128)}, f32[1024,128]{1,0:T(8,128)S(1)}) custom-call(f32[9,256,128]{2,1,0:T(8,128)S(1)} %get-tuple-element.29.base_ref, bf16[9,8,128]{2,1,0:T(8,128)(2,1)S(1)} %collective-permute-done.5.left_ref, bf16[9,8,128]{2,1,0:T(8,128)(2,1)S(1)} %collective-permute-done.6.right_ref, ...), custom_call_target="tpu_custom_call" | custom-call | flops 1207959552 | bytes 16777216 | tf_op jit(solution)/shard_map/state/pallas_call | solution.py:21
  78.9 3.9 %collective-permute-start.17 = (bf16[128,512]{1,0:T(8,128)(2,1)S(1)}, bf16[128,512]{1,0:T(8,128)(2,1)S(1)}, u32[]{:S(2)}, u32[]{:S(2)}) collective-permute-start(bf16[128,512]{1,0:T(8,128)(2,1)S(1)} %fusion.4), channel_id=1, source_target_pairs={{0,8},{4,12},{8,0},{12,4},{16,24},{20,28},{24,16},{28,20},{1,9},{5... | collective-permute-start | bytes 393224 | tf_op jit(solution)/shard_map/ppermute | solution.py:332
  82.9 1.4 %fusion = f32[256,128]{1,0:T(8,128)S(1)} fusion(bf16[1024,128]{1,0:T(8,128)(2,1)S(1)} %convert.3, bf16[512,256]{1,0:T(8,128)(2,1)} %collective-permute-done.10, bf16[512,256]{1,0:T(8,128)(2,1)} %param.13), kind=kOutput, calls=%fused_computation.1 | convolution fusion | flops 68157440 | bytes 917504 | tf_op jit(solution)/shard_map/dot_general | solution.py:481
  84.5 2.5 %collective-permute-done.17 = bf16[128,512]{1,0:T(8,128)(2,1)S(1)} collective-permute-done((bf16[128,512]{1,0:T(8,128)(2,1)S(1)}, bf16[128,512]{1,0:T(8,128)(2,1)S(1)}, u32[]{:S(2)}, u32[]{:S(2)}) %collective-permute-start.17) | collective-permute-done | bytes 131104 | tf_op jit(solution)/shard_map/ppermute | solution.py:332
  87.1 1.9 %collective-permute-start.18 = (bf16[128,512]{1,0:T(8,128)(2,1)S(1)}, bf16[128,512]{1,0:T(8,128)(2,1)S(1)}, u32[]{:S(2)}, u32[]{:S(2)}) collective-permute-start(bf16[128,512]{1,0:T(8,128)(2,1)S(1)} %add_convert_fusion.2), channel_id=1, source_target_pairs={{0,16},{4,20},{8,24},{12,28},{16,0},{20,4},{24,8},{28,12},{1,17},{... | collective-permute-start | bytes 393224 | tf_op jit(solution)/shard_map/ppermute | solution.py:332
  89.1 3.4 %collective-permute-done.18 = bf16[128,512]{1,0:T(8,128)(2,1)S(1)} collective-permute-done((bf16[128,512]{1,0:T(8,128)(2,1)S(1)}, bf16[128,512]{1,0:T(8,128)(2,1)S(1)}, u32[]{:S(2)}, u32[]{:S(2)}) %collective-permute-start.18) | collective-permute-done | bytes 131104 | tf_op jit(solution)/shard_map/ppermute | solution.py:332
  95.0 2.5 %collective-permute-done.19 = bf16[128,512]{1,0:T(8,128)(2,1)S(1)} collective-permute-done((bf16[128,512]{1,0:T(8,128)(2,1)S(1)}, bf16[128,512]{1,0:T(8,128)(2,1)S(1)}, u32[]{:S(2)}, u32[]{:S(2)}) %collective-permute-start.19) | collective-permute-done | bytes 131104 | tf_op jit(solution)/shard_map/ppermute | solution.py:332
  97.6 2.2 %collective-permute-start.20 = (bf16[128,512]{1,0:T(8,128)(2,1)S(1)}, bf16[128,512]{1,0:T(8,128)(2,1)S(1)}, u32[]{:S(2)}, u32[]{:S(2)}) collective-permute-start(bf16[128,512]{1,0:T(8,128)(2,1)S(1)} %add_convert_fusion), channel_id=1, source_target_pairs={{0,2},{1,3},{2,0},{3,1},{4,6},{5,7},{6,4},{7,5},{8,10},{9,11},{10,... | collective-permute-start | bytes 393224 | tf_op jit(solution)/shard_map/ppermute | solution.py:332
  99.8 1.3 %collective-permute-start.9 = (bf16[512,128]{1,0:T(8,128)(2,1)S(1)}, bf16[512,128]{1,0:T(8,128)(2,1)S(1)}, u32[]{:S(2)}, u32[]{:S(2)}) collective-permute-start(bf16[512,128]{1,0:T(8,128)(2,1)S(1)} %slice.103), channel_id=1, source_target_pairs={{0,4},{4,8},{8,12},{12,16},{16,20},{20,24},{24,28},{1,5},{5,9},{9,... | collective-permute-start | bytes 393224 | tf_op jit(solution)/shard_map/ppermute | solution.py:316
  101.1 2.1 %collective-permute-start.14 = (f32[306,128]{1,0:T(8,128)S(1)}, f32[306,128]{1,0:T(8,128)S(1)}, u32[]{:S(2)}, u32[]{:S(2)}) collective-permute-start(f32[306,128]{1,0:T(8,128)S(1)} %add.36), channel_id=1, source_target_pairs={{0,1},{1,0},{2,3},{3,2},{4,5},{5,4},{6,7},{7,6},{8,9},{9,8},{10,11... | collective-permute-start | bytes 470024 | tf_op jit(solution)/shard_map/ppermute | solution.py:332
  103.2 1.7 %collective-permute-done.20 = bf16[128,512]{1,0:T(8,128)(2,1)S(1)} collective-permute-done((bf16[128,512]{1,0:T(8,128)(2,1)S(1)}, bf16[128,512]{1,0:T(8,128)(2,1)S(1)}, u32[]{:S(2)}, u32[]{:S(2)}) %collective-permute-start.20) | collective-permute-done | bytes 131104 | tf_op jit(solution)/shard_map/ppermute | solution.py:332
  105.2 1.7 %collective-permute-done.14 = f32[306,128]{1,0:T(8,128)S(1)} collective-permute-done((f32[306,128]{1,0:T(8,128)S(1)}, f32[306,128]{1,0:T(8,128)S(1)}, u32[]{:S(2)}, u32[]{:S(2)}) %collective-permute-start.14) | collective-permute-done | bytes 156704 | tf_op jit(solution)/shard_map/ppermute | solution.py:332
  107.0 2.5 %collective-permute-start.15 = (f32[306,128]{1,0:T(8,128)S(1)}, f32[306,128]{1,0:T(8,128)S(1)}, u32[]{:S(2)}, u32[]{:S(2)}) collective-permute-start(f32[306,128]{1,0:T(8,128)S(1)} %add.37), channel_id=1, source_target_pairs={{0,2},{1,3},{2,0},{3,1},{4,6},{5,7},{6,4},{7,5},{8,10},{9,11},{10,... | collective-permute-start | bytes 470024 | tf_op jit(solution)/shard_map/ppermute | solution.py:332
  110.5 7.6 %collective-permute-done.15 = f32[306,128]{1,0:T(8,128)S(1)} collective-permute-done((f32[306,128]{1,0:T(8,128)S(1)}, f32[306,128]{1,0:T(8,128)S(1)}, u32[]{:S(2)}, u32[]{:S(2)}) %collective-permute-start.15) | collective-permute-done | bytes 156704 | tf_op jit(solution)/shard_map/ppermute | solution.py:332
  (100 shorter events, 23.4 us)
Async XLA Ops:
  0.6 9.0 %copy-start.7 = (bf16[9,256,128]{2,1,0:T(8,128)(2,1)S(1)}, bf16[9,256,128]{2,1,0:T(8,128)(2,1)}, u32[]{:S(2)}) copy-start(bf16[9,256,128]{2,1,0:T(8,128)(2,1)} %state_ref.1) | copy-start | bytes 1769476
  2.7 6.9 %collective-permute-start = (bf16[128,512]{1,0:T(8,128)(2,1)S(1)}, bf16[128,512]{1,0:T(8,128)(2,1)S(1)}, u32[]{:S(2)}, u32[]{:S(2)}) collective-permute-start(bf16[128,512]{1,0:T(8,128)(2,1)S(1)} %convolution_convert_fusion.window_ref), channel_id=1, source_target_pairs={{4,0},{8,4},{12,8},{16,12},{20,16},{24,20},{28,24},{5,1},{9,5},{13... | collective-permute-start | bytes 393224 | tf_op jit(solution)/shard_map/ppermute | solution.py:316
  12.0 17.3 %copy-start.3 = (f32[9,256,128]{2,1,0:T(8,128)}, f32[9,256,128]{2,1,0:T(8,128)S(1)}, u32[]{:S(2)}) copy-start(f32[9,256,128]{2,1,0:T(8,128)S(1)} %get-tuple-element.24.field_ref) | copy-start | bytes 3538948
  12.0 11.8 %copy-start.10 = (bf16[128,512]{1,0:T(8,128)(2,1)S(1)}, bf16[128,512]{1,0:T(8,128)(2,1)}, u32[]{:S(2)}) copy-start(bf16[128,512]{1,0:T(8,128)(2,1)} %w_in_ref.1) | copy-start | bytes 393220
  12.1 12.6 %copy-start.11 = (bf16[512,128]{1,0:T(8,128)(2,1)S(1)}, bf16[512,128]{1,0:T(8,128)(2,1)}, u32[]{:S(2)}) copy-start(bf16[512,128]{1,0:T(8,128)(2,1)} %w_out_ref.1) | copy-start | bytes 393220
  12.1 13.3 %copy-start.9 = (f32[7,7,128]{2,1,0:T(8,128)S(1)}, f32[7,7,128]{2,1,0:T(8,128)}, u32[]{:S(2)}) copy-start(f32[7,7,128]{2,1,0:T(8,128)} %kernel_ref.7) | copy-start | bytes 75268
  12.1 7.0 %collective-permute-start.1 = (bf16[9,8,128]{2,1,0:T(8,128)(2,1)S(1)}, bf16[9,8,128]{2,1,0:T(8,128)(2,1)S(1)}, u32[]{:S(2)}, u32[]{:S(2)}) collective-permute-start(bf16[9,8,128]{2,1,0:T(8,128)(2,1)S(1)} %get-tuple-element.53), channel_id=1, source_target_pairs={{0,1},{1,2},{2,3},{3,0},{4,5},{5,6},{6,7},{7,4},{8,9},{9,10},{10,1... | collective-permute-start | bytes 55304 | tf_op jit(solution)/shard_map/ppermute | solution.py:316
  15.2 4.2 %collective-permute-start.2 = (bf16[9,8,128]{2,1,0:T(8,128)(2,1)S(1)}, bf16[9,8,128]{2,1,0:T(8,128)(2,1)S(1)}, u32[]{:S(2)}, u32[]{:S(2)}) collective-permute-start(bf16[9,8,128]{2,1,0:T(8,128)(2,1)S(1)} %get-tuple-element.52), channel_id=1, source_target_pairs={{0,3},{1,0},{2,1},{3,2},{4,7},{5,4},{6,5},{7,6},{8,11},{9,8},{10,9... | collective-permute-start | bytes 55304 | tf_op jit(solution)/shard_map/ppermute | solution.py:316
  19.5 9.9 %collective-permute-start.4 = (bf16[3,272,128]{2,1,0:T(8,128)(2,1)S(1)}, bf16[3,272,128]{2,1,0:T(8,128)(2,1)S(1)}, u32[]{:S(2)}, u32[]{:S(2)}) collective-permute-start(bf16[3,272,128]{2,1,0:T(8,128)(2,1)S(1)} %pad_maximum_fusion.1), channel_id=1, source_target_pairs={{4,0},{8,4},{12,8},{16,12},{20,16},{24,20},{28,24},{5,1},{9,5},{13... | collective-permute-start | bytes 626696 | tf_op jit(solution)/shard_map/ppermute | solution.py:316
  20.8 9.2 %collective-permute-start.3 = (bf16[3,272,128]{2,1,0:T(8,128)(2,1)S(1)}, bf16[3,272,128]{2,1,0:T(8,128)(2,1)S(1)}, u32[]{:S(2)}, u32[]{:S(2)}) collective-permute-start(bf16[3,272,128]{2,1,0:T(8,128)(2,1)S(1)} %pad_maximum_fusion), channel_id=1, source_target_pairs={{0,4},{4,8},{8,12},{12,16},{16,20},{20,24},{24,28},{1,5},{5,9},{9,... | collective-permute-start | bytes 626696 | tf_op jit(solution)/shard_map/ppermute | solution.py:316
  25.4 5.3 %copy-start.8 = (bf16[9,256,128]{2,1,0:T(8,128)(2,1)S(1)}, bf16[9,256,128]{2,1,0:T(8,128)(2,1)}, u32[]{:S(2)}) copy-start(bf16[9,256,128]{2,1,0:T(8,128)(2,1)} %cotangent_ref.3) | copy-start | bytes 1769476
  25.4 5.3 %copy-start.12 = (bf16[512,128]{1,0:T(8,128)(2,1)S(1)}, bf16[512,128]{1,0:T(8,128)(2,1)}, u32[]{:S(2)}) copy-start(bf16[512,128]{1,0:T(8,128)(2,1)} %w_out_ref.1) | copy-start | bytes 393220
  25.4 5.3 %copy-start.13 = (bf16[128,512]{0,1:T(8,128)(2,1)S(1)}, bf16[128,512]{0,1:T(8,128)(2,1)}, u32[]{:S(2)}) copy-start(bf16[128,512]{0,1:T(8,128)(2,1)} %copy.20) | copy-start | bytes 393220
  25.4 5.3 %copy-start.14 = (bf16[512,128]{0,1:T(8,128)(2,1)S(1)}, bf16[512,128]{0,1:T(8,128)(2,1)}, u32[]{:S(2)}) copy-start(bf16[512,128]{0,1:T(8,128)(2,1)} %copy.21) | copy-start | bytes 393220
  44.5 12.9 %copy-start.5 = (f32[9,256,128]{2,1,0:T(8,128)}, f32[9,256,128]{2,1,0:T(8,128)S(1)}, u32[]{:S(2)}) copy-start(f32[9,256,128]{2,1,0:T(8,128)S(1)} %get-tuple-element.27.g_ref) | copy-start | bytes 3538948
  44.5 5.6 %collective-permute-start.5 = (bf16[9,8,128]{2,1,0:T(8,128)(2,1)S(1)}, bf16[9,8,128]{2,1,0:T(8,128)(2,1)S(1)}, u32[]{:S(2)}, u32[]{:S(2)}) collective-permute-start(bf16[9,8,128]{2,1,0:T(8,128)(2,1)S(1)} %get-tuple-element.51), channel_id=1, source_target_pairs={{0,1},{1,2},{2,3},{3,0},{4,5},{5,6},{6,7},{7,4},{8,9},{9,10},{10,1... | collective-permute-start | bytes 55304 | tf_op jit(solution)/shard_map/ppermute | solution.py:316
  45.8 4.4 %collective-permute-start.6 = (bf16[9,8,128]{2,1,0:T(8,128)(2,1)S(1)}, bf16[9,8,128]{2,1,0:T(8,128)(2,1)S(1)}, u32[]{:S(2)}, u32[]{:S(2)}) collective-permute-start(bf16[9,8,128]{2,1,0:T(8,128)(2,1)S(1)} %get-tuple-element.50), channel_id=1, source_target_pairs={{0,3},{1,0},{2,1},{3,2},{4,7},{5,4},{6,5},{7,6},{8,11},{9,8},{10,9... | collective-permute-start | bytes 55304 | tf_op jit(solution)/shard_map/ppermute | solution.py:316
  50.9 19.4 %collective-permute-start.8 = (bf16[3,272,128]{2,1,0:T(8,128)(2,1)}, bf16[3,272,128]{2,1,0:T(8,128)(2,1)S(1)}, u32[]{:S(2)}, u32[]{:S(2)}) collective-permute-start(bf16[3,272,128]{2,1,0:T(8,128)(2,1)} %pad_maximum_fusion.3), channel_id=1, source_target_pairs={{4,0},{8,4},{12,8},{16,12},{20,16},{24,20},{28,24},{5,1},{9,5},{13... | collective-permute-start | bytes 626696 | tf_op jit(solution)/shard_map/ppermute | solution.py:316
  52.8 17.4 %collective-permute-start.7 = (bf16[3,272,128]{2,1,0:T(8,128)(2,1)}, bf16[3,272,128]{2,1,0:T(8,128)(2,1)}, u32[]{:S(2)}, u32[]{:S(2)}) collective-permute-start(bf16[3,272,128]{2,1,0:T(8,128)(2,1)} %pad_maximum_fusion.2), channel_id=1, source_target_pairs={{0,4},{4,8},{8,12},{12,16},{16,20},{20,24},{24,28},{1,5},{5,9},{9,... | collective-permute-start | bytes 626696 | tf_op jit(solution)/shard_map/ppermute | solution.py:316
  57.4 20.5 %collective-permute-start.16 = (f32[128,512]{1,0:T(8,128)}, f32[128,512]{1,0:T(8,128)}, u32[]{:S(2)}, u32[]{:S(2)}) collective-permute-start(f32[128,512]{1,0:T(8,128)} %select_bitcast_fusion.1), channel_id=1, source_target_pairs={{0,4},{4,0},{8,12},{12,8},{16,20},{20,16},{24,28},{28,24},{1,5},{5... | collective-permute-start | bytes 786440 | tf_op jit(solution)/shard_map/ppermute | solution.py:332
  58.5 24.4 %collective-permute-start.10 = (bf16[512,256]{1,0:T(8,128)(2,1)}, bf16[512,256]{1,0:T(8,128)(2,1)}, u32[]{:S(2)}, u32[]{:S(2)}) collective-permute-start(bf16[512,256]{1,0:T(8,128)(2,1)} %param.13), channel_id=1, source_target_pairs={{4,0},{8,4},{12,8},{16,12},{20,16},{24,20},{28,24},{5,1},{9,5},{13... | collective-permute-start | bytes 786440 | tf_op jit(solution)/shard_map/ppermute | solution.py:316
  78.9 8.1 %collective-permute-start.17 = (bf16[128,512]{1,0:T(8,128)(2,1)S(1)}, bf16[128,512]{1,0:T(8,128)(2,1)S(1)}, u32[]{:S(2)}, u32[]{:S(2)}) collective-permute-start(bf16[128,512]{1,0:T(8,128)(2,1)S(1)} %fusion.4), channel_id=1, source_target_pairs={{0,8},{4,12},{8,0},{12,4},{16,24},{20,28},{24,16},{28,20},{1,9},{5... | collective-permute-start | bytes 393224 | tf_op jit(solution)/shard_map/ppermute | solution.py:332
  84.3 4.7 %collective-permute-start.11 = (f32[306,128]{1,0:T(8,128)S(1)}, f32[306,128]{1,0:T(8,128)S(1)}, u32[]{:S(2)}, u32[]{:S(2)}) collective-permute-start(f32[306,128]{1,0:T(8,128)S(1)} %pad_maximum_fusion.4), channel_id=1, source_target_pairs={{0,4},{4,0},{8,12},{12,8},{16,20},{20,16},{24,28},{28,24},{1,5},{5... | collective-permute-start | bytes 470024 | tf_op jit(solution)/shard_map/ppermute | solution.py:332
  87.1 5.4 %collective-permute-start.18 = (bf16[128,512]{1,0:T(8,128)(2,1)S(1)}, bf16[128,512]{1,0:T(8,128)(2,1)S(1)}, u32[]{:S(2)}, u32[]{:S(2)}) collective-permute-start(bf16[128,512]{1,0:T(8,128)(2,1)S(1)} %add_convert_fusion.2), channel_id=1, source_target_pairs={{0,16},{4,20},{8,24},{12,28},{16,0},{20,4},{24,8},{28,12},{1,17},{... | collective-permute-start | bytes 393224 | tf_op jit(solution)/shard_map/ppermute | solution.py:332
  89.0 5.3 %collective-permute-start.12 = (f32[306,128]{1,0:T(8,128)S(1)}, f32[306,128]{1,0:T(8,128)S(1)}, u32[]{:S(2)}, u32[]{:S(2)}) collective-permute-start(f32[306,128]{1,0:T(8,128)S(1)} %fusion.15), channel_id=1, source_target_pairs={{0,8},{4,12},{8,0},{12,4},{16,24},{20,28},{24,16},{28,20},{1,9},{5... | collective-permute-start | bytes 470024 | tf_op jit(solution)/shard_map/ppermute | solution.py:332
  92.5 5.0 %collective-permute-start.19 = (bf16[128,512]{1,0:T(8,128)(2,1)S(1)}, bf16[128,512]{1,0:T(8,128)(2,1)S(1)}, u32[]{:S(2)}, u32[]{:S(2)}) collective-permute-start(bf16[128,512]{1,0:T(8,128)(2,1)S(1)} %add_convert_fusion.1), channel_id=1, source_target_pairs={{0,1},{1,0},{2,3},{3,2},{4,5},{5,4},{6,7},{7,6},{8,9},{9,8},{10,11... | collective-permute-start | bytes 393224 | tf_op jit(solution)/shard_map/ppermute | solution.py:332
  94.4 6.7 %collective-permute-start.13 = (f32[306,128]{1,0:T(8,128)S(1)}, f32[306,128]{1,0:T(8,128)S(1)}, u32[]{:S(2)}, u32[]{:S(2)}) collective-permute-start(f32[306,128]{1,0:T(8,128)S(1)} %add.35), channel_id=1, source_target_pairs={{0,16},{4,20},{8,24},{12,28},{16,0},{20,4},{24,8},{28,12},{1,17},{... | collective-permute-start | bytes 470024 | tf_op jit(solution)/shard_map/ppermute | solution.py:332
  97.6 7.3 %collective-permute-start.20 = (bf16[128,512]{1,0:T(8,128)(2,1)S(1)}, bf16[128,512]{1,0:T(8,128)(2,1)S(1)}, u32[]{:S(2)}, u32[]{:S(2)}) collective-permute-start(bf16[128,512]{1,0:T(8,128)(2,1)S(1)} %add_convert_fusion), channel_id=1, source_target_pairs={{0,2},{1,3},{2,0},{3,1},{4,6},{5,7},{6,4},{7,5},{8,10},{9,11},{10,... | collective-permute-start | bytes 393224 | tf_op jit(solution)/shard_map/ppermute | solution.py:332
  99.8 9.7 %collective-permute-start.9 = (bf16[512,128]{1,0:T(8,128)(2,1)S(1)}, bf16[512,128]{1,0:T(8,128)(2,1)S(1)}, u32[]{:S(2)}, u32[]{:S(2)}) collective-permute-start(bf16[512,128]{1,0:T(8,128)(2,1)S(1)} %slice.103), channel_id=1, source_target_pairs={{0,4},{4,8},{8,12},{12,16},{16,20},{20,24},{24,28},{1,5},{5,9},{9,... | collective-permute-start | bytes 393224 | tf_op jit(solution)/shard_map/ppermute | solution.py:316
  101.1 5.8 %collective-permute-start.14 = (f32[306,128]{1,0:T(8,128)S(1)}, f32[306,128]{1,0:T(8,128)S(1)}, u32[]{:S(2)}, u32[]{:S(2)}) collective-permute-start(f32[306,128]{1,0:T(8,128)S(1)} %add.36), channel_id=1, source_target_pairs={{0,1},{1,0},{2,3},{3,2},{4,5},{5,4},{6,7},{7,6},{8,9},{9,8},{10,11... | collective-permute-start | bytes 470024 | tf_op jit(solution)/shard_map/ppermute | solution.py:332
  104.9 15.0 %collective-permute-start.21 = (f32[128,512]{1,0:T(8,128)S(1)}, f32[128,512]{1,0:T(8,128)S(1)}, u32[]{:S(2)}, u32[]{:S(2)}) collective-permute-start(f32[128,512]{1,0:T(8,128)S(1)} %convert_add_fusion), channel_id=1, source_target_pairs={{0,4},{4,0},{8,12},{12,8},{16,20},{20,16},{24,28},{28,24},{1,5},{5... | collective-permute-start | bytes 786440 | tf_op jit(solution)/shard_map/ppermute | solution.py:332
  107.0 11.2 %collective-permute-start.15 = (f32[306,128]{1,0:T(8,128)S(1)}, f32[306,128]{1,0:T(8,128)S(1)}, u32[]{:S(2)}, u32[]{:S(2)}) collective-permute-start(f32[306,128]{1,0:T(8,128)S(1)} %add.37), channel_id=1, source_target_pairs={{0,2},{1,3},{2,0},{3,1},{4,6},{5,7},{6,4},{7,5},{8,10},{9,11},{10,... | collective-permute-start | bytes 470024 | tf_op jit(solution)/shard_map/ppermute | solution.py:332
  (11 other events, 22.0 us)

commit v3 on v2

--- a/solution.py
+++ b/solution.py
@@ -16,7 +16,7 @@
 f32 = jnp.float32
 
 
-def kernel_call(body, outs, scratch, args, name, flops, nbytes):
+def kernel_call(body, outs, scratch, args, flops, nbytes):
     vmem = pl.BlockSpec(memory_space=pltpu.VMEM)
     return pl.pallas_call(
         body,
@@ -26,7 +26,6 @@
         scratch_shapes=[pltpu.VMEM(shape, dtype) for shape, dtype in scratch],
         compiler_params=pltpu.CompilerParams(vmem_limit_bytes=LIMIT),
         cost_estimate=pl.CostEstimate(flops=flops, bytes_accessed=nbytes, transcendentals=0),
-        name=name,
     )(*args)
 
 
@@ -50,14 +49,14 @@
 
 
 def margins_kernel(index_ref, weight_ref, window_ref, dense_ref, part_ref):
-    margins, height, width = index_ref.shape
+    height, margins, width = index_ref.shape
     own = window_ref.shape[1]
     places = lax.broadcasted_iota(jnp.int32, (ROWS, width), 0).astype(f32).astype(bf16)
 
     @pl.loop(0, height)
     def _(row):
-        index = [index_ref[slot, pl.ds(row, 1), :] for slot in range(margins)]
-        weight = [weight_ref[slot, pl.ds(row, 1), :] for slot in range(margins)]
+        index = [index_ref[row, slot : slot + 1, :] for slot in range(margins)]
+        weight = [weight_ref[row, slot : slot + 1, :] for slot in range(margins)]
         weight = merged_margins(index, weight)
         cells = pl.ds(pl.multiple_of(row * width, width), width)
         for block in range(dense_ref.shape[0] // ROWS):
@@ -69,7 +68,7 @@
 
 
 def field_kernel(dense_ref, window_ref, part_ref, state_ref, field_ref, side_ref, end_ref):
-    height, width, channels = field_ref.shape
+    height, width, _ = field_ref.shape
     own = window_ref.shape[1]
 
     @pl.loop(0, height)
@@ -107,8 +106,8 @@
                     sums[out] = term if sums[out] is None else sums[out] + term
 
 
-def local_taps(padded_ref, spread_ref, out_ref):
-    height, width, channels = out_ref.shape
+def local_taps(padded_ref, spread_ref, out_ref, start=0):
+    height, width, _ = out_ref.shape
 
     @pl.loop(0, width // 8)
     def _(block):
@@ -116,7 +115,7 @@
         sums = [None] * height
 
         def load(row, tap):
-            return padded_ref[row - 3, pl.ds(col + (tap + EDGE - 3), 8), :]
+            return padded_ref[row - 3, pl.ds(col + (start + tap + EDGE - 3), 8), :]
 
         tap_sums(sums, range(3, height + 3), load, spread_ref)
         for row in range(height):
@@ -130,26 +129,32 @@
     padded_ref[:, EDGE : EDGE + width, :] = source_ref[...]
 
 
-def rest_taps(base_ref, left_ref, right_ref, low_ref, high_ref, spread_ref, out_ref, strip, ends):
-    height, width, channels = base_ref.shape
+def rest_taps(base_refs, left_ref, right_ref, low_ref, high_ref, spread_ref, out_ref, strip, ends):
+    height, width, _ = out_ref.shape
     strip[...] = jnp.zeros(strip.shape, f32)
     strip[0, :, :EDGE, :] = left_ref[...].astype(f32)
     strip[1, :, 2 * EDGE :, :] = right_ref[...].astype(f32)
     ends[0:3] = low_ref[...].astype(f32)
     ends[3:6] = high_ref[...].astype(f32)
 
-    @pl.loop(0, width // 8)
-    def _(block):
-        col = pl.multiple_of(block * 8, 8)
-        sums = [base_ref[row, pl.ds(col, 8), :] for row in range(height)]
-
-        def load(row, tap):
-            place = row if row < 3 else row - height
-            return ends[place, pl.ds(col + (tap + EDGE - 3), 8), :]
-
-        tap_sums(sums, (0, 1, 2, height + 3, height + 4, height + 5), load, spread_ref)
-        for row in range(height):
-            out_ref[row, pl.ds(col, 8), :] = sums[row]
+    def part(base_ref, start):
+        @pl.loop(0, base_ref.shape[1] // 8)
+        def _(block):
+            col = pl.multiple_of(block * 8, 8)
+            sums = [base_ref[row, pl.ds(col, 8), :] for row in range(height)]
+
+            def load(row, tap):
+                place = row if row < 3 else row - height
+                return ends[place, pl.ds(col + (start + tap + EDGE - 3), 8), :]
+
+            tap_sums(sums, (0, 1, 2, height + 3, height + 4, height + 5), load, spread_ref)
+            for row in range(height):
+                out_ref[row, pl.ds(col + start, 8), :] = sums[row]
+
+    start = 0
+    for base_ref in base_refs:
+        part(base_ref, start)
+        start += base_ref.shape[1]
 
     @pl.loop(0, 2)
     def _(side):
@@ -164,14 +169,15 @@
             out_ref[row, pl.ds(col, 8), :] = sums[row]
 
 
-def conv_kernel(field_ref, kernel_ref, out_ref, padded, weights):
-    spread(kernel_ref, weights, False)
+def conv_kernel(start, flip, field_ref, kernel_ref, out_ref, padded, weights):
+    spread(kernel_ref, weights, flip)
     pad_cols(field_ref, padded)
-    local_taps(padded, weights, out_ref)
+    local_taps(padded, weights, out_ref, start)
 
 
 def mlp_kernel(
-    base_ref,
+    first_ref,
+    second_ref,
     field_ref,
     left_ref,
     right_ref,
@@ -183,11 +189,10 @@
     gain_ref,
     w_in_ref,
     w_out_ref,
-    w_in_t_ref,
-    w_out_t_ref,
     g_ref,
     padded_ref,
-    pair_ref,
+    kept_ref,
+    given_ref,
     gain_out_ref,
     side_ref,
     end_ref,
@@ -195,17 +200,21 @@
     weights,
     strip,
     ends,
+    pair_ref,
+    gain_sum,
 ):
-    height, width, channels = base_ref.shape
+    height, width, channels = g_ref.shape
+    transposed = (((1,), (1,)), ((), ()))
     spread(kernel_ref, weights, False)
-    rest_taps(base_ref, left_ref, right_ref, low_ref, high_ref, weights, conv, strip, ends)
+    bases = (first_ref, second_ref)
+    rest_taps(bases, left_ref, right_ref, low_ref, high_ref, weights, conv, strip, ends)
     padded_ref[3 : 3 + height, EDGE : EDGE + width, :] = field_ref[...]
     padded_ref[3 : 3 + height, :EDGE, :] = strip[0, :, :EDGE, :]
     padded_ref[3 : 3 + height, EDGE + width :, :] = strip[1, :, 2 * EDGE :, :]
     padded_ref[:3] = ends[0:3]
     padded_ref[3 + height :] = ends[3:6]
     pair_ref[...] = jnp.zeros(pair_ref.shape, f32)
-    gain_out_ref[...] = jnp.zeros(gain_out_ref.shape, f32)
+    gain_sum[...] = jnp.zeros(gain_sum.shape, f32)
     gain = gain_ref[...]
 
     @pl.loop(0, height)
@@ -218,7 +227,9 @@
         mask = jnp.broadcast_to(mask_ref[pl.ds(row, 1), :].astype(f32), (channels, width)).T
         gy_rows = (mask * cotangent_ref[row].astype(f32)).astype(bf16)
         pre = jnp.dot(ln_rows, w_in_ref[...], preferred_element_type=f32)
-        g_hidden = jnp.dot(gy_rows, w_out_t_ref[...], preferred_element_type=f32)
+        g_hidden = lax.dot_general(
+            gy_rows, w_out_ref[...], transposed, preferred_element_type=f32
+        )
         square = pre * pre
         half = 0.5 + 0.5 * jnp.tanh(pre * (ROOT + (ROOT * CUBIC) * square))
         hidden = pre * half
@@ -231,8 +242,8 @@
         pair_ref[1] += lax.dot_general(
             gy_rows, hidden, (((0,), (0,)), ((), ())), preferred_element_type=f32
         )
-        g_ln = jnp.dot(g_pre, w_in_t_ref[...], preferred_element_type=f32)
-        gain_out_ref[...] += jnp.sum((g_ln * normed).reshape(width // 8, 8, channels), axis=0)
+        g_ln = lax.dot_general(g_pre, w_in_ref[...], transposed, preferred_element_type=f32)
+        gain_sum[...] += jnp.sum((g_ln * normed).reshape(width // 8, 8, channels), axis=0)
         g_norm = g_ln * gain
         g_conv = (
             g_norm
@@ -245,11 +256,15 @@
 
     end_ref[0] = g_ref[height - 3 :].astype(bf16)
     end_ref[1] = g_ref[:3].astype(bf16)
-
-
-def grads_kernel(g_ref, field_ref, kernel_ref, grad_ref, out_ref, padded, weights):
+    gain_out_ref[...] = jnp.sum(gain_sum[...], axis=0, keepdims=True)
+    odd = lax.rem(lax.axis_index("lat"), 2)
+    kept_ref[...] = pair_ref[odd]
+    given_ref[...] = pair_ref[1 - odd]
+
+
+def taps_kernel(g_ref, field_ref, gain_ref, grad_ref):
     height, width, channels = g_ref.shape
-    taps = kernel_ref.shape[0]
+    taps = field_ref.shape[0] - height + 1
     for col_tap in range(taps):
 
         def body(block, sums):
@@ -268,9 +283,7 @@
         for row_tap in range(taps):
             place = row_tap * taps + col_tap
             grad_ref[place : place + 1, :] = jnp.sum(sums[row_tap], axis=0, keepdims=True)
-    spread(kernel_ref, weights, True)
-    pad_cols(g_ref, padded)
-    local_taps(padded, weights, out_ref)
+    grad_ref[taps * taps : taps * taps + 1, :] = gain_ref[...]
 
 
 def state_kernel(
@@ -281,18 +294,16 @@
     high_ref,
     kernel_ref,
     cotangent_ref,
-    dense_ref,
     state_ref,
-    window_ref,
+    halves,
     weights,
     strip,
     ends,
     sums,
-    halves,
 ):
     height, width, channels = base_ref.shape
     spread(kernel_ref, weights, True)
-    rest_taps(base_ref, left_ref, right_ref, low_ref, high_ref, weights, sums, strip, ends)
+    rest_taps((base_ref,), left_ref, right_ref, low_ref, high_ref, weights, sums, strip, ends)
 
     @pl.loop(0, height)
     def _(row):
@@ -303,11 +314,46 @@
         halves[cells, :channels] = high
         halves[cells, channels:] = (state - high.astype(f32)).astype(bf16)
 
+
+def window_kernel(dense_ref, halves_ref, embed_ref, next_ref, window_ref, return_ref, late_ref):
+    channels = window_ref.shape[1]
+    own = embed_ref.shape[0]
+
     @pl.loop(0, window_ref.shape[0] // 256)
     def _(block):
         slots = pl.ds(pl.multiple_of(block * 256, 256), 256)
-        both = jnp.dot(dense_ref[slots, :], halves[...], preferred_element_type=f32)
+        both = jnp.dot(dense_ref[slots, :], halves_ref[...], preferred_element_type=f32)
         window_ref[slots, :] = both[:, :channels] + both[:, channels:]
+
+    return_ref[...] = window_ref[own:].astype(bf16)
+    rows = (((0,), (0,)), ((), ()))
+    late_ref[...] = lax.dot_general(
+        embed_ref[...], window_ref[:own].astype(bf16), rows, preferred_element_type=f32
+    ) + lax.dot_general(next_ref[...], return_ref[...], rows, preferred_element_type=f32)
+
+
+def finish_kernel(
+    pair_ref, other_ref, late_ref, add_ref, in_ref, out_ref, projection_ref, kernel_ref, gain_ref
+):
+    even = lax.rem(lax.axis_index("lat"), 2) == 0
+
+    @pl.when(even)
+    def _():
+        in_ref[...] = pair_ref[...]
+        out_ref[...] = other_ref[...].T
+
+    @pl.when(jnp.logical_not(even))
+    def _():
+        in_ref[...] = other_ref[...]
+        out_ref[...] = pair_ref[...].T
+
+    rows = projection_ref.shape[0]
+    taps = kernel_ref.shape[0]
+    late = late_ref[...].astype(f32) + add_ref[...].astype(f32)
+    projection_ref[...] = late[:rows]
+    for tap in range(taps):
+        kernel_ref[tap] = late[rows + tap * taps : rows + (tap + 1) * taps]
+    gain_ref[...] = late[rows + taps * taps :]
 
 
 def shifted(x, axis, by, wrap=False):
@@ -332,43 +378,27 @@
     return lax.ppermute(x, axis, [(i, i ^ mask) for i in range(size)])
 
 
-def masks(axis):
-    size = lax.axis_size(axis)
-    if size & (size - 1):
-        return None
-    return [1 << k for k in range(size.bit_length() - 1)]
-
-
-def fold(value, axis, chosen, dtype=bf16):
-    for mask in chosen:
-        mine = value.astype(dtype)
+def steps_of(first=0):
+    steps = []
+    for axis in ("lat", "lon"):
+        size = lax.axis_size(axis)
+        if size & (size - 1):
+            raise ValueError("axis size")
+        steps += [(axis, 1 << k) for k in range(size.bit_length() - 1)]
+    return steps[first:]
+
+
+def fold(value, steps, name):
+    for place, (axis, mask) in enumerate(steps):
+        mine = value.astype(f32 if (axis, mask) == ("lat", 1) else bf16)
         other = xor_swap(mine, axis, mask)
+        if name == "late" and place == len(steps) - 1:
+            return mine, other
         value = mine.astype(f32) + other.astype(f32)
     return value
 
 
-def sum_over_mesh(value):
-    for axis in ("lat", "lon"):
-        steps = masks(axis)
-        value = lax.psum(value, axis) if steps is None else fold(value, axis, steps, f32)
-    return value
-
-
-def sum_pair_over_mesh(pair):
-    steps = masks("lat")
-    if not steps or masks("lon") is None:
-        return lax.psum(pair, ("lat", "lon"))
-    odd = lax.rem(lax.axis_index("lat"), 2) == 1
-    kept = jnp.where(odd, pair[1], pair[0])
-    given = xor_swap(jnp.where(odd, pair[0], pair[1]), "lat", 1)
-    value = kept + given
-    value = fold(value, "lat", steps[1:])
-    value = fold(value, "lon", masks("lon"))
-    other = xor_swap(value, "lat", 1)
-    return jnp.where(odd, other, value), jnp.where(odd, value, other)
-
-
-def shards(
+def step(
     ocean_state,
     cotangent,
     atm_embed,
@@ -402,8 +432,7 @@
         margins_kernel,
         [((slots, cells), bf16), (grid, f32)],
         [],
-        (margin_index, margin_weight, own),
-        "margins",
+        (margin_index.transpose(1, 0, 2), margin_weight.transpose(1, 0, 2), own),
         2 * cells * cells_atm * channels,
         8 << 20,
     )
@@ -412,33 +441,44 @@
         [(grid, f32), ((2, height, EDGE, channels), bf16), ((2, 3, width, channels), bf16)],
         [],
         (dense, following, part, ocean_state),
-        "field",
         2 * cells * cells_atm * channels,
         8 << 20,
     )
     left, right, low, high = exchange(side, end)
-    (conv,) = kernel_call(
-        conv_kernel,
-        [(grid, f32)],
-        [((height, wide, channels), f32), tap_scratch],
-        (field, dw_kernel),
-        "conv",
-        cells * channels * 98,
-        16 << 20,
-    )
-    g_conv, padded, pair, gain_rows, side, end = kernel_call(
+    half = (height, width // 2, channels)
+    padded_scratch = ((height, wide, channels), f32)
+    convs = [
+        kernel_call(
+            functools.partial(conv_kernel, start, False),
+            [(half, f32)],
+            [padded_scratch, tap_scratch],
+            (field, dw_kernel),
+            cells * channels * 49,
+            8 << 20,
+        )[0]
+        for start in (0, width // 2)
+    ]
+    g_conv, padded, kept, given, gain_sum, side, end = kernel_call(
         mlp_kernel,
         [
             (grid, f32),
             ((height + 6, wide, channels), f32),
-            ((2, channels, hidden), f32),
-            ((8, channels), f32),
+            ((channels, hidden), f32),
+            ((channels, hidden), f32),
+            ((1, channels), f32),
             ((2, height, EDGE, channels), bf16),
             ((2, 3, width, channels), bf16),
         ],
-        [(grid, f32), tap_scratch, strip, ends],
+        [
+            (grid, f32),
+            tap_scratch,
+            strip,
+            ends,
+            ((2, channels, hidden), f32),
+            ((8, channels), f32),
+        ],
         (
-            conv,
+            *convs,
             field,
             left,
             right,
@@ -450,63 +490,85 @@
             norm_gain[None],
             w_in,
             w_out,
-            w_in.T,
-            w_out.T,
         ),
-        "mlp",
         cells * channels * hidden * 10,
         32 << 20,
     )
     left, right, low, high = exchange(side, end)
-    grad_in, grad_out = sum_pair_over_mesh(pair)
-    grad_kernel, back = kernel_call(
-        grads_kernel,
-        [((taps * taps, channels), f32), (grid, f32)],
-        [((height, wide, channels), f32), tap_scratch],
-        (g_conv, padded, dw_kernel),
-        "grads",
-        cells * channels * 196,
-        32 << 20,
-    )
-    grad_state, g_window = kernel_call(
+    received = xor_swap(given, "lat", 1)
+    pair = fold(kept + received, steps_of(1), "early")
+    other = xor_swap(pair, "lat", 1)
+    (grad_taps,) = kernel_call(
+        taps_kernel,
+        [((taps * taps + 1, channels), f32)],
+        [],
+        (g_conv, padded, gain_sum),
+        cells * channels * 98,
+        16 << 20,
+    )
+    (back,) = kernel_call(
+        functools.partial(conv_kernel, 0, True),
+        [(grid, f32)],
+        [padded_scratch, tap_scratch],
+        (g_conv, dw_kernel),
+        cells * channels * 98,
+        16 << 20,
+    )
+    grad_state, halves = kernel_call(
         state_kernel,
-        [(grid, f32), ((slots, channels), f32)],
-        [tap_scratch, strip, ends, (grid, f32), ((cells, 2 * channels), bf16)],
-        (back, left, right, low, high, dw_kernel, cotangent, dense),
-        "state",
+        [(grid, f32), ((cells, 2 * channels), bf16)],
+        [tap_scratch, strip, ends, (grid, f32)],
+        (back, left, right, low, high, dw_kernel, cotangent),
+        cells * channels * 20,
+        8 << 20,
+    )
+    g_window, returned, grad_projection = kernel_call(
+        window_kernel,
+        [
+            ((slots, channels), f32),
+            ((cells_atm, channels), bf16),
+            (projection.shape, f32),
+        ],
+        [],
+        (dense, halves, atm_embed, next_embed),
         cells * slots * channels * 4,
-        16 << 20,
-    )
-    returned = shifted(g_window[cells_atm:].astype(bf16), "lat", 1)
-    grad_projection = lax.dot_general(
-        jnp.concatenate([atm_embed, next_embed], axis=0),
-        g_window.astype(bf16),
-        (((0,), (0,)), ((), ())),
-        preferred_element_type=f32,
-    )
-    late = jnp.concatenate(
-        [grad_projection, grad_kernel, jnp.sum(gain_rows, axis=0)[None]], axis=0
-    )
-    late = sum_over_mesh(late)
+        8 << 20,
+    )
+    returned = shifted(returned, "lat", 1)
+    late = jnp.concatenate([grad_projection, grad_taps], axis=0)
+    late, late_other = fold(late, steps_of(), "late")
     g_projected = (g_window[:cells_atm] + returned.astype(f32)).astype(bf16)
     grad_embed = lax.dot_general(
         g_projected, projection, (((1,), (1,)), ((), ())), preferred_element_type=f32
     )
-    rows = projection.shape[0]
+    grad_in, grad_out, grad_projection, grad_kernel, grad_gain = kernel_call(
+        finish_kernel,
+        [
+            (w_in.shape, f32),
+            (w_out.shape, f32),
+            (projection.shape, f32),
+            (dw_kernel.shape, f32),
+            ((1, channels), f32),
+        ],
+        [],
+        (pair, other, late, late_other),
+        channels * hidden,
+        2 << 20,
+    )
     return (
         grad_state,
         grad_embed,
-        late[:rows],
-        late[rows : rows + taps * taps].reshape(dw_kernel.shape),
-        late[rows + taps * taps],
+        grad_projection,
+        grad_kernel,
+        grad_gain[0],
         grad_in,
-        grad_out.T,
+        grad_out,
     )
 
 
 def solution(mesh):
     return jax.shard_map(
-        shards,
+        step,
         mesh=mesh,
         in_specs=(
             P("lat", "lon", None),

time: 122 us -> 103 us (0.84)
  local copies, waits for them, and re-layouts: 14.8 us -> 2.48 us
  waiting for transfers between devices: 24.2 us -> 17 us
  starting transfers between devices: 38.3 us -> 42.5 us
  other arithmetic: 4.25 us -> 0.35 us
  matrix products: 3.56 us -> 2.2 us
    unnamed x47 -> x22, local copies, waits for them, and re-layouts: 12.9 us -> 2.41 us
    ppermute x11, waiting for transfers between devices: 20.4 us -> 14.5 us  [xor_swap(): return lax.ppermute(x, axis, [(i, i ^ mask) for i in range(size)])]
    ppermute x11, starting transfers between devices: 15.9 us -> 20.2 us  [xor_swap(): return lax.ppermute(x, axis, [(i, i ^ mask) for i in range(size)])]
    dot_general x3 -> x2, matrix products: 3.56 us -> 2.2 us  [the longest x1 1.17 us: step(): lax.dot_general(projection, atm_embed, (((0,), (1,)), ((), ())), preferre...]
    ppermute x11, waiting for transfers between devices: 3.83 us -> 2.5 us  [shifted(): return lax.ppermute(x, axis, pairs)]
    pallas_call x6 -> x10, Pallas kernels: 35.4 us -> 36.6 us  [kernel_call(): pl.pallas_call(body, in_specs=[vmem] * len(args), out_specs=[vmem] * len(...]
  transfers between devices with their start and end apart: 22 -> 22, of which waited for: 10 -> 7; matrix products, arithmetic and copies ran while one was open for 8% -> 1% of each run, Pallas kernels for 18% -> 22%
where the time goes in v3:
time: 103 us; the launch traced here: 102 us
  starting transfers between devices  42.5 us (41%)
  Pallas kernels  36.6 us (36%)
  waiting for transfers between devices  17 us (17%)
  local copies, waits for them, and re-layouts  2.48 us (2%)
  matrix products  2.2 us (2%)
  between operations  1.07 us (1%)
    pallas_call x10, Pallas kernels, kernel_call(): pl.pallas_call(body, in_specs=[vmem] * len(args), out_specs=[vmem] * len(...  36.6 us
    ppermute x11, starting transfers between devices, shifted(): return lax.ppermute(x, axis, pairs)  22.4 us
    ppermute x11, starting transfers between devices, xor_swap(): return lax.ppermute(x, axis, [(i, i ^ mask) for i in range(size)])  20.2 us
    ppermute x11, waiting for transfers between devices, xor_swap(): return lax.ppermute(x, axis, [(i, i ^ mask) for i in range(size)])  14.5 us
    ppermute x11, waiting for transfers between devices, shifted(): return lax.ppermute(x, axis, pairs)  2.5 us
    unnamed x22, local copies, waits for them, and re-layouts  2.41 us
  transfers between devices with their start and end apart: 22, of which 7 were waited for; matrix products, arithmetic and copies ran while one was open for 1% of the time, Pallas kernels for 22%

profile of v3, /device:TPU:0, one launch (start us, length us, event | category | flops | bytes accessed | tf_op | source)
XLA Modules:
  0.0 102.3 jit_solution(9287288830961385527)
XLA Ops:
  2.7 1.3 %collective-permute-start = (bf16[128,512]{1,0:T(8,128)(2,1)S(1)}, bf16[128,512]{1,0:T(8,128)(2,1)S(1)}, u32[]{:S(2)}, u32[]{:S(2)}) collective-permute-start(bf16[128,512]{1,0:T(8,128)(2,1)S(1)} %convolution_convert_fusion.window_ref), channel_id=1, source_target_pairs={{4,0},{8,4},{12,8},{16,12},{20,16},{24,20},{28,24},{5,1},{9,5},{13... | collective-permute-start | bytes 393224 | tf_op jit(solution)/shard_map/ppermute | solution.py:362
  5.5 4.1 %shard_map.162 = (bf16[1024,2304]{1,0:T(8,128)(2,1)S(1)}, f32[9,256,128]{2,1,0:T(8,128)S(1)}) custom-call(s32[9,4,256]{2,1,0:T(4,128)S(1)} %bitcast.23, f32[9,4,256]{2,1,0:T(4,128)S(1)} %bitcast.24, bf16[128,512]{1,0:T(8,128)(2,1)S(1)} %convolution_convert_fusion.window_ref), custom_call_target="tpu_custom_call" | custom-call | flops 301989888 | bytes 8388608 | tf_op jit(solution)/shard_map/pallas_call | solution.py:21
  9.6 2.4 %shard_map.163 = (f32[9,256,128]{2,1,0:T(8,128)S(1)}, bf16[2,9,8,128]{3,2,1,0:T(8,128)(2,1)S(1)}, bf16[2,3,256,128]{3,2,1,0:T(8,128)(2,1)S(1)}) custom-call(bf16[1024,2304]{1,0:T(8,128)(2,1)S(1)} %get-tuple-element.29.dense_ref, bf16[128,512]{1,0:T(8,128)(2,1)S(1)} %collective-permute-done.window_ref, f32[9,256,128]{2,1,0:T(8,128)S(1)} %get-tuple-element.30.part_ref, ...), custom_call_target="tpu_custom_call" | custom-call | flops 301989888 | bytes 8388608 | tf_op jit(solution)/shard_map/pallas_call | solution.py:21
  12.0 3.1 %collective-permute-start.1 = (bf16[9,8,128]{2,1,0:T(8,128)(2,1)S(1)}, bf16[9,8,128]{2,1,0:T(8,128)(2,1)S(1)}, u32[]{:S(2)}, u32[]{:S(2)}) collective-permute-start(bf16[9,8,128]{2,1,0:T(8,128)(2,1)S(1)} %get-tuple-element.58), channel_id=1, source_target_pairs={{0,1},{1,2},{2,3},{3,0},{4,5},{5,6},{6,7},{7,4},{8,9},{9,10},{10,1... | collective-permute-start | bytes 55304 | tf_op jit(solution)/shard_map/ppermute | solution.py:362
  15.1 2.1 %collective-permute-start.2 = (bf16[9,8,128]{2,1,0:T(8,128)(2,1)S(1)}, bf16[9,8,128]{2,1,0:T(8,128)(2,1)S(1)}, u32[]{:S(2)}, u32[]{:S(2)}) collective-permute-start(bf16[9,8,128]{2,1,0:T(8,128)(2,1)S(1)} %get-tuple-element.57), channel_id=1, source_target_pairs={{0,3},{1,0},{2,1},{3,2},{4,7},{5,4},{6,5},{7,6},{8,11},{9,8},{10,9... | collective-permute-start | bytes 55304 | tf_op jit(solution)/shard_map/ppermute | solution.py:362
  17.2 1.7 %collective-permute-done.1.left_ref = bf16[9,8,128]{2,1,0:T(8,128)(2,1)S(1)} collective-permute-done((bf16[9,8,128]{2,1,0:T(8,128)(2,1)S(1)}, bf16[9,8,128]{2,1,0:T(8,128)(2,1)S(1)}, u32[]{:S(2)}, u32[]{:S(2)}) %collective-permute-start.1) | collective-permute-done | bytes 18464 | tf_op jit(solution)/shard_map/ppermute | solution.py:362
  19.4 1.3 %collective-permute-start.4 = (bf16[3,272,128]{2,1,0:T(8,128)(2,1)S(1)}, bf16[3,272,128]{2,1,0:T(8,128)(2,1)S(1)}, u32[]{:S(2)}, u32[]{:S(2)}) collective-permute-start(bf16[3,272,128]{2,1,0:T(8,128)(2,1)S(1)} %pad_maximum_fusion.1), channel_id=1, source_target_pairs={{4,0},{8,4},{12,8},{16,12},{20,16},{24,20},{28,24},{5,1},{9,5},{13... | collective-permute-start | bytes 626696 | tf_op jit(solution)/shard_map/ppermute | solution.py:362
  20.7 3.0 %collective-permute-start.3 = (bf16[3,272,128]{2,1,0:T(8,128)(2,1)S(1)}, bf16[3,272,128]{2,1,0:T(8,128)(2,1)S(1)}, u32[]{:S(2)}, u32[]{:S(2)}) collective-permute-start(bf16[3,272,128]{2,1,0:T(8,128)(2,1)S(1)} %pad_maximum_fusion), channel_id=1, source_target_pairs={{0,4},{4,8},{8,12},{12,16},{16,20},{20,24},{24,28},{1,5},{5,9},{9,... | collective-permute-start | bytes 626696 | tf_op jit(solution)/shard_map/ppermute | solution.py:362
  23.8 2.0 %shard_map.164.first_ref = f32[9,128,128]{2,1,0:T(8,128)S(1)} custom-call(f32[9,256,128]{2,1,0:T(8,128)S(1)} %get-tuple-element.31.field_ref, f32[7,7,128]{2,1,0:T(8,128)S(1)} %copy-done.4), custom_call_target="tpu_custom_call" | custom-call | flops 14450688 | bytes 8388608 | tf_op jit(solution)/shard_map/pallas_call | solution.py:21
  25.8 2.0 %shard_map.165.second_ref = f32[9,128,128]{2,1,0:T(8,128)S(1)} custom-call(f32[9,256,128]{2,1,0:T(8,128)S(1)} %get-tuple-element.31.field_ref, f32[7,7,128]{2,1,0:T(8,128)S(1)} %copy-done.4), custom_call_target="tpu_custom_call" | custom-call | flops 14450688 | bytes 8388608 | tf_op jit(solution)/shard_map/pallas_call | solution.py:21
  27.9 10.9 %shard_map.166 = (f32[9,256,128]{2,1,0:T(8,128)S(1)}, f32[15,272,128]{2,1,0:T(8,128)S(1)}, f32[128,512]{1,0:T(8,128)S(1)}, f32[128,512]{1,0:T(8,128)S(1)}, f32[1...) custom-call(f32[9,128,128]{2,1,0:T(8,128)S(1)} %shard_map.164.first_ref, ...), custom_call_target="tpu_custom_call" | custom-call | flops 1509949440 | bytes 33554432 | tf_op jit(solution)/shard_map/pallas_call | solution.py:21
  40.0 2.6 %collective-permute-start.6 = (bf16[9,8,128]{2,1,0:T(8,128)(2,1)S(1)}, bf16[9,8,128]{2,1,0:T(8,128)(2,1)S(1)}, u32[]{:S(2)}, u32[]{:S(2)}) collective-permute-start(bf16[9,8,128]{2,1,0:T(8,128)(2,1)S(1)} %get-tuple-element.55), channel_id=1, source_target_pairs={{0,3},{1,0},{2,1},{3,2},{4,7},{5,4},{6,5},{7,6},{8,11},{9,8},{10,9... | collective-permute-start | bytes 55304 | tf_op jit(solution)/shard_map/ppermute | solution.py:362
  42.7 1.3 %collective-permute-start.11 = (f32[128,512]{1,0:T(8,128)S(1)}, f32[128,512]{1,0:T(8,128)S(1)}, u32[]{:S(2)}, u32[]{:S(2)}) collective-permute-start(f32[128,512]{1,0:T(8,128)S(1)} %get-tuple-element.42), channel_id=1, source_target_pairs={{0,4},{4,0},{8,12},{12,8},{16,20},{20,16},{24,28},{28,24},{1,5},{5... | collective-permute-start | bytes 786440 | tf_op jit(solution)/shard_map/ppermute | solution.py:378
  44.4 1.3 %collective-permute-start.8 = (bf16[3,272,128]{2,1,0:T(8,128)(2,1)S(1)}, bf16[3,272,128]{2,1,0:T(8,128)(2,1)S(1)}, u32[]{:S(2)}, u32[]{:S(2)}) collective-permute-start(bf16[3,272,128]{2,1,0:T(8,128)(2,1)S(1)} %pad_maximum_fusion.3), channel_id=1, source_target_pairs={{4,0},{8,4},{12,8},{16,12},{20,16},{24,20},{28,24},{5,1},{9,5},{13... | collective-permute-start | bytes 626696 | tf_op jit(solution)/shard_map/ppermute | solution.py:362
  45.7 3.2 %collective-permute-start.7 = (bf16[3,272,128]{2,1,0:T(8,128)(2,1)S(1)}, bf16[3,272,128]{2,1,0:T(8,128)(2,1)S(1)}, u32[]{:S(2)}, u32[]{:S(2)}) collective-permute-start(bf16[3,272,128]{2,1,0:T(8,128)(2,1)S(1)} %pad_maximum_fusion.2), channel_id=1, source_target_pairs={{0,4},{4,8},{8,12},{12,16},{16,20},{20,24},{24,28},{1,5},{5,9},{9,... | collective-permute-start | bytes 626696 | tf_op jit(solution)/shard_map/ppermute | solution.py:362
  48.9 1.3 %collective-permute-start.9 = (bf16[512,256]{1,0:T(8,128)(2,1)S(1)}, bf16[512,256]{1,0:T(8,128)(2,1)S(1)}, u32[]{:S(2)}, u32[]{:S(2)}) collective-permute-start(bf16[512,256]{1,0:T(8,128)(2,1)S(1)} %copy-done.1), channel_id=1, source_target_pairs={{4,0},{8,4},{12,8},{16,12},{20,16},{24,20},{28,24},{5,1},{9,5},{13... | collective-permute-start | bytes 786440 | tf_op jit(solution)/shard_map/ppermute | solution.py:362
  50.2 3.9 %shard_map.167.base_ref = f32[9,256,128]{2,1,0:T(8,128)S(1)} custom-call(f32[9,256,128]{2,1,0:T(8,128)S(1)} %get-tuple-element.34.field_ref.g_ref, f32[7,7,128]{2,1,0:T(8,128)S(1)} %copy-done.4), custom_call_target="tpu_custom_call" | custom-call | flops 28901376 | bytes 16777216 | tf_op jit(solution)/shard_map/pallas_call | solution.py:21
  54.1 5.4 %shard_map.170 = f32[50,128]{1,0:T(8,128)S(1)} custom-call(f32[9,256,128]{2,1,0:T(8,128)S(1)} %get-tuple-element.34.field_ref.g_ref, f32[15,272,128]{2,1,0:T(8,128)S(1)} %get-tuple-element.44.field_ref, f32[1,128]{1,0:T(1,128)S(1)} %get-tuple-element.45.gain_ref), custom_call_target="tpu_custom_call" | custom-call | flops 28901376 | bytes 16777216 | tf_op jit(solution)/shard_map/pallas_call | solution.py:21
  59.5 2.9 %shard_map.168 = (f32[9,256,128]{2,1,0:T(8,128)}, bf16[2304,256]{1,0:T(8,128)(2,1)S(1)}) custom-call(f32[9,256,128]{2,1,0:T(8,128)S(1)} %shard_map.167.base_ref, bf16[9,8,128]{2,1,0:T(8,128)(2,1)S(1)} %collective-permute-done.5.left_ref, bf16[9,8,128]{2,1,0:T(8,128)(2,1)S(1)} %collective-permute-done.6.right_ref, ...), custom_call_target="tpu_custom_call" | custom-call | flops 5898240 | bytes 8388608 | tf_op jit(solution)/shard_map/pallas_call | solution.py:21
  62.4 4.3 %collective-permute-start.12 = (bf16[128,512]{1,0:T(8,128)(2,1)S(1)}, bf16[128,512]{1,0:T(8,128)(2,1)S(1)}, u32[]{:S(2)}, u32[]{:S(2)}) collective-permute-start(bf16[128,512]{1,0:T(8,128)(2,1)S(1)} %add_convert_fusion.3), channel_id=1, source_target_pairs={{0,8},{4,12},{8,0},{12,4},{16,24},{20,28},{24,16},{28,20},{1,9},{5... | collective-permute-start | bytes 393224 | tf_op jit(solution)/shard_map/ppermute | solution.py:378
  66.7 2.2 %shard_map.169 = (f32[1024,128]{1,0:T(8,128)S(1)}, bf16[512,128]{1,0:T(8,128)(2,1)S(1)}, f32[256,128]{1,0:T(8,128)S(1)}) custom-call(bf16[1024,2304]{1,0:T(8,128)(2,1)S(1)} %get-tuple-element.29.dense_ref, bf16[2304,256]{1,0:T(8,128)(2,1)S(1)} %get-tuple-element.38.halves_ref, bf16[512,256]{1,0:T(8,128)(2,1)S(1)} %copy-done.1, ...), custom_call_target="tpu_custom_call" | custom-call | flops 1207959552 | bytes 8388608 | tf_op jit(solution)/shard_map/pallas_call | solution.py:21
  69.0 1.4 %collective-permute-start.17 = (f32[306,128]{1,0:T(8,128)S(1)}, f32[306,128]{1,0:T(8,128)S(1)}, u32[]{:S(2)}, u32[]{:S(2)}) collective-permute-start(f32[306,128]{1,0:T(8,128)S(1)} %pad_maximum_fusion.4), channel_id=1, source_target_pairs={{0,4},{4,0},{8,12},{12,8},{16,20},{20,16},{24,28},{28,24},{1,5},{5... | collective-permute-start | bytes 470024 | tf_op jit(solution)/shard_map/ppermute | solution.py:378
  70.4 1.9 %collective-permute-start.10 = (bf16[512,128]{1,0:T(8,128)(2,1)S(1)}, bf16[512,128]{1,0:T(8,128)(2,1)S(1)}, u32[]{:S(2)}, u32[]{:S(2)}) collective-permute-start(bf16[512,128]{1,0:T(8,128)(2,1)S(1)} %get-tuple-element.40), channel_id=1, source_target_pairs={{0,4},{4,8},{8,12},{12,16},{16,20},{20,24},{24,28},{1,5},{5,9},{9,... | collective-permute-start | bytes 393224 | tf_op jit(solution)/shard_map/ppermute | solution.py:362
  72.4 2.1 %collective-permute-start.13 = (bf16[128,512]{1,0:T(8,128)(2,1)S(1)}, bf16[128,512]{1,0:T(8,128)(2,1)S(1)}, u32[]{:S(2)}, u32[]{:S(2)}) collective-permute-start(bf16[128,512]{1,0:T(8,128)(2,1)S(1)} %add_convert_fusion.2), channel_id=1, source_target_pairs={{0,16},{4,20},{8,24},{12,28},{16,0},{20,4},{24,8},{28,12},{1,17},{... | collective-permute-start | bytes 393224 | tf_op jit(solution)/shard_map/ppermute | solution.py:378
  74.5 1.9 %collective-permute-start.18 = (bf16[306,128]{1,0:T(8,128)(2,1)S(1)}, bf16[306,128]{1,0:T(8,128)(2,1)S(1)}, u32[]{:S(2)}, u32[]{:S(2)}) collective-permute-start(bf16[306,128]{1,0:T(8,128)(2,1)S(1)} %add_convert_fusion.8), channel_id=1, source_target_pairs={{0,8},{4,12},{8,0},{12,4},{16,24},{20,28},{24,16},{28,20},{1,9},{5... | collective-permute-start | bytes 235016 | tf_op jit(solution)/shard_map/ppermute | solution.py:378
  76.4 2.9 %collective-permute-done.13 = bf16[128,512]{1,0:T(8,128)(2,1)S(1)} collective-permute-done((bf16[128,512]{1,0:T(8,128)(2,1)S(1)}, bf16[128,512]{1,0:T(8,128)(2,1)S(1)}, u32[]{:S(2)}, u32[]{:S(2)}) %collective-permute-start.13) | collective-permute-done | bytes 131104 | tf_op jit(solution)/shard_map/ppermute | solution.py:378
  80.5 2.5 %collective-permute-start.19 = (bf16[306,128]{1,0:T(8,128)(2,1)S(1)}, bf16[306,128]{1,0:T(8,128)(2,1)S(1)}, u32[]{:S(2)}, u32[]{:S(2)}) collective-permute-start(bf16[306,128]{1,0:T(8,128)(2,1)S(1)} %add_convert_fusion.7), channel_id=1, source_target_pairs={{0,16},{4,20},{8,24},{12,28},{16,0},{20,4},{24,8},{28,12},{1,17},{... | collective-permute-start | bytes 235016 | tf_op jit(solution)/shard_map/ppermute | solution.py:378
  83.1 1.9 %collective-permute-done.14 = bf16[128,512]{1,0:T(8,128)(2,1)S(1)} collective-permute-done((bf16[128,512]{1,0:T(8,128)(2,1)S(1)}, bf16[128,512]{1,0:T(8,128)(2,1)S(1)}, u32[]{:S(2)}, u32[]{:S(2)}) %collective-permute-start.14) | collective-permute-done | bytes 131104 | tf_op jit(solution)/shard_map/ppermute | solution.py:378
  85.0 2.8 %collective-permute-start.15 = (bf16[128,512]{1,0:T(8,128)(2,1)S(1)}, bf16[128,512]{1,0:T(8,128)(2,1)S(1)}, u32[]{:S(2)}, u32[]{:S(2)}) collective-permute-start(bf16[128,512]{1,0:T(8,128)(2,1)S(1)} %add_convert_fusion), channel_id=1, source_target_pairs={{0,2},{1,3},{2,0},{3,1},{4,6},{5,7},{6,4},{7,5},{8,10},{9,11},{10,... | collective-permute-start | bytes 393224 | tf_op jit(solution)/shard_map/ppermute | solution.py:378
  87.8 1.8 %collective-permute-start.20 = (bf16[306,128]{1,0:T(8,128)(2,1)S(1)}, bf16[306,128]{1,0:T(8,128)(2,1)S(1)}, u32[]{:S(2)}, u32[]{:S(2)}) collective-permute-start(bf16[306,128]{1,0:T(8,128)(2,1)S(1)} %add_convert_fusion.6), channel_id=1, source_target_pairs={{0,1},{1,0},{2,3},{3,2},{4,5},{5,4},{6,7},{7,6},{8,9},{9,8},{10,11... | collective-permute-start | bytes 235016 | tf_op jit(solution)/shard_map/ppermute | solution.py:378
  89.6 4.1 %collective-permute-done.15 = bf16[128,512]{1,0:T(8,128)(2,1)S(1)} collective-permute-done((bf16[128,512]{1,0:T(8,128)(2,1)S(1)}, bf16[128,512]{1,0:T(8,128)(2,1)S(1)}, u32[]{:S(2)}, u32[]{:S(2)}) %collective-permute-start.15) | collective-permute-done | bytes 131104 | tf_op jit(solution)/shard_map/ppermute | solution.py:378
  95.7 5.6 %collective-permute-done.21.add_ref = bf16[306,128]{1,0:T(8,128)(2,1)S(1)} collective-permute-done((bf16[306,128]{1,0:T(8,128)(2,1)S(1)}, bf16[306,128]{1,0:T(8,128)(2,1)S(1)}, u32[]{:S(2)}, u32[]{:S(2)}) %collective-permute-start.21) | collective-permute-done | bytes 78368 | tf_op jit(solution)/shard_map/ppermute | solution.py:378
  (68 shorter events, 10.0 us)
Async XLA Ops:
  0.6 0.8 copy-start
  0.6 8.9 %copy-start.2 = (bf16[9,256,128]{2,1,0:T(8,128)(2,1)S(1)}, bf16[9,256,128]{2,1,0:T(8,128)(2,1)}, u32[]{:S(2)}) copy-start(bf16[9,256,128]{2,1,0:T(8,128)(2,1)} %state_ref.1) | copy-start | bytes 1769476
  2.7 6.9 %collective-permute-start = (bf16[128,512]{1,0:T(8,128)(2,1)S(1)}, bf16[128,512]{1,0:T(8,128)(2,1)S(1)}, u32[]{:S(2)}, u32[]{:S(2)}) collective-permute-start(bf16[128,512]{1,0:T(8,128)(2,1)S(1)} %convolution_convert_fusion.window_ref), channel_id=1, source_target_pairs={{4,0},{8,4},{12,8},{16,12},{20,16},{24,20},{28,24},{5,1},{9,5},{13... | collective-permute-start | bytes 393224 | tf_op jit(solution)/shard_map/ppermute | solution.py:362
  4.0 0.8 copy-start.7
  12.0 11.8 %copy-start.4 = (f32[7,7,128]{2,1,0:T(8,128)S(1)}, f32[7,7,128]{2,1,0:T(8,128)}, u32[]{:S(2)}) copy-start(f32[7,7,128]{2,1,0:T(8,128)} %kernel_ref.9) | copy-start | bytes 75268
  12.0 7.0 %collective-permute-start.1 = (bf16[9,8,128]{2,1,0:T(8,128)(2,1)S(1)}, bf16[9,8,128]{2,1,0:T(8,128)(2,1)S(1)}, u32[]{:S(2)}, u32[]{:S(2)}) collective-permute-start(bf16[9,8,128]{2,1,0:T(8,128)(2,1)S(1)} %get-tuple-element.58), channel_id=1, source_target_pairs={{0,1},{1,2},{2,3},{3,0},{4,5},{5,6},{6,7},{7,4},{8,9},{9,10},{10,1... | collective-permute-start | bytes 55304 | tf_op jit(solution)/shard_map/ppermute | solution.py:362
  15.1 4.2 %collective-permute-start.2 = (bf16[9,8,128]{2,1,0:T(8,128)(2,1)S(1)}, bf16[9,8,128]{2,1,0:T(8,128)(2,1)S(1)}, u32[]{:S(2)}, u32[]{:S(2)}) collective-permute-start(bf16[9,8,128]{2,1,0:T(8,128)(2,1)S(1)} %get-tuple-element.57), channel_id=1, source_target_pairs={{0,3},{1,0},{2,1},{3,2},{4,7},{5,4},{6,5},{7,6},{8,11},{9,8},{10,9... | collective-permute-start | bytes 55304 | tf_op jit(solution)/shard_map/ppermute | solution.py:362
  19.4 8.4 %collective-permute-start.4 = (bf16[3,272,128]{2,1,0:T(8,128)(2,1)S(1)}, bf16[3,272,128]{2,1,0:T(8,128)(2,1)S(1)}, u32[]{:S(2)}, u32[]{:S(2)}) collective-permute-start(bf16[3,272,128]{2,1,0:T(8,128)(2,1)S(1)} %pad_maximum_fusion.1), channel_id=1, source_target_pairs={{4,0},{8,4},{12,8},{16,12},{20,16},{24,20},{28,24},{5,1},{9,5},{13... | collective-permute-start | bytes 626696 | tf_op jit(solution)/shard_map/ppermute | solution.py:362
  20.7 7.1 %collective-permute-start.3 = (bf16[3,272,128]{2,1,0:T(8,128)(2,1)S(1)}, bf16[3,272,128]{2,1,0:T(8,128)(2,1)S(1)}, u32[]{:S(2)}, u32[]{:S(2)}) collective-permute-start(bf16[3,272,128]{2,1,0:T(8,128)(2,1)S(1)} %pad_maximum_fusion), channel_id=1, source_target_pairs={{0,4},{4,8},{8,12},{12,16},{16,20},{20,24},{24,28},{1,5},{5,9},{9,... | collective-permute-start | bytes 626696 | tf_op jit(solution)/shard_map/ppermute | solution.py:362
  25.7 2.1 %copy-start.3 = (bf16[9,256,128]{2,1,0:T(8,128)(2,1)S(1)}, bf16[9,256,128]{2,1,0:T(8,128)(2,1)}, u32[]{:S(2)}) copy-start(bf16[9,256,128]{2,1,0:T(8,128)(2,1)} %cotangent_ref.3) | copy-start | bytes 1769476
  25.8 2.1 %copy-start.5 = (bf16[128,512]{1,0:T(8,128)(2,1)S(1)}, bf16[128,512]{1,0:T(8,128)(2,1)}, u32[]{:S(2)}) copy-start(bf16[128,512]{1,0:T(8,128)(2,1)} %w_in_ref.1) | copy-start | bytes 393220
  25.8 2.1 %copy-start.6 = (bf16[512,128]{1,0:T(8,128)(2,1)S(1)}, bf16[512,128]{1,0:T(8,128)(2,1)}, u32[]{:S(2)}) copy-start(bf16[512,128]{1,0:T(8,128)(2,1)} %w_out_ref.1) | copy-start | bytes 393220
  25.8 2.1 %copy-start.9 = (s32[9,256]{1,0:T(8,128)S(1)}, s32[9,256]{1,0:T(8,128)}, u32[]{:S(2)}) copy-start(s32[9,256]{1,0:T(8,128)} %mask_ref.1) | copy-start | bytes 27652
  25.8 2.1 %copy-start.10 = (f32[128]{0:T(128)S(1)}, f32[128]{0:T(128)}, u32[]{:S(2)}) copy-start(f32[128]{0:T(128)} %param.16) | copy-start | bytes 1540
  38.7 10.2 %copy-start.1 = (bf16[512,256]{1,0:T(8,128)(2,1)S(1)}, bf16[512,256]{1,0:T(8,128)(2,1)}, u32[]{:S(2)}) copy-start(bf16[512,256]{1,0:T(8,128)(2,1)} %embed_ref.1) | copy-start | bytes 786436
  38.8 5.6 %collective-permute-start.5 = (bf16[9,8,128]{2,1,0:T(8,128)(2,1)S(1)}, bf16[9,8,128]{2,1,0:T(8,128)(2,1)S(1)}, u32[]{:S(2)}, u32[]{:S(2)}) collective-permute-start(bf16[9,8,128]{2,1,0:T(8,128)(2,1)S(1)} %get-tuple-element.56), channel_id=1, source_target_pairs={{0,1},{1,2},{2,3},{3,0},{4,5},{5,6},{6,7},{7,4},{8,9},{9,10},{10,1... | collective-permute-start | bytes 55304 | tf_op jit(solution)/shard_map/ppermute | solution.py:362
  40.0 4.4 %collective-permute-start.6 = (bf16[9,8,128]{2,1,0:T(8,128)(2,1)S(1)}, bf16[9,8,128]{2,1,0:T(8,128)(2,1)S(1)}, u32[]{:S(2)}, u32[]{:S(2)}) collective-permute-start(bf16[9,8,128]{2,1,0:T(8,128)(2,1)S(1)} %get-tuple-element.55), channel_id=1, source_target_pairs={{0,3},{1,0},{2,1},{3,2},{4,7},{5,4},{6,5},{7,6},{8,11},{9,8},{10,9... | collective-permute-start | bytes 55304 | tf_op jit(solution)/shard_map/ppermute | solution.py:362
  42.7 19.7 %collective-permute-start.11 = (f32[128,512]{1,0:T(8,128)S(1)}, f32[128,512]{1,0:T(8,128)S(1)}, u32[]{:S(2)}, u32[]{:S(2)}) collective-permute-start(f32[128,512]{1,0:T(8,128)S(1)} %get-tuple-element.42), channel_id=1, source_target_pairs={{0,4},{4,0},{8,12},{12,8},{16,20},{20,16},{24,28},{28,24},{1,5},{5... | collective-permute-start | bytes 786440 | tf_op jit(solution)/shard_map/ppermute | solution.py:378
  44.4 15.1 %collective-permute-start.8 = (bf16[3,272,128]{2,1,0:T(8,128)(2,1)S(1)}, bf16[3,272,128]{2,1,0:T(8,128)(2,1)S(1)}, u32[]{:S(2)}, u32[]{:S(2)}) collective-permute-start(bf16[3,272,128]{2,1,0:T(8,128)(2,1)S(1)} %pad_maximum_fusion.3), channel_id=1, source_target_pairs={{4,0},{8,4},{12,8},{16,12},{20,16},{24,20},{28,24},{5,1},{9,5},{13... | collective-permute-start | bytes 626696 | tf_op jit(solution)/shard_map/ppermute | solution.py:362
  45.7 13.8 %collective-permute-start.7 = (bf16[3,272,128]{2,1,0:T(8,128)(2,1)S(1)}, bf16[3,272,128]{2,1,0:T(8,128)(2,1)S(1)}, u32[]{:S(2)}, u32[]{:S(2)}) collective-permute-start(bf16[3,272,128]{2,1,0:T(8,128)(2,1)S(1)} %pad_maximum_fusion.2), channel_id=1, source_target_pairs={{0,4},{4,8},{8,12},{12,16},{16,20},{20,24},{24,28},{1,5},{5,9},{9,... | collective-permute-start | bytes 626696 | tf_op jit(solution)/shard_map/ppermute | solution.py:362
  48.9 17.8 %collective-permute-start.9 = (bf16[512,256]{1,0:T(8,128)(2,1)S(1)}, bf16[512,256]{1,0:T(8,128)(2,1)S(1)}, u32[]{:S(2)}, u32[]{:S(2)}) collective-permute-start(bf16[512,256]{1,0:T(8,128)(2,1)S(1)} %copy-done.1), channel_id=1, source_target_pairs={{4,0},{8,4},{12,8},{16,12},{20,16},{24,20},{28,24},{5,1},{9,5},{13... | collective-permute-start | bytes 786440 | tf_op jit(solution)/shard_map/ppermute | solution.py:362
  62.4 9.9 %collective-permute-start.12 = (bf16[128,512]{1,0:T(8,128)(2,1)S(1)}, bf16[128,512]{1,0:T(8,128)(2,1)S(1)}, u32[]{:S(2)}, u32[]{:S(2)}) collective-permute-start(bf16[128,512]{1,0:T(8,128)(2,1)S(1)} %add_convert_fusion.3), channel_id=1, source_target_pairs={{0,8},{4,12},{8,0},{12,4},{16,24},{20,28},{24,16},{28,20},{1,9},{5... | collective-permute-start | bytes 393224 | tf_op jit(solution)/shard_map/ppermute | solution.py:378
  69.0 5.5 %collective-permute-start.17 = (f32[306,128]{1,0:T(8,128)S(1)}, f32[306,128]{1,0:T(8,128)S(1)}, u32[]{:S(2)}, u32[]{:S(2)}) collective-permute-start(f32[306,128]{1,0:T(8,128)S(1)} %pad_maximum_fusion.4), channel_id=1, source_target_pairs={{0,4},{4,0},{8,12},{12,8},{16,20},{20,16},{24,28},{28,24},{1,5},{5... | collective-permute-start | bytes 470024 | tf_op jit(solution)/shard_map/ppermute | solution.py:378
  70.4 24.2 %collective-permute-start.10 = (bf16[512,128]{1,0:T(8,128)(2,1)S(1)}, bf16[512,128]{1,0:T(8,128)(2,1)S(1)}, u32[]{:S(2)}, u32[]{:S(2)}) collective-permute-start(bf16[512,128]{1,0:T(8,128)(2,1)S(1)} %get-tuple-element.40), channel_id=1, source_target_pairs={{0,4},{4,8},{8,12},{12,16},{16,20},{20,24},{24,28},{1,5},{5,9},{9,... | collective-permute-start | bytes 393224 | tf_op jit(solution)/shard_map/ppermute | solution.py:362
  72.4 6.9 %collective-permute-start.13 = (bf16[128,512]{1,0:T(8,128)(2,1)S(1)}, bf16[128,512]{1,0:T(8,128)(2,1)S(1)}, u32[]{:S(2)}, u32[]{:S(2)}) collective-permute-start(bf16[128,512]{1,0:T(8,128)(2,1)S(1)} %add_convert_fusion.2), channel_id=1, source_target_pairs={{0,16},{4,20},{8,24},{12,28},{16,0},{20,4},{24,8},{28,12},{1,17},{... | collective-permute-start | bytes 393224 | tf_op jit(solution)/shard_map/ppermute | solution.py:378
  74.5 6.0 %collective-permute-start.18 = (bf16[306,128]{1,0:T(8,128)(2,1)S(1)}, bf16[306,128]{1,0:T(8,128)(2,1)S(1)}, u32[]{:S(2)}, u32[]{:S(2)}) collective-permute-start(bf16[306,128]{1,0:T(8,128)(2,1)S(1)} %add_convert_fusion.8), channel_id=1, source_target_pairs={{0,8},{4,12},{8,0},{12,4},{16,24},{20,28},{24,16},{28,20},{1,9},{5... | collective-permute-start | bytes 235016 | tf_op jit(solution)/shard_map/ppermute | solution.py:378
  79.3 5.7 %collective-permute-start.14 = (bf16[128,512]{1,0:T(8,128)(2,1)S(1)}, bf16[128,512]{1,0:T(8,128)(2,1)S(1)}, u32[]{:S(2)}, u32[]{:S(2)}) collective-permute-start(bf16[128,512]{1,0:T(8,128)(2,1)S(1)} %add_convert_fusion.1), channel_id=1, source_target_pairs={{0,1},{1,0},{2,3},{3,2},{4,5},{5,4},{6,7},{7,6},{8,9},{9,8},{10,11... | collective-permute-start | bytes 393224 | tf_op jit(solution)/shard_map/ppermute | solution.py:378
  80.5 7.3 %collective-permute-start.19 = (bf16[306,128]{1,0:T(8,128)(2,1)S(1)}, bf16[306,128]{1,0:T(8,128)(2,1)S(1)}, u32[]{:S(2)}, u32[]{:S(2)}) collective-permute-start(bf16[306,128]{1,0:T(8,128)(2,1)S(1)} %add_convert_fusion.7), channel_id=1, source_target_pairs={{0,16},{4,20},{8,24},{12,28},{16,0},{20,4},{24,8},{28,12},{1,17},{... | collective-permute-start | bytes 235016 | tf_op jit(solution)/shard_map/ppermute | solution.py:378
  85.0 8.7 %collective-permute-start.15 = (bf16[128,512]{1,0:T(8,128)(2,1)S(1)}, bf16[128,512]{1,0:T(8,128)(2,1)S(1)}, u32[]{:S(2)}, u32[]{:S(2)}) collective-permute-start(bf16[128,512]{1,0:T(8,128)(2,1)S(1)} %add_convert_fusion), channel_id=1, source_target_pairs={{0,2},{1,3},{2,0},{3,1},{4,6},{5,7},{6,4},{7,5},{8,10},{9,11},{10,... | collective-permute-start | bytes 393224 | tf_op jit(solution)/shard_map/ppermute | solution.py:378
  87.8 6.0 %collective-permute-start.20 = (bf16[306,128]{1,0:T(8,128)(2,1)S(1)}, bf16[306,128]{1,0:T(8,128)(2,1)S(1)}, u32[]{:S(2)}, u32[]{:S(2)}) collective-permute-start(bf16[306,128]{1,0:T(8,128)(2,1)S(1)} %add_convert_fusion.6), channel_id=1, source_target_pairs={{0,1},{1,0},{2,3},{3,2},{4,5},{5,4},{6,7},{7,6},{8,9},{9,8},{10,11... | collective-permute-start | bytes 235016 | tf_op jit(solution)/shard_map/ppermute | solution.py:378
  93.7 7.6 %collective-permute-start.16 = (f32[128,512]{1,0:T(8,128)S(1)}, f32[128,512]{1,0:T(8,128)S(1)}, u32[]{:S(2)}, u32[]{:S(2)}) collective-permute-start(f32[128,512]{1,0:T(8,128)S(1)} %convert_add_fusion.pair_ref), channel_id=1, source_target_pairs={{0,4},{4,0},{8,12},{12,8},{16,20},{20,16},{24,28},{28,24},{1,5},{5... | collective-permute-start | bytes 786440 | tf_op jit(solution)/shard_map/ppermute | solution.py:378
  93.9 7.5 %collective-permute-start.21 = (bf16[306,128]{1,0:T(8,128)(2,1)S(1)}, bf16[306,128]{1,0:T(8,128)(2,1)S(1)}, u32[]{:S(2)}, u32[]{:S(2)}) collective-permute-start(bf16[306,128]{1,0:T(8,128)(2,1)S(1)} %add_convert_fusion.5.late_ref), channel_id=1, source_target_pairs={{0,2},{1,3},{2,0},{3,1},{4,6},{5,7},{6,4},{7,5},{8,10},{9,11},{10,... | collective-permute-start | bytes 235016 | tf_op jit(solution)/shard_map/ppermute | solution.py:378
  (1 other events, 0.8 us)
